TPU v7x, 512 devices: a whole 4x4x16 slice. The times are simulated.
512 devices in a mesh: dp: 32 (over z, core), seq: 16 (over y, x).
Axes of the slice: x: 4, y: 4, z: 16, core: 2. Of those that a mesh axis runs over, the one named last changes fastest.
Arguments:
- tokens: bfloat16 [65536, 1280], P(('dp', 'seq')), parts along dimension 0, may hold values from -6 to 6
- segment_ids: int32 [65536], P('dp'), parts along dimension 0, may hold values from 0 to 31, as said below
- w_qkv: bfloat16 [1280, 3840], P(None, 'seq')
- w_out: bfloat16 [1280, 1280], P('seq'), may hold values from -0.15625 to 0.15625
- w_merge: bfloat16 [5120, 4096], P(None, 'seq'), may hold values from -0.078125 to 0.078125
- gain_attn: float32 [1280], replicated, may hold values from 0.1 to 1.9
- gain_merge: float32 [1280], replicated, may hold values from 0.1 to 1.9
Outputs:
- merged_out: bfloat16 [16384, 4096], P(('dp', 'seq')), parts along dimension 0
There are 32 independent parts, one for each index of `dp`. A program takes and returns all parts, laid end to end along the dimension named above; an argument that names none is the same for every part. Nothing has to cross between parts.
Inputs may be any that keep to these rules, and one draw needn't show every extreme that they name: `segment_ids`: Non-decreasing along the packed tokens, starting at 0, rising by 0 or 1 from one token to the next, and equal within every aligned group of 4 tokens (an image's 2x2 patch blocks are stored together). There are exactly 32 images.
All inputs are finite; a program needn't handle non-finite values.
Results may differ from a plain program's by a relative error of at most 0.011.
Values may be sent and summed in bfloat16 or wider, within the bound.
No kernel may reach another device: no remote copies, remote signals or barrier semaphores. Data moves between devices by JAX's collectives and lax.ppermute only.
A program may use at most 64 MiB of HBM per device.

v0:
```python
import jax
import jax.numpy as jnp
from jax import lax
from jax.experimental import pallas as pl
from jax.experimental.pallas import tpu as pltpu
from jax.sharding import Mesh
from jax.sharding import PartitionSpec as P


D = 1280
HEADS = 16
HEAD_DIM = 80
TQ = 512
TK = 512
LOG2E = 1.4426950408889634


def layer_norm(vector, scale_gain):
    average = jnp.mean(vector, axis=-1, keepdims=True)
    centred = vector - average
    spread_sq = jnp.mean(centred * centred, axis=-1, keepdims=True)
    return centred * lax.rsqrt(spread_sq + 1e-06) * scale_gain


def swap_cores(value):
    return lax.ppermute(value, "c", [(0, 1), (1, 0)])


def shift_rows(value, step, rows):
    return lax.ppermute(value, "y", [(at, (at + step) % rows) for at in range(rows)])


def attention_kernel(bounds, qkv, seg_col, seg_row, out, keys, seg_wide):
    tiles, _, chunk = qkv.shape
    step = pl.program_id(0)
    per_chunk = chunk // TK

    @pl.when(step == 0)
    def _():
        for index in range(tiles):
            keys[index * chunk:(index + 1) * chunk, :] = qkv[index, HEAD_DIM:2 * HEAD_DIM, :].T
        seg_wide[...] = jnp.broadcast_to(seg_col[...], seg_wide.shape)

    part = step // (chunk // TQ)
    offset = pl.multiple_of((step % (chunk // TQ)) * TQ, TQ)
    queries = qkv[part, 0:HEAD_DIM, pl.ds(offset, TQ)]
    query_seg = seg_row[0:1, pl.ds(pl.multiple_of(step * TQ, TQ), TQ)]
    factor = (HEAD_DIM ** -0.5) * LOG2E

    def body(tile, carry):
        top, total, acc = carry
        start = pl.multiple_of(tile * TK, TK)
        scores = lax.dot_general(
            keys[pl.ds(start, TK), :], queries, (((1,), (0,)), ((), ())),
            preferred_element_type=jnp.float32)
        wide = seg_wide[pl.ds(start, TK), :]
        same = jnp.concatenate([wide] * (TQ // 128), axis=1) == query_seg
        scores = jnp.where(same, scores, -jnp.inf)
        new_top = jnp.maximum(top, jnp.max(scores, axis=0, keepdims=True))
        safe = jnp.where(new_top == -jnp.inf, 0.0, new_top)
        decay = jnp.exp2((top - safe) * factor)
        expo = jnp.exp2((scores - safe) * factor)
        total = total * decay + jnp.sum(expo, axis=0, keepdims=True)
        values = qkv[tile // per_chunk, 2 * HEAD_DIM:3 * HEAD_DIM,
                     pl.ds(pl.multiple_of((tile % per_chunk) * TK, TK), TK)]
        acc = acc * decay + lax.dot_general(
            values, expo.astype(jnp.bfloat16), (((1,), (0,)), ((), ())),
            preferred_element_type=jnp.float32)
        return new_top, total, acc

    first, last = bounds[0, step], bounds[1, step]
    _, total, acc = lax.fori_loop(
        first, last, body,
        (jnp.full((1, TQ), -jnp.inf, jnp.float32), jnp.zeros((1, TQ), jnp.float32),
         jnp.zeros((HEAD_DIM, TQ), jnp.float32)))
    result = (acc / total).astype(jnp.bfloat16)
    for copy in range(out.shape[1]):
        out[0, copy] = result


def attention(qkv, segments, segment_ids, copies):
    tiles, _, chunk = qkv.shape
    count = tiles * chunk
    edges = segment_ids.reshape(count // TK, TK)
    key_low, key_high = edges[:, 0], edges[:, -1]
    query_edges = segment_ids.reshape(count // TQ, TQ)
    query_low, query_high = query_edges[:, 0], query_edges[:, -1]
    first = jnp.sum(key_high[None, :] < query_low[:, None], axis=1)
    last = jnp.sum(key_low[None, :] <= query_high[:, None], axis=1)
    bounds = jnp.stack([first, last]).astype(jnp.int32)
    per = chunk // TQ
    return pl.pallas_call(
        attention_kernel,
        out_shape=jax.ShapeDtypeStruct((tiles, copies, HEAD_DIM, chunk), jnp.bfloat16),
        grid_spec=pltpu.PrefetchScalarGridSpec(
            num_scalar_prefetch=1,
            grid=(count // TQ,),
            in_specs=[
                pl.BlockSpec(qkv.shape, lambda i, b: (0, 0, 0)),
                pl.BlockSpec((count, 1), lambda i, b: (0, 0)),
                pl.BlockSpec((1, count), lambda i, b: (0, 0)),
            ],
            out_specs=pl.BlockSpec((1, copies, HEAD_DIM, TQ), lambda i, b: (i // per, 0, 0, i % per)),
            scratch_shapes=[pltpu.VMEM((count, HEAD_DIM), jnp.bfloat16), pltpu.VMEM((count, 128), jnp.int32)],
        ),
        name="attention",
    )(bounds, qkv, segments[:, None], segments[None, :])


def shift_cols(value, step, cols):
    return lax.ppermute(value, "x", [(at, (at + step) % cols) for at in range(cols)])


def shift_planes(value, step, planes):
    return lax.ppermute(value, "z", [(at, (at + step) % planes) for at in range(planes)])


def matmul(left, right, left_dim, right_dim):
    return lax.dot_general(
        left, right, (((left_dim,), (right_dim,)), ((), ())), preferred_element_type=jnp.float32)


def whole(shape):
    return pl.BlockSpec(shape, lambda *_: (0,) * len(shape))


def spread_kernel(tokens, out, wide):
    copies, count, _ = out.shape
    group = count // 4
    for lane in range(wide.shape[0]):
        wide[lane] = tokens[:, lane * 128:(lane + 1) * 128].astype(jnp.float32)
        for spot in range(4):
            part = wide[lane, pl.ds(spot, group, stride=4), :].astype(jnp.bfloat16)
            for copy in range(copies):
                out[copy, spot * group:(spot + 1) * group, lane * 128:(lane + 1) * 128] = part


def spread_tokens(tokens, copies):
    count, width = tokens.shape
    return pl.pallas_call(
        spread_kernel,
        out_shape=jax.ShapeDtypeStruct((copies, count, width), jnp.bfloat16),
        grid=(1,),
        in_specs=[whole(tokens.shape)],
        out_specs=whole((copies, count, width)),
        scratch_shapes=[pltpu.VMEM((width // 128, count, 128), jnp.float32)],
        name="spread",
    )(tokens)


def qkv_kernel(place, tokens, gain, own, first, second, third, other, out, normed):
    row, core = place[0], place[1]
    rows, wide, _ = out.shape
    half = D // 2
    count = normed.shape[0]
    value = layer_norm(tokens[...].reshape(count, D).astype(jnp.float32), gain[...])
    normed[...] = value.astype(jnp.bfloat16)
    out[row] = matmul(own[...], normed[...], 1, 1).astype(jnp.bfloat16)
    mine = normed[:, pl.ds(pl.multiple_of(core * half, half), half)]
    rest = normed[:, pl.ds(pl.multiple_of((1 - core) * half, half), half)]
    for index, part in enumerate((first, second, third)):
        value = matmul(part[0:wide, :], mine, 1, 1) + matmul(other[index], rest, 1, 1)
        out[(row + 1 + index) % rows] = value.astype(jnp.bfloat16)


def project_qkv(place, row_tokens, gain, weights, parts, other, rows):
    cols, count, _ = row_tokens.shape
    wide = weights.shape[0]
    return pl.pallas_call(
        qkv_kernel,
        out_shape=jax.ShapeDtypeStruct((rows, wide, cols * count), jnp.bfloat16),
        grid_spec=pltpu.PrefetchScalarGridSpec(
            num_scalar_prefetch=1,
            grid=(cols // 2,),
            in_specs=[pl.BlockSpec((2, count, D), lambda i, p: (i, 0, 0)), whole((1, D)), whole(weights.shape)]
            + [whole(part.shape) for part in parts] + [whole(other.shape)],
            out_specs=pl.BlockSpec((rows, wide, 2 * count), lambda i, p: (0, 0, i)),
            scratch_shapes=[pltpu.VMEM((2 * count, D), jnp.bfloat16)],
        ),
        name="project_qkv",
    )(place, row_tokens, gain[None], weights, *parts, other)


def hidden_kernel(place, back, residual, mine, other, gain, out, left, hidden):
    row, col, core = place[0], place[1], place[2]
    cols, rows = mine.shape[0], mine.shape[1]
    half = D // 2
    count = hidden.shape[0]
    for at_col in range(cols):
        for at_row in range(rows):
            head = ((row + at_row) % rows) * cols + (col + cols - at_col) % cols
            at = (at_col * rows + at_row) * HEAD_DIM
            left[at:at + HEAD_DIM, :] = back[head]
    turned = left[...].T
    hidden[:, pl.ds(pl.multiple_of(core * half, half), half)] = matmul(turned, mine[...].reshape(D, half), 1, 0)
    hidden[:, pl.ds(pl.multiple_of((1 - core) * half, half), half)] = matmul(
        turned, other[...].reshape(D, half), 1, 0)
    total = residual[...].reshape(count, D).astype(jnp.float32) + hidden[...]
    value = layer_norm(total, gain[...]).astype(jnp.bfloat16)
    group = count // 4
    for spot in range(4):
        out[spot, 0] = value[spot * group:(spot + 1) * group, :]


def merge_rows(place, back, row_tokens, mine, other, gain):
    cols, count, _ = row_tokens.shape
    return pl.pallas_call(
        hidden_kernel,
        out_shape=jax.ShapeDtypeStruct((4, cols, count // 4, D), jnp.bfloat16),
        grid_spec=pltpu.PrefetchScalarGridSpec(
            num_scalar_prefetch=1,
            grid=(cols,),
            in_specs=[
                pl.BlockSpec((HEADS, HEAD_DIM, count), lambda i, p: (0, 0, i)),
                pl.BlockSpec((1, count, D), lambda i, p: (i, 0, 0)),
                whole(mine.shape), whole(other.shape), whole((1, D)),
            ],
            out_specs=pl.BlockSpec((4, 1, count // 4, D), lambda i, p: (0, i, 0, 0)),
            scratch_shapes=[pltpu.VMEM((D, count), jnp.bfloat16), pltpu.VMEM((count, D), jnp.float32)],
        ),
        name="merge_rows",
    )(place, back, row_tokens, mine, other, gain[None])


def merge_kernel(order, rows, own, *rest):
    parts, out = rest[:-1], rest[-1]
    width = own.shape[1]
    total = matmul(rows[0], own[0:D, :], 1, 0)
    for spot in range(1, 4):
        total = total + matmul(rows[spot], own[spot * D:(spot + 1) * D, :], 1, 0)
    out[:, 0:width] = total.astype(jnp.bfloat16)
    for block in range(len(parts) // 4):
        total = matmul(rows[order[0]], parts[4 * block][...], 1, 0)
        for index in range(1, 4):
            total = total + matmul(rows[order[index]], parts[4 * block + index][...], 1, 0)
        out[:, (block + 1) * width:(block + 2) * width] = total.astype(jnp.bfloat16)


def merge(order, rows, own, parts):
    width = own.shape[1] * (1 + len(parts) // 4)
    return pl.pallas_call(
        merge_kernel,
        out_shape=jax.ShapeDtypeStruct((rows.shape[1], width), jnp.bfloat16),
        grid_spec=pltpu.PrefetchScalarGridSpec(
            num_scalar_prefetch=1,
            grid=(1,),
            in_specs=[whole(rows.shape), whole(own.shape)] + [whole(part.shape) for part in parts],
            out_specs=whole((rows.shape[1], width)),
        ),
        name="merge",
    )(order, rows, own, *parts)


BACK_BY = (0, 1, 3, 2)


def place_kernel(place, got, out):
    cols, _, wide = got.shape
    rows = len(BACK_BY)
    width = wide // rows
    for at_col in range(cols):
        for index, back_by in enumerate(BACK_BY):
            at = (((place[0] + rows - back_by) % rows) * cols + at_col) * width
            out[:, pl.ds(pl.multiple_of(at, width), width)] = got[at_col, :, index * width:(index + 1) * width]


def place_columns(place, got):
    cols, count, wide = got.shape
    return pl.pallas_call(
        place_kernel,
        out_shape=jax.ShapeDtypeStruct((count, cols * wide), jnp.bfloat16),
        grid_spec=pltpu.PrefetchScalarGridSpec(
            num_scalar_prefetch=1, grid=(1,), in_specs=[whole(got.shape)],
            out_specs=whole((count, cols * wide))),
        name="place_columns",
    )(place, got)


def block_step(tokens, segment_ids, w_qkv, w_out, w_merge, gain_attn, gain_merge):
    rows, cols, planes = lax.axis_size("y"), lax.axis_size("x"), lax.axis_size("z")
    row, col, core = lax.axis_index("y"), lax.axis_index("x"), lax.axis_index("c")
    parity = lax.axis_index("z") % 2
    tok_local = tokens.shape[0]
    groups = tok_local // 4
    row_count = cols * tok_local
    half = D // 2
    wide = w_qkv.shape[1]
    row_tokens = lax.all_to_all(
        spread_tokens(tokens, cols), "x", split_axis=0, concat_axis=0, tiled=True)
    segments = segment_ids.reshape(rows * cols, groups, 4).transpose(0, 2, 1).reshape(-1)

    weights = w_qkv.T
    own = jnp.concatenate([
        lax.dynamic_slice_in_dim(weights, core * half, half, 1),
        lax.dynamic_slice_in_dim(w_out, core * half, half, 1)], axis=0)
    ahead = [shift_rows(own, step, rows) for step in (3, 2, 1)]
    other_qkv = swap_cores(jnp.stack([part[:wide] for part in ahead]))

    order = [parity * 2 + core, (1 - parity) * 2 + core, parity * 2 + 1 - core, (1 - parity) * 2 + 1 - core]
    own_piece = lax.dynamic_slice_in_dim(w_merge, order[0] * D, D, 0)
    first_y = shift_rows(own_piece, 1, rows)
    third_y = shift_rows(own_piece, 3, rows)

    qkv = project_qkv(
        jnp.stack([row, core]).astype(jnp.int32), row_tokens, gain_attn, weights, ahead, other_qkv, rows)
    by_head = lax.all_to_all(qkv, "y", split_axis=0, concat_axis=0, tiled=True)

    out_rows = jnp.stack([own[wide:]] + [part[wide:] for part in ahead])
    out_parts = [out_rows] + [shift_cols(out_rows, step, cols) for step in (1, 2, 3)]
    first_z = shift_planes(first_y, 1, planes)
    third_z = shift_planes(third_y, planes - 1, planes)
    second_y = shift_rows(own_piece, 2, rows)

    attended = attention(by_head, segments, segment_ids, cols)
    back = lax.all_to_all(
        attended.reshape(rows * cols, HEAD_DIM, row_count), ("y", "x"),
        split_axis=0, concat_axis=0, tiled=True)
    second_z = shift_planes(second_y, 1, planes)
    mine_out = jnp.stack(out_parts)
    other_out = swap_cores(mine_out)
    parts = []
    for part_y, part_z in ((first_y, first_z), (third_y, third_z)):
        parts += [part_y, part_z, swap_cores(part_y), swap_cores(part_z)]
    parts += [second_y, second_z, swap_cores(second_y), swap_cores(second_z)]

    merged = merge_rows(
        jnp.stack([row, col, core]).astype(jnp.int32), back, row_tokens, mine_out, other_out, gain_merge)
    block = merge(
        jnp.stack(order).astype(jnp.int32), merged.reshape(4, cols * groups, D), w_merge, parts)
    got = lax.all_to_all(
        block.reshape(cols, groups, block.shape[1]), "x", split_axis=0, concat_axis=0, tiled=True)
    return place_columns(row[None].astype(jnp.int32), got)


def solution(mesh):
    torus = Mesh(mesh.devices.reshape(mesh.shape["dp"] // 2, 2, 4, 4), ("z", "c", "y", "x"))
    dp, seq, both = ("z", "c"), ("y", "x"), ("z", "c", "y", "x")
    in_specs = (P(both, None), P(dp), P(None, seq), P(seq, None), P(None, seq), P(), P())
    return jax.shard_map(block_step, mesh=torus, in_specs=in_specs, out_specs=P(both, None), check_vma=False)
```

profile of v0, /device:TPU:320, one launch (start us, length us, event | category | flops | bytes accessed | tf_op | source)
XLA Modules:
  0.0 179.7 jit_solution(5219386013392631977)
XLA Ops:
  0.0 1.0 dynamic-slice_bitcast_fusion
  1.1 3.5 %collective-permute-start.2 = (bf16[320,640]{1,0:T(8,128)(2,1)S(1)}, bf16[320,640]{1,0:T(8,128)(2,1)S(1)}, u32[]{:S(2)}, u32[]{:S(2)}) collective-permute-start(bf16[320,640]{1,0:T(8,128)(2,1)S(1)} %pad_maximum_fusion.2), channel_id=1, source_target_pairs={{0,4},{4,8},{8,12},{12,0},{1,5},{5,9},{9,13},{13,1},{2,6},{6,10},{... | collective-permute-start | bytes 1228808 | tf_op jit(solution)/shard_map/ppermute | solution.py:30
  4.6 4.8 %collective-permute-start.1 = (bf16[320,640]{1,0:T(8,128)(2,1)S(1)}, bf16[320,640]{1,0:T(8,128)(2,1)S(1)}, u32[]{:S(2)}, u32[]{:S(2)}) collective-permute-start(bf16[320,640]{1,0:T(8,128)(2,1)S(1)} %pad_maximum_fusion.2), channel_id=1, source_target_pairs={{0,8},{4,12},{8,0},{12,4},{1,9},{5,13},{9,1},{13,5},{2,10},{6,14},... | collective-permute-start | bytes 1228808 | tf_op jit(solution)/shard_map/ppermute | solution.py:30
  9.4 3.3 %collective-permute-start = (bf16[320,640]{1,0:T(8,128)(2,1)S(1)}, bf16[320,640]{1,0:T(8,128)(2,1)S(1)}, u32[]{:S(2)}, u32[]{:S(2)}) collective-permute-start(bf16[320,640]{1,0:T(8,128)(2,1)S(1)} %pad_maximum_fusion.2), channel_id=1, source_target_pairs={{0,12},{4,0},{8,4},{12,8},{1,13},{5,1},{9,5},{13,9},{2,14},{6,2},{... | collective-permute-start | bytes 1228808 | tf_op jit(solution)/shard_map/ppermute | solution.py:30
  12.7 2.3 %spread.1 = bf16[4,128,1280]{2,1,0:T(8,128)(2,1)} custom-call(bf16[128,1280]{1,0:T(8,128)(2,1)} %tokens.1), custom_call_target="tpu_custom_call" | custom-call | tf_op jit(solution)/shard_map/spread/pallas_call | solution.py:140
  15.0 4.3 %all-to-all-start = ((bf16[4,128,1280]{2,1,0:T(8,128)(2,1)}), bf16[4,128,1280]{2,1,0:T(8,128)(2,1)S(1)}, u32[]{:S(2)}, u32[]{:S(2)}) async-start(bf16[4,128,1280]{2,1,0:T(8,128)(2,1)} %spread.1), calls=%async_computation | async-start | bytes 2621440 | tf_op jit(solution)/shard_map/all_to_all | solution.py:288
  19.3 0.0 collective-permute-done.2.third
  19.4 6.1 %collective-permute-done.1.second = bf16[320,640]{1,0:T(8,128)(2,1)S(1)} collective-permute-done((bf16[320,640]{1,0:T(8,128)(2,1)S(1)}, bf16[320,640]{1,0:T(8,128)(2,1)S(1)}, u32[]{:S(2)}, u32[]{:S(2)}) %collective-permute-start.1) | collective-permute-done | bytes 409632 | tf_op jit(solution)/shard_map/ppermute | solution.py:30
  25.5 1.4 collective-permute-done.first
  26.8 1.1 fusion
  27.9 3.4 %collective-permute-start.4 = (bf16[4,80,640]{2,1,0:T(8,128)(2,1)}, bf16[4,80,640]{2,1,0:T(8,128)(2,1)S(1)}, u32[]{:S(2)}, u32[]{:S(2)}) collective-permute-start(bf16[4,80,640]{2,1,0:T(8,128)(2,1)} %get-tuple-element.10), channel_id=1, source_target_pairs={{0,1},{1,2},{2,3},{3,0},{4,5},{5,6},{6,7},{7,4},{8,9},{9,10},{10,1... | collective-permute-start | bytes 1228808 | tf_op jit(solution)/shard_map/ppermute | solution.py:111
  31.3 4.6 %collective-permute-start.5 = (bf16[4,80,640]{2,1,0:T(8,128)(2,1)}, bf16[4,80,640]{2,1,0:T(8,128)(2,1)}, u32[]{:S(2)}, u32[]{:S(2)}) collective-permute-start(bf16[4,80,640]{2,1,0:T(8,128)(2,1)} %get-tuple-element.10), channel_id=1, source_target_pairs={{0,2},{1,3},{2,0},{3,1},{4,6},{5,7},{6,4},{7,5},{8,10},{9,11},{10,... | collective-permute-start | bytes 1228808 | tf_op jit(solution)/shard_map/ppermute | solution.py:111
  36.0 3.3 %collective-permute-start.6 = (bf16[4,80,640]{2,1,0:T(8,128)(2,1)}, bf16[4,80,640]{2,1,0:T(8,128)(2,1)}, u32[]{:S(2)}, u32[]{:S(2)}) collective-permute-start(bf16[4,80,640]{2,1,0:T(8,128)(2,1)} %get-tuple-element.10), channel_id=1, source_target_pairs={{0,3},{1,0},{2,1},{3,2},{4,7},{5,4},{6,5},{7,6},{8,11},{9,8},{10,9... | collective-permute-start | bytes 1228808 | tf_op jit(solution)/shard_map/ppermute | solution.py:111
  39.4 1.1 pad_maximum_fusion.1
  40.5 1.9 %collective-permute-start.3 = (bf16[3,240,640]{2,1,0:T(8,128)(2,1)}, bf16[3,240,640]{2,1,0:T(8,128)(2,1)}, u32[]{:S(2)}, u32[]{:S(2)}) collective-permute-start(bf16[3,240,640]{2,1,0:T(8,128)(2,1)} %pad_maximum_fusion.1), channel_id=1, source_target_pairs={{0,16},{16,0},{1,17},{17,1},{2,18},{18,2},{3,19},{19,3},{4,20},{20... | collective-permute-start | bytes 2764808 | tf_op jit(solution)/shard_map/ppermute | solution.py:26
  42.4 5.0 %collective-permute-done.4 = bf16[4,80,640]{2,1,0:T(8,128)(2,1)S(1)} collective-permute-done((bf16[4,80,640]{2,1,0:T(8,128)(2,1)}, bf16[4,80,640]{2,1,0:T(8,128)(2,1)S(1)}, u32[]{:S(2)}, u32[]{:S(2)}) %collective-permute-start.4) | collective-permute-done | bytes 409632 | tf_op jit(solution)/shard_map/ppermute | solution.py:111
  47.4 6.6 %collective-permute-done.5 = bf16[4,80,640]{2,1,0:T(8,128)(2,1)} collective-permute-done((bf16[4,80,640]{2,1,0:T(8,128)(2,1)}, bf16[4,80,640]{2,1,0:T(8,128)(2,1)}, u32[]{:S(2)}, u32[]{:S(2)}) %collective-permute-start.5) | collective-permute-done | bytes 409632 | tf_op jit(solution)/shard_map/ppermute | solution.py:111
  54.0 1.6 pad_maximum_fusion.mine
  55.7 1.9 %collective-permute-start.7 = (bf16[4,4,80,640]{3,2,1,0:T(8,128)(2,1)S(1)}, bf16[4,4,80,640]{3,2,1,0:T(8,128)(2,1)}, u32[]{:S(2)}, u32[]{:S(2)}) collective-permute-start(bf16[4,4,80,640]{3,2,1,0:T(8,128)(2,1)S(1)} %pad_maximum_fusion.mine), channel_id=1, source_target_pairs={{0,16},{16,0},{1,17},{17,1},{2,18},{18,2},{3,19},{19,3},{4,20},{20... | collective-permute-start | bytes 4915208 | tf_op jit(solution)/shard_map/ppermute | solution.py:26
  57.6 2.0 %constant_dynamic-slice_fusion = bf16[1280,256]{1,0:T(8,128)(2,1)} fusion(bf16[5120,256]{1,0:T(8,128)(2,1)} %own.1, s32[]{:T(128)S(6)} %select_n.16), kind=kLoop, calls=%fused_computation.16 | loop fusion | bytes 1310724 | tf_op jit(solution)/shard_map/dynamic_slice | solution.py:300
  59.6 4.4 %collective-permute-start.8 = (bf16[1280,256]{1,0:T(8,128)(2,1)}, bf16[1280,256]{1,0:T(8,128)(2,1)}, u32[]{:S(2)}, u32[]{:S(2)}) collective-permute-start(bf16[1280,256]{1,0:T(8,128)(2,1)} %constant_dynamic-slice_fusion), channel_id=1, source_target_pairs={{0,4},{4,8},{8,12},{12,0},{1,5},{5,9},{9,13},{13,1},{2,6},{6,10},{... | collective-permute-start | bytes 1966088 | tf_op jit(solution)/shard_map/ppermute | solution.py:30
  64.0 2.7 %collective-permute-start.12 = (bf16[1280,256]{1,0:T(8,128)(2,1)}, bf16[1280,256]{1,0:T(8,128)(2,1)}, u32[]{:S(2)}, u32[]{:S(2)}) collective-permute-start(bf16[1280,256]{1,0:T(8,128)(2,1)} %constant_dynamic-slice_fusion), channel_id=1, source_target_pairs={{0,12},{4,0},{8,4},{12,8},{1,13},{5,1},{9,5},{13,9},{2,14},{6,2},{... | collective-permute-start | bytes 1966088 | tf_op jit(solution)/shard_map/ppermute | solution.py:30
  66.7 3.2 %collective-permute-start.16 = (bf16[1280,256]{1,0:T(8,128)(2,1)}, bf16[1280,256]{1,0:T(8,128)(2,1)}, u32[]{:S(2)}, u32[]{:S(2)}) collective-permute-start(bf16[1280,256]{1,0:T(8,128)(2,1)} %constant_dynamic-slice_fusion), channel_id=1, source_target_pairs={{0,8},{4,12},{8,0},{12,4},{1,9},{5,13},{9,1},{13,5},{2,10},{6,14},... | collective-permute-start | bytes 1966088 | tf_op jit(solution)/shard_map/ppermute | solution.py:30
  69.9 0.6 pad_add_fusion.3.place
  70.5 0.6 broadcast_in_dim.10.gain
  71.1 0.0 all-to-all-done.tokens.residual
  71.1 0.0 collective-permute-done.3.other
  71.1 1.0 copy-done.1
  72.2 6.4 %project_qkv.1 = bf16[4,240,512]{2,1,0:T(8,128)(2,1)} custom-call(s32[2]{0:T(128)} %pad_add_fusion.3.place, bf16[4,128,1280]{2,1,0:T(8,128)(2,1)} %copy-done.1, f32[1,1280]{1,0:T(1,128)} %broadcast_in_dim.10.gain, bf16[240,1280]{1,0:T(8,128)(2,1)} %bitcast.37, bf16[320,640]{1,0:T(8,128)(2,1)} %copy-done.7, bf16[320,640]{1,0:T(8,128)(2,1)} %copy-done.6, ...), custom_call_target="tpu_custom_call" | custom-call | tf_op jit(solution)/shard_map/project_qkv/pallas_call | solution.py:169
  78.5 4.0 %all-to-all-start.1 = ((bf16[4,240,512]{2,1,0:T(8,128)(2,1)}), bf16[4,240,512]{2,1,0:T(8,128)(2,1)S(1)}, u32[]{:S(2)}, u32[]{:S(2)}) async-start(bf16[4,240,512]{2,1,0:T(8,128)(2,1)} %project_qkv.1), calls=%async_computation.1 | async-start | bytes 1966080 | tf_op jit(solution)/shard_map/all_to_all | solution.py:306
  82.6 0.3 reshape.19
  82.8 0.2 copy.14
  83.0 2.1 %broadcast_in_dim_reshape.8.seg_col = s32[2048,1]{1,0:T(8,128)} reshape(s32[16,4,32]{2,1,0:T(4,128)S(1)} %copy.14) | data formatting | bytes 16384 | tf_op jit(solution)/shard_map/broadcast_in_dim;reshape | solution.py:107
  85.1 0.7 broadcast_in_dim_reshape.7.seg_row
  85.8 0.2 slice_reduce_fusion.1
  85.9 0.2 convert_reduce_fusion.1
  86.2 0.0 collective-permute-done.8.rest_0_
  86.2 2.9 %collective-permute-start.9 = (bf16[1280,256]{1,0:T(8,128)(2,1)}, bf16[1280,256]{1,0:T(8,128)(2,1)}, u32[]{:S(2)}, u32[]{:S(2)}) collective-permute-start(bf16[1280,256]{1,0:T(8,128)(2,1)} %collective-permute-done.8.rest_0_), channel_id=1, source_target_pairs={{0,32},{32,64},{64,96},{96,128},{128,160},{160,192},{192,224},{224... | collective-permute-start | bytes 1966088 | tf_op jit(solution)/shard_map/ppermute | solution.py:115
  89.1 1.9 %collective-permute-start.10 = (bf16[1280,256]{1,0:T(8,128)(2,1)}, bf16[1280,256]{1,0:T(8,128)(2,1)}, u32[]{:S(2)}, u32[]{:S(2)}) collective-permute-start(bf16[1280,256]{1,0:T(8,128)(2,1)} %collective-permute-done.8.rest_0_), channel_id=1, source_target_pairs={{0,16},{16,0},{1,17},{17,1},{2,18},{18,2},{3,19},{19,3},{4,20},{20... | collective-permute-start | bytes 1966088 | tf_op jit(solution)/shard_map/ppermute | solution.py:26
  91.0 2.9 %collective-permute-start.13 = (bf16[1280,256]{1,0:T(8,128)(2,1)}, bf16[1280,256]{1,0:T(8,128)(2,1)}, u32[]{:S(2)}, u32[]{:S(2)}) collective-permute-start(bf16[1280,256]{1,0:T(8,128)(2,1)} %collective-permute-done.12.rest_4_), channel_id=1, source_target_pairs={{0,480},{32,0},{64,32},{96,64},{128,96},{160,128},{192,160},{224,1... | collective-permute-start | bytes 1966088 | tf_op jit(solution)/shard_map/ppermute | solution.py:115
  94.0 1.6 collective-permute-done.16.rest_8_
  95.6 2.9 %collective-permute-start.17 = (bf16[1280,256]{1,0:T(8,128)(2,1)}, bf16[1280,256]{1,0:T(8,128)(2,1)}, u32[]{:S(2)}, u32[]{:S(2)}) collective-permute-start(bf16[1280,256]{1,0:T(8,128)(2,1)} %collective-permute-done.16.rest_8_), channel_id=1, source_target_pairs={{0,32},{32,64},{64,96},{96,128},{128,160},{160,192},{192,224},{224... | collective-permute-start | bytes 1966088 | tf_op jit(solution)/shard_map/ppermute | solution.py:115
  98.5 0.5 pad_add_fusion.bounds
  99.0 6.5 %all-to-all-done.1.qkv = bf16[4,240,512]{2,1,0:T(8,128)(2,1)S(1)} async-done(((bf16[4,240,512]{2,1,0:T(8,128)(2,1)}), bf16[4,240,512]{2,1,0:T(8,128)(2,1)S(1)}, u32[]{:S(2)}, u32[]{:S(2)}) %all-to-all-start.1) | async-done | bytes 983072 | tf_op jit(solution)/shard_map/all_to_all | solution.py:306
  105.5 0.9 copy-done.4
  106.5 11.2 %attention.1 = bf16[4,4,80,512]{3,2,1,0:T(8,128)(2,1)} custom-call(s32[2,4]{1,0:T(2,128)} %pad_add_fusion.bounds, bf16[4,240,512]{2,1,0:T(8,128)(2,1)} %copy-done.4, s32[2048,1]{1,0:T(8,128)} %broadcast_in_dim_reshape.8.seg_col, s32[1,2048]{1,0:T(1,128)} %broadcast_in_dim_reshape.7.seg_row), custom_call_target="tpu_custom_call" | custom-call | tf_op jit(solution)/shard_map/attention/pallas_call | solution.py:92
  117.7 8.6 %all-to-all-start.2 = ((bf16[16,80,512]{2,1,0:T(8,128)(2,1)}), bf16[16,80,512]{2,1,0:T(8,128)(2,1)S(1)}, u32[]{:S(2)}, u32[]{:S(2)}) async-start(bf16[16,80,512]{2,1,0:T(8,128)(2,1)} %bitcast.36), calls=%async_computation.2 | async-start | bytes 2621440 | tf_op jit(solution)/shard_map/all_to_all | solution.py:315
  126.4 0.0 collective-permute-done.9.rest_1_
  126.4 3.5 %collective-permute-start.14 = (bf16[1280,256]{1,0:T(8,128)(2,1)}, bf16[1280,256]{1,0:T(8,128)(2,1)}, u32[]{:S(2)}, u32[]{:S(2)}) collective-permute-start(bf16[1280,256]{1,0:T(8,128)(2,1)} %collective-permute-done.12.rest_4_), channel_id=1, source_target_pairs={{0,16},{16,0},{1,17},{17,1},{2,18},{18,2},{3,19},{19,3},{4,20},{20... | collective-permute-start | bytes 1966088 | tf_op jit(solution)/shard_map/ppermute | solution.py:26
  129.9 0.0 collective-permute-done.13.rest_5_
  129.9 1.9 %collective-permute-start.18 = (bf16[1280,256]{1,0:T(8,128)(2,1)}, bf16[1280,256]{1,0:T(8,128)(2,1)}, u32[]{:S(2)}, u32[]{:S(2)}) collective-permute-start(bf16[1280,256]{1,0:T(8,128)(2,1)} %collective-permute-done.16.rest_8_), channel_id=1, source_target_pairs={{0,16},{16,0},{1,17},{17,1},{2,18},{18,2},{3,19},{19,3},{4,20},{20... | collective-permute-start | bytes 1966088 | tf_op jit(solution)/shard_map/ppermute | solution.py:26
  131.9 2.4 %collective-permute-start.11 = (bf16[1280,256]{1,0:T(8,128)(2,1)}, bf16[1280,256]{1,0:T(8,128)(2,1)}, u32[]{:S(2)}, u32[]{:S(2)}) collective-permute-start(bf16[1280,256]{1,0:T(8,128)(2,1)} %collective-permute-done.9.rest_1_), channel_id=1, source_target_pairs={{0,16},{16,0},{1,17},{17,1},{2,18},{18,2},{3,19},{19,3},{4,20},{20... | collective-permute-start | bytes 1966088 | tf_op jit(solution)/shard_map/ppermute | solution.py:26
  134.3 1.9 %collective-permute-start.15 = (bf16[1280,256]{1,0:T(8,128)(2,1)}, bf16[1280,256]{1,0:T(8,128)(2,1)}, u32[]{:S(2)}, u32[]{:S(2)}) collective-permute-start(bf16[1280,256]{1,0:T(8,128)(2,1)} %collective-permute-done.13.rest_5_), channel_id=1, source_target_pairs={{0,16},{16,0},{1,17},{17,1},{2,18},{18,2},{3,19},{19,3},{4,20},{20... | collective-permute-start | bytes 1966088 | tf_op jit(solution)/shard_map/ppermute | solution.py:26
  136.2 2.4 %collective-permute-start.19 = (bf16[1280,256]{1,0:T(8,128)(2,1)}, bf16[1280,256]{1,0:T(8,128)(2,1)S(1)}, u32[]{:S(2)}, u32[]{:S(2)}) collective-permute-start(bf16[1280,256]{1,0:T(8,128)(2,1)} %collective-permute-done.17.rest_9_), channel_id=1, source_target_pairs={{0,16},{16,0},{1,17},{17,1},{2,18},{18,2},{3,19},{19,3},{4,20},{20... | collective-permute-start | bytes 1966088 | tf_op jit(solution)/shard_map/ppermute | solution.py:26
  138.7 0.6 broadcast_in_dim.11.gain
  139.3 0.6 pad_add_fusion.2.place
  139.9 0.7 pad_add_fusion.1.order
  140.5 8.5 %all-to-all-done.2.back = bf16[16,80,512]{2,1,0:T(8,128)(2,1)S(1)} async-done(((bf16[16,80,512]{2,1,0:T(8,128)(2,1)}), bf16[16,80,512]{2,1,0:T(8,128)(2,1)S(1)}, u32[]{:S(2)}, u32[]{:S(2)}) %all-to-all-start.2) | async-done | bytes 1310752 | tf_op jit(solution)/shard_map/all_to_all | solution.py:315
  149.1 1.0 copy-done.3
  150.1 7.9 %merge_rows.1 = bf16[4,4,32,1280]{3,2,1,0:T(8,128)(2,1)} custom-call(s32[3]{0:T(128)} %pad_add_fusion.2.place, bf16[16,80,512]{2,1,0:T(8,128)(2,1)} %copy-done.3, bf16[4,128,1280]{2,1,0:T(8,128)(2,1)} %copy-done.1, bf16[4,4,80,640]{3,2,1,0:T(8,128)(2,1)} %copy-done.2, bf16[4,4,80,640]{3,2,1,0:T(8,128)(2,1)} %collective-permute-done.7.other, ...), custom_call_target="tpu_custom_call" | custom-call | tf_op jit(solution)/shard_map/merge_rows/pallas_call | solution.py:207
  158.1 0.8 copy-done.8
  158.9 7.4 %merge.1 = bf16[128,1024]{1,0:T(8,128)(2,1)} custom-call(s32[4]{0:T(128)} %pad_add_fusion.1.order, bf16[4,128,1280]{2,1,0:T(8,128)(2,1)} %bitcast.35, bf16[5120,256]{1,0:T(8,128)(2,1)} %own.1, bf16[1280,256]{1,0:T(8,128)(2,1)} %collective-permute-done.8.rest_0_, bf16[1280,256]{1,0:T(8,128)(2,1)} %collective-permute-done.9.rest_1_, ...), custom_call_target="tpu_custom_call" | custom-call | tf_op jit(solution)/shard_map/merge/pallas_call | solution.py:241
  166.3 11.7 %all_to_all.20.got = bf16[4,32,1024]{2,1,0:T(8,128)(2,1)} all-to-all(bf16[4,32,1024]{2,1,0:T(8,128)(2,1)} %bitcast.38), channel_id=1, replica_groups=mesh['z'=16,'c'=2,'y'=4,'x'=4] {'x'}, dimensions={0} | all-to-all | bytes 524288 | tf_op jit(solution)/shard_map/all_to_all | solution.py:330
  178.0 1.7 place_columns.1
  (42 shorter events, 0.3 us)
Async XLA Ops:
  0.0 1.0 copy-start
  1.1 18.2 %collective-permute-start.2 = (bf16[320,640]{1,0:T(8,128)(2,1)S(1)}, bf16[320,640]{1,0:T(8,128)(2,1)S(1)}, u32[]{:S(2)}, u32[]{:S(2)}) collective-permute-start(bf16[320,640]{1,0:T(8,128)(2,1)S(1)} %pad_maximum_fusion.2), channel_id=1, source_target_pairs={{0,4},{4,8},{8,12},{12,0},{1,5},{5,9},{9,13},{13,1},{2,6},{6,10},{... | collective-permute-start | bytes 1228808 | tf_op jit(solution)/shard_map/ppermute | solution.py:30
  4.6 20.8 %collective-permute-start.1 = (bf16[320,640]{1,0:T(8,128)(2,1)S(1)}, bf16[320,640]{1,0:T(8,128)(2,1)S(1)}, u32[]{:S(2)}, u32[]{:S(2)}) collective-permute-start(bf16[320,640]{1,0:T(8,128)(2,1)S(1)} %pad_maximum_fusion.2), channel_id=1, source_target_pairs={{0,8},{4,12},{8,0},{12,4},{1,9},{5,13},{9,1},{13,5},{2,10},{6,14},... | collective-permute-start | bytes 1228808 | tf_op jit(solution)/shard_map/ppermute | solution.py:30
  9.4 17.4 %collective-permute-start = (bf16[320,640]{1,0:T(8,128)(2,1)S(1)}, bf16[320,640]{1,0:T(8,128)(2,1)S(1)}, u32[]{:S(2)}, u32[]{:S(2)}) collective-permute-start(bf16[320,640]{1,0:T(8,128)(2,1)S(1)} %pad_maximum_fusion.2), channel_id=1, source_target_pairs={{0,12},{4,0},{8,4},{12,8},{1,13},{5,1},{9,5},{13,9},{2,14},{6,2},{... | collective-permute-start | bytes 1228808 | tf_op jit(solution)/shard_map/ppermute | solution.py:30
  15.0 56.1 %all-to-all-start = ((bf16[4,128,1280]{2,1,0:T(8,128)(2,1)}), bf16[4,128,1280]{2,1,0:T(8,128)(2,1)S(1)}, u32[]{:S(2)}, u32[]{:S(2)}) async-start(bf16[4,128,1280]{2,1,0:T(8,128)(2,1)} %spread.1), calls=%async_computation | async-start | bytes 2621440 | tf_op jit(solution)/shard_map/all_to_all | solution.py:288
  19.3 20.1 %copy-start.5 = (bf16[320,640]{1,0:T(8,128)(2,1)}, bf16[320,640]{1,0:T(8,128)(2,1)S(1)}, u32[]{:S(2)}) copy-start(bf16[320,640]{1,0:T(8,128)(2,1)S(1)} %collective-permute-done.2.third) | copy-start | bytes 1228804
  25.4 14.0 %copy-start.6 = (bf16[320,640]{1,0:T(8,128)(2,1)}, bf16[320,640]{1,0:T(8,128)(2,1)S(1)}, u32[]{:S(2)}) copy-start(bf16[320,640]{1,0:T(8,128)(2,1)S(1)} %collective-permute-done.1.second) | copy-start | bytes 1228804
  26.8 12.6 %copy-start.7 = (bf16[320,640]{1,0:T(8,128)(2,1)}, bf16[320,640]{1,0:T(8,128)(2,1)S(1)}, u32[]{:S(2)}) copy-start(bf16[320,640]{1,0:T(8,128)(2,1)S(1)} %collective-permute-done.first) | copy-start | bytes 1228804
  27.9 19.5 %collective-permute-start.4 = (bf16[4,80,640]{2,1,0:T(8,128)(2,1)}, bf16[4,80,640]{2,1,0:T(8,128)(2,1)S(1)}, u32[]{:S(2)}, u32[]{:S(2)}) collective-permute-start(bf16[4,80,640]{2,1,0:T(8,128)(2,1)} %get-tuple-element.10), channel_id=1, source_target_pairs={{0,1},{1,2},{2,3},{3,0},{4,5},{5,6},{6,7},{7,4},{8,9},{9,10},{10,1... | collective-permute-start | bytes 1228808 | tf_op jit(solution)/shard_map/ppermute | solution.py:111
  31.3 22.7 %collective-permute-start.5 = (bf16[4,80,640]{2,1,0:T(8,128)(2,1)}, bf16[4,80,640]{2,1,0:T(8,128)(2,1)}, u32[]{:S(2)}, u32[]{:S(2)}) collective-permute-start(bf16[4,80,640]{2,1,0:T(8,128)(2,1)} %get-tuple-element.10), channel_id=1, source_target_pairs={{0,2},{1,3},{2,0},{3,1},{4,6},{5,7},{6,4},{7,5},{8,10},{9,11},{10,... | collective-permute-start | bytes 1228808 | tf_op jit(solution)/shard_map/ppermute | solution.py:111
  36.0 18.1 %collective-permute-start.6 = (bf16[4,80,640]{2,1,0:T(8,128)(2,1)}, bf16[4,80,640]{2,1,0:T(8,128)(2,1)}, u32[]{:S(2)}, u32[]{:S(2)}) collective-permute-start(bf16[4,80,640]{2,1,0:T(8,128)(2,1)} %get-tuple-element.10), channel_id=1, source_target_pairs={{0,3},{1,0},{2,1},{3,2},{4,7},{5,4},{6,5},{7,6},{8,11},{9,8},{10,9... | collective-permute-start | bytes 1228808 | tf_op jit(solution)/shard_map/ppermute | solution.py:111
  40.5 30.6 %collective-permute-start.3 = (bf16[3,240,640]{2,1,0:T(8,128)(2,1)}, bf16[3,240,640]{2,1,0:T(8,128)(2,1)}, u32[]{:S(2)}, u32[]{:S(2)}) collective-permute-start(bf16[3,240,640]{2,1,0:T(8,128)(2,1)} %pad_maximum_fusion.1), channel_id=1, source_target_pairs={{0,16},{16,0},{1,17},{17,1},{2,18},{18,2},{3,19},{19,3},{4,20},{20... | collective-permute-start | bytes 2764808 | tf_op jit(solution)/shard_map/ppermute | solution.py:26
  47.4 6.6 %copy-start.9 = (bf16[4,80,640]{2,1,0:T(8,128)(2,1)}, bf16[4,80,640]{2,1,0:T(8,128)(2,1)S(1)}, u32[]{:S(2)}) copy-start(bf16[4,80,640]{2,1,0:T(8,128)(2,1)S(1)} %collective-permute-done.4) | copy-start | bytes 1228804
  54.0 16.5 %copy-start.11 = (f32[1280]{0:T(1024)S(1)}, f32[1280]{0:T(1024)}, u32[]{:S(2)}) copy-start(f32[1280]{0:T(1024)} %param.12) | copy-start | bytes 15364
  55.7 29.4 %copy-start.2 = (bf16[4,4,80,640]{3,2,1,0:T(8,128)(2,1)}, bf16[4,4,80,640]{3,2,1,0:T(8,128)(2,1)S(1)}, u32[]{:S(2)}) copy-start(bf16[4,4,80,640]{3,2,1,0:T(8,128)(2,1)S(1)} %pad_maximum_fusion.mine) | copy-start | bytes 4915204
  55.7 80.5 %collective-permute-start.7 = (bf16[4,4,80,640]{3,2,1,0:T(8,128)(2,1)S(1)}, bf16[4,4,80,640]{3,2,1,0:T(8,128)(2,1)}, u32[]{:S(2)}, u32[]{:S(2)}) collective-permute-start(bf16[4,4,80,640]{3,2,1,0:T(8,128)(2,1)S(1)} %pad_maximum_fusion.mine), channel_id=1, source_target_pairs={{0,16},{16,0},{1,17},{17,1},{2,18},{18,2},{3,19},{19,3},{4,20},{20... | collective-permute-start | bytes 4915208 | tf_op jit(solution)/shard_map/ppermute | solution.py:26
  59.6 26.5 %collective-permute-start.8 = (bf16[1280,256]{1,0:T(8,128)(2,1)}, bf16[1280,256]{1,0:T(8,128)(2,1)}, u32[]{:S(2)}, u32[]{:S(2)}) collective-permute-start(bf16[1280,256]{1,0:T(8,128)(2,1)} %constant_dynamic-slice_fusion), channel_id=1, source_target_pairs={{0,4},{4,8},{8,12},{12,0},{1,5},{5,9},{9,13},{13,1},{2,6},{6,10},{... | collective-permute-start | bytes 1966088 | tf_op jit(solution)/shard_map/ppermute | solution.py:30
  64.0 27.1 %collective-permute-start.12 = (bf16[1280,256]{1,0:T(8,128)(2,1)}, bf16[1280,256]{1,0:T(8,128)(2,1)}, u32[]{:S(2)}, u32[]{:S(2)}) collective-permute-start(bf16[1280,256]{1,0:T(8,128)(2,1)} %constant_dynamic-slice_fusion), channel_id=1, source_target_pairs={{0,12},{4,0},{8,4},{12,8},{1,13},{5,1},{9,5},{13,9},{2,14},{6,2},{... | collective-permute-start | bytes 1966088 | tf_op jit(solution)/shard_map/ppermute | solution.py:30
  66.7 28.9 %collective-permute-start.16 = (bf16[1280,256]{1,0:T(8,128)(2,1)}, bf16[1280,256]{1,0:T(8,128)(2,1)}, u32[]{:S(2)}, u32[]{:S(2)}) collective-permute-start(bf16[1280,256]{1,0:T(8,128)(2,1)} %constant_dynamic-slice_fusion), channel_id=1, source_target_pairs={{0,8},{4,12},{8,0},{12,4},{1,9},{5,13},{9,1},{13,5},{2,10},{6,14},... | collective-permute-start | bytes 1966088 | tf_op jit(solution)/shard_map/ppermute | solution.py:30
  71.1 1.1 copy-start.1
  78.5 4.0 %copy-start.10 = (s32[2048]{0:T(1024)S(1)}, s32[2048]{0:T(1024)}, u32[]{:S(2)}) copy-start(s32[2048]{0:T(1024)} %param.8) | copy-start | bytes 24580
  78.5 27.0 %all-to-all-start.1 = ((bf16[4,240,512]{2,1,0:T(8,128)(2,1)}), bf16[4,240,512]{2,1,0:T(8,128)(2,1)S(1)}, u32[]{:S(2)}, u32[]{:S(2)}) async-start(bf16[4,240,512]{2,1,0:T(8,128)(2,1)} %project_qkv.1), calls=%async_computation.1 | async-start | bytes 1966080 | tf_op jit(solution)/shard_map/all_to_all | solution.py:306
  86.2 40.2 %collective-permute-start.9 = (bf16[1280,256]{1,0:T(8,128)(2,1)}, bf16[1280,256]{1,0:T(8,128)(2,1)}, u32[]{:S(2)}, u32[]{:S(2)}) collective-permute-start(bf16[1280,256]{1,0:T(8,128)(2,1)} %collective-permute-done.8.rest_0_), channel_id=1, source_target_pairs={{0,32},{32,64},{64,96},{96,128},{128,160},{160,192},{192,224},{224... | collective-permute-start | bytes 1966088 | tf_op jit(solution)/shard_map/ppermute | solution.py:115
  89.1 45.2 %collective-permute-start.10 = (bf16[1280,256]{1,0:T(8,128)(2,1)}, bf16[1280,256]{1,0:T(8,128)(2,1)}, u32[]{:S(2)}, u32[]{:S(2)}) collective-permute-start(bf16[1280,256]{1,0:T(8,128)(2,1)} %collective-permute-done.8.rest_0_), channel_id=1, source_target_pairs={{0,16},{16,0},{1,17},{17,1},{2,18},{18,2},{3,19},{19,3},{4,20},{20... | collective-permute-start | bytes 1966088 | tf_op jit(solution)/shard_map/ppermute | solution.py:26
  91.0 38.9 %collective-permute-start.13 = (bf16[1280,256]{1,0:T(8,128)(2,1)}, bf16[1280,256]{1,0:T(8,128)(2,1)}, u32[]{:S(2)}, u32[]{:S(2)}) collective-permute-start(bf16[1280,256]{1,0:T(8,128)(2,1)} %collective-permute-done.12.rest_4_), channel_id=1, source_target_pairs={{0,480},{32,0},{64,32},{96,64},{128,96},{160,128},{192,160},{224,1... | collective-permute-start | bytes 1966088 | tf_op jit(solution)/shard_map/ppermute | solution.py:115
  95.6 36.3 %collective-permute-start.17 = (bf16[1280,256]{1,0:T(8,128)(2,1)}, bf16[1280,256]{1,0:T(8,128)(2,1)}, u32[]{:S(2)}, u32[]{:S(2)}) collective-permute-start(bf16[1280,256]{1,0:T(8,128)(2,1)} %collective-permute-done.16.rest_8_), channel_id=1, source_target_pairs={{0,32},{32,64},{64,96},{96,128},{128,160},{160,192},{192,224},{224... | collective-permute-start | bytes 1966088 | tf_op jit(solution)/shard_map/ppermute | solution.py:115
  105.5 0.9 copy-start.4
  117.7 21.0 %copy-start.12 = (f32[1280]{0:T(1024)S(1)}, f32[1280]{0:T(1024)}, u32[]{:S(2)}) copy-start(f32[1280]{0:T(1024)} %param.13) | copy-start | bytes 15364
  117.7 31.3 %all-to-all-start.2 = ((bf16[16,80,512]{2,1,0:T(8,128)(2,1)}), bf16[16,80,512]{2,1,0:T(8,128)(2,1)S(1)}, u32[]{:S(2)}, u32[]{:S(2)}) async-start(bf16[16,80,512]{2,1,0:T(8,128)(2,1)} %bitcast.36), calls=%async_computation.2 | async-start | bytes 2621440 | tf_op jit(solution)/shard_map/all_to_all | solution.py:315
  126.4 31.7 %collective-permute-start.14 = (bf16[1280,256]{1,0:T(8,128)(2,1)}, bf16[1280,256]{1,0:T(8,128)(2,1)}, u32[]{:S(2)}, u32[]{:S(2)}) collective-permute-start(bf16[1280,256]{1,0:T(8,128)(2,1)} %collective-permute-done.12.rest_4_), channel_id=1, source_target_pairs={{0,16},{16,0},{1,17},{17,1},{2,18},{18,2},{3,19},{19,3},{4,20},{20... | collective-permute-start | bytes 1966088 | tf_op jit(solution)/shard_map/ppermute | solution.py:26
  129.9 28.1 %collective-permute-start.18 = (bf16[1280,256]{1,0:T(8,128)(2,1)}, bf16[1280,256]{1,0:T(8,128)(2,1)}, u32[]{:S(2)}, u32[]{:S(2)}) collective-permute-start(bf16[1280,256]{1,0:T(8,128)(2,1)} %collective-permute-done.16.rest_8_), channel_id=1, source_target_pairs={{0,16},{16,0},{1,17},{17,1},{2,18},{18,2},{3,19},{19,3},{4,20},{20... | collective-permute-start | bytes 1966088 | tf_op jit(solution)/shard_map/ppermute | solution.py:26
  131.9 26.2 %collective-permute-start.11 = (bf16[1280,256]{1,0:T(8,128)(2,1)}, bf16[1280,256]{1,0:T(8,128)(2,1)}, u32[]{:S(2)}, u32[]{:S(2)}) collective-permute-start(bf16[1280,256]{1,0:T(8,128)(2,1)} %collective-permute-done.9.rest_1_), channel_id=1, source_target_pairs={{0,16},{16,0},{1,17},{17,1},{2,18},{18,2},{3,19},{19,3},{4,20},{20... | collective-permute-start | bytes 1966088 | tf_op jit(solution)/shard_map/ppermute | solution.py:26
  134.3 23.8 %collective-permute-start.15 = (bf16[1280,256]{1,0:T(8,128)(2,1)}, bf16[1280,256]{1,0:T(8,128)(2,1)}, u32[]{:S(2)}, u32[]{:S(2)}) collective-permute-start(bf16[1280,256]{1,0:T(8,128)(2,1)} %collective-permute-done.13.rest_5_), channel_id=1, source_target_pairs={{0,16},{16,0},{1,17},{17,1},{2,18},{18,2},{3,19},{19,3},{4,20},{20... | collective-permute-start | bytes 1966088 | tf_op jit(solution)/shard_map/ppermute | solution.py:26
  136.2 21.8 %collective-permute-start.19 = (bf16[1280,256]{1,0:T(8,128)(2,1)}, bf16[1280,256]{1,0:T(8,128)(2,1)S(1)}, u32[]{:S(2)}, u32[]{:S(2)}) collective-permute-start(bf16[1280,256]{1,0:T(8,128)(2,1)} %collective-permute-done.17.rest_9_), channel_id=1, source_target_pairs={{0,16},{16,0},{1,17},{17,1},{2,18},{18,2},{3,19},{19,3},{4,20},{20... | collective-permute-start | bytes 1966088 | tf_op jit(solution)/shard_map/ppermute | solution.py:26
  149.1 1.0 copy-start.3
  158.1 0.9 copy-start.8
where the time goes:
time: 181 us; the launch traced here: 180 us
  starting transfers between devices  76.8 us (42%)
  Pallas kernels  37 us (20%)
  waiting for transfers between devices  35.7 us (20%)
  local copies, waits for them, and re-layouts  11.7 us (6%)
  blocking collectives  11.7 us (6%)
  other arithmetic  6.41 us (4%)
    ppermute x6, starting transfers between devices, shift_rows(): lax.ppermute(value, 'y', [(at, (at + step) % rows) for at in range(rows)])  21.8 us
    ppermute x8, starting transfers between devices, swap_cores(): return lax.ppermute(value, 'c', [(0, 1), (1, 0)])  18 us
    all_to_all x1, blocking collectives, block_step(): lax.all_to_all(block.reshape(cols, groups, block.shape[1]), 'x', split_ax...  11.7 us
    ppermute x3, waiting for transfers between devices, shift_cols(): lax.ppermute(value, 'x', [(at, (at + step) % cols) for at in range(cols)])  11.6 us
    ppermute x3, starting transfers between devices, shift_cols(): lax.ppermute(value, 'x', [(at, (at + step) % cols) for at in range(cols)])  11.4 us
    pallas_call x1, Pallas kernels, attention(): pl.pallas_call(attention_kernel, out_shape=jax.ShapeDtypeStruct((tiles, c...  11.2 us
    ppermute x6, waiting for transfers between devices, shift_rows(): lax.ppermute(value, 'y', [(at, (at + step) % rows) for at in range(rows)])  9.04 us
    ppermute x3, starting transfers between devices, shift_planes(): lax.ppermute(value, 'z', [(at, (at + step) % planes) for at in range(plan...  8.76 us
  transfers between devices with their start and end apart: 23, of which 7 were waited for; matrix products, arithmetic and copies ran while one was open for 7% of the time, Pallas kernels for 16%

commit v1 on v0

--- a/solution.py
+++ b/solution.py
@@ -78,16 +78,21 @@
         out[0, copy] = result
 
 
-def attention(qkv, segments, segment_ids, copies):
-    tiles, _, chunk = qkv.shape
-    count = tiles * chunk
-    edges = segment_ids.reshape(count // TK, TK)
+def attention_inputs(segments, segment_ids):
+    edges = segment_ids.reshape(-1, TK)
     key_low, key_high = edges[:, 0], edges[:, -1]
-    query_edges = segment_ids.reshape(count // TQ, TQ)
+    query_edges = segment_ids.reshape(-1, TQ)
     query_low, query_high = query_edges[:, 0], query_edges[:, -1]
     first = jnp.sum(key_high[None, :] < query_low[:, None], axis=1)
     last = jnp.sum(key_low[None, :] <= query_high[:, None], axis=1)
     bounds = jnp.stack([first, last]).astype(jnp.int32)
+    return bounds, segments[:, None], segments[None, :]
+
+
+def attention(qkv, layout, copies):
+    tiles, _, chunk = qkv.shape
+    count = tiles * chunk
+    bounds, seg_col, seg_row = layout
     per = chunk // TQ
     return pl.pallas_call(
         attention_kernel,
@@ -104,7 +109,7 @@
             scratch_shapes=[pltpu.VMEM((count, HEAD_DIM), jnp.bfloat16), pltpu.VMEM((count, 128), jnp.int32)],
         ),
         name="attention",
-    )(bounds, qkv, segments[:, None], segments[None, :])
+    )(bounds, qkv, seg_col, seg_row)
 
 
 def shift_cols(value, step, cols):
@@ -172,17 +177,17 @@
         grid_spec=pltpu.PrefetchScalarGridSpec(
             num_scalar_prefetch=1,
             grid=(cols // 2,),
-            in_specs=[pl.BlockSpec((2, count, D), lambda i, p: (i, 0, 0)), whole((1, D)), whole(weights.shape)]
+            in_specs=[pl.BlockSpec((2, count, D), lambda i, p: (i, 0, 0)), whole((D,)), whole(weights.shape)]
             + [whole(part.shape) for part in parts] + [whole(other.shape)],
             out_specs=pl.BlockSpec((rows, wide, 2 * count), lambda i, p: (0, 0, i)),
             scratch_shapes=[pltpu.VMEM((2 * count, D), jnp.bfloat16)],
         ),
         name="project_qkv",
-    )(place, row_tokens, gain[None], weights, *parts, other)
+    )(place, row_tokens, gain, weights, *parts, other)
 
 
 def hidden_kernel(place, back, residual, mine, other, gain, out, left, hidden):
-    row, col, core = place[0], place[1], place[2]
+    row, core, col = place[0], place[1], place[2]
     cols, rows = mine.shape[0], mine.shape[1]
     half = D // 2
     count = hidden.shape[0]
@@ -213,17 +218,19 @@
             in_specs=[
                 pl.BlockSpec((HEADS, HEAD_DIM, count), lambda i, p: (0, 0, i)),
                 pl.BlockSpec((1, count, D), lambda i, p: (i, 0, 0)),
-                whole(mine.shape), whole(other.shape), whole((1, D)),
+                whole(mine.shape), whole(other.shape), whole((D,)),
             ],
             out_specs=pl.BlockSpec((4, 1, count // 4, D), lambda i, p: (0, i, 0, 0)),
             scratch_shapes=[pltpu.VMEM((D, count), jnp.bfloat16), pltpu.VMEM((count, D), jnp.float32)],
         ),
         name="merge_rows",
-    )(place, back, row_tokens, mine, other, gain[None])
-
-
-def merge_kernel(order, rows, own, *rest):
+    )(place, back, row_tokens, mine, other, gain)
+
+
+def merge_kernel(place, rows, own, *rest):
     parts, out = rest[:-1], rest[-1]
+    core, parity = place[1], place[3]
+    order = (parity * 2 + core, 2 - parity * 2 + core, parity * 2 + 1 - core, 3 - parity * 2 - core)
     width = own.shape[1]
     total = matmul(rows[0], own[0:D, :], 1, 0)
     for spot in range(1, 4):
@@ -236,7 +243,7 @@
         out[:, (block + 1) * width:(block + 2) * width] = total.astype(jnp.bfloat16)
 
 
-def merge(order, rows, own, parts):
+def merge(place, rows, own, parts):
     width = own.shape[1] * (1 + len(parts) // 4)
     return pl.pallas_call(
         merge_kernel,
@@ -248,7 +255,7 @@
             out_specs=whole((rows.shape[1], width)),
         ),
         name="merge",
-    )(order, rows, own, *parts)
+    )(place, rows, own, *parts)
 
 
 BACK_BY = (0, 1, 3, 2)
@@ -285,9 +292,11 @@
     row_count = cols * tok_local
     half = D // 2
     wide = w_qkv.shape[1]
+    place = jnp.stack([row, core, col, parity]).astype(jnp.int32)
+    segments = segment_ids.reshape(rows * cols, groups, 4).transpose(0, 2, 1).reshape(-1)
+    layout = attention_inputs(segments, segment_ids)
     row_tokens = lax.all_to_all(
         spread_tokens(tokens, cols), "x", split_axis=0, concat_axis=0, tiled=True)
-    segments = segment_ids.reshape(rows * cols, groups, 4).transpose(0, 2, 1).reshape(-1)
 
     weights = w_qkv.T
     own = jnp.concatenate([
@@ -296,22 +305,22 @@
     ahead = [shift_rows(own, step, rows) for step in (3, 2, 1)]
     other_qkv = swap_cores(jnp.stack([part[:wide] for part in ahead]))
 
-    order = [parity * 2 + core, (1 - parity) * 2 + core, parity * 2 + 1 - core, (1 - parity) * 2 + 1 - core]
-    own_piece = lax.dynamic_slice_in_dim(w_merge, order[0] * D, D, 0)
+    own_piece = lax.dynamic_slice_in_dim(w_merge, (parity * 2 + core) * D, D, 0)
     first_y = shift_rows(own_piece, 1, rows)
     third_y = shift_rows(own_piece, 3, rows)
 
     qkv = project_qkv(
-        jnp.stack([row, core]).astype(jnp.int32), row_tokens, gain_attn, weights, ahead, other_qkv, rows)
+        place, row_tokens, gain_attn, weights, ahead, other_qkv, rows)
     by_head = lax.all_to_all(qkv, "y", split_axis=0, concat_axis=0, tiled=True)
 
     out_rows = jnp.stack([own[wide:]] + [part[wide:] for part in ahead])
-    out_parts = [out_rows] + [shift_cols(out_rows, step, cols) for step in (1, 2, 3)]
+    next_out = shift_cols(out_rows, 1, cols)
+    out_parts = [out_rows, next_out] + [shift_cols(out_rows, step, cols) for step in (2, 3)]
     first_z = shift_planes(first_y, 1, planes)
     third_z = shift_planes(third_y, planes - 1, planes)
     second_y = shift_rows(own_piece, 2, rows)
 
-    attended = attention(by_head, segments, segment_ids, cols)
+    attended = attention(by_head, layout, cols)
     back = lax.all_to_all(
         attended.reshape(rows * cols, HEAD_DIM, row_count), ("y", "x"),
         split_axis=0, concat_axis=0, tiled=True)
@@ -324,12 +333,12 @@
     parts += [second_y, second_z, swap_cores(second_y), swap_cores(second_z)]
 
     merged = merge_rows(
-        jnp.stack([row, col, core]).astype(jnp.int32), back, row_tokens, mine_out, other_out, gain_merge)
+        place, back, row_tokens, mine_out, other_out, gain_merge)
     block = merge(
-        jnp.stack(order).astype(jnp.int32), merged.reshape(4, cols * groups, D), w_merge, parts)
+        place, merged.reshape(4, cols * groups, D), w_merge, parts)
     got = lax.all_to_all(
         block.reshape(cols, groups, block.shape[1]), "x", split_axis=0, concat_axis=0, tiled=True)
-    return place_columns(row[None].astype(jnp.int32), got)
+    return place_columns(place, got)
 
 
 def solution(mesh):

time: 181 us -> 181 us (level)
  waiting for transfers between devices: 35.7 us -> 38.1 us
    all_to_all x1, waiting for transfers between devices: 8.53 us -> 10.4 us  [block_step(): lax.all_to_all(attended.reshape(rows * cols, HEAD_DIM, row_count), ('y',...]
    unnamed x26 -> x22, local copies, waits for them, and re-layouts: 3.91 us -> 3.95 us
  transfers between devices with their start and end apart: 23 -> 23, of which waited for: 7 -> 7; matrix products, arithmetic and copies ran while one was open for 7% -> 6% of each run, Pallas kernels for 16% -> 15%
where the time goes in v1:
time: 181 us; the launch traced here: 180 us
  starting transfers between devices  76.7 us (42%)
  waiting for transfers between devices  38.1 us (21%)
  Pallas kernels  37.5 us (21%)
  blocking collectives  11.7 us (6%)
  local copies, waits for them, and re-layouts  10.5 us (6%)
  other arithmetic  5.16 us (3%)
    ppermute x6, starting transfers between devices, shift_rows(): lax.ppermute(value, 'y', [(at, (at + step) % rows) for at in range(rows)])  21.7 us
    ppermute x8, starting transfers between devices, swap_cores(): return lax.ppermute(value, 'c', [(0, 1), (1, 0)])  18 us
    all_to_all x1, blocking collectives, block_step(): lax.all_to_all(block.reshape(cols, groups, block.shape[1]), 'x', split_ax...  11.7 us
    ppermute x3, waiting for transfers between devices, shift_cols(): lax.ppermute(value, 'x', [(at, (at + step) % cols) for at in range(cols)])  11.6 us
    ppermute x3, starting transfers between devices, shift_cols(): lax.ppermute(value, 'x', [(at, (at + step) % cols) for at in range(cols)])  11.4 us
    pallas_call x1, Pallas kernels, attention(): pl.pallas_call(attention_kernel, out_shape=jax.ShapeDtypeStruct((tiles, c...  11.2 us
    all_to_all x1, waiting for transfers between devices, block_step(): lax.all_to_all(attended.reshape(rows * cols, HEAD_DIM, row_count), ('y',...  10.4 us
    ppermute x6, waiting for transfers between devices, shift_rows(): lax.ppermute(value, 'y', [(at, (at + step) % rows) for at in range(rows)])  9.61 us
  transfers between devices with their start and end apart: 23, of which 7 were waited for; matrix products, arithmetic and copies ran while one was open for 6% of the time, Pallas kernels for 15%

profile of v1, /device:TPU:320, one launch (start us, length us, event | category | flops | bytes accessed | tf_op | source)
XLA Modules:
  0.0 180.1 jit_solution(6448052975136507742)
XLA Ops:
  0.0 1.0 dynamic-slice_bitcast_fusion
  1.1 3.5 %collective-permute-start.2 = (bf16[320,640]{1,0:T(8,128)(2,1)S(1)}, bf16[320,640]{1,0:T(8,128)(2,1)S(1)}, u32[]{:S(2)}, u32[]{:S(2)}) collective-permute-start(bf16[320,640]{1,0:T(8,128)(2,1)S(1)} %pad_maximum_fusion.2), channel_id=1, source_target_pairs={{0,4},{4,8},{8,12},{12,0},{1,5},{5,9},{9,13},{13,1},{2,6},{6,10},{... | collective-permute-start | bytes 1228808 | tf_op jit(solution)/shard_map/ppermute | solution.py:30
  4.6 4.8 %collective-permute-start.1 = (bf16[320,640]{1,0:T(8,128)(2,1)S(1)}, bf16[320,640]{1,0:T(8,128)(2,1)S(1)}, u32[]{:S(2)}, u32[]{:S(2)}) collective-permute-start(bf16[320,640]{1,0:T(8,128)(2,1)S(1)} %pad_maximum_fusion.2), channel_id=1, source_target_pairs={{0,8},{4,12},{8,0},{12,4},{1,9},{5,13},{9,1},{13,5},{2,10},{6,14},... | collective-permute-start | bytes 1228808 | tf_op jit(solution)/shard_map/ppermute | solution.py:30
  9.4 3.3 %collective-permute-start = (bf16[320,640]{1,0:T(8,128)(2,1)S(1)}, bf16[320,640]{1,0:T(8,128)(2,1)S(1)}, u32[]{:S(2)}, u32[]{:S(2)}) collective-permute-start(bf16[320,640]{1,0:T(8,128)(2,1)S(1)} %pad_maximum_fusion.2), channel_id=1, source_target_pairs={{0,12},{4,0},{8,4},{12,8},{1,13},{5,1},{9,5},{13,9},{2,14},{6,2},{... | collective-permute-start | bytes 1228808 | tf_op jit(solution)/shard_map/ppermute | solution.py:30
  12.7 2.3 %spread.1 = bf16[4,128,1280]{2,1,0:T(8,128)(2,1)} custom-call(bf16[128,1280]{1,0:T(8,128)(2,1)} %tokens.1), custom_call_target="tpu_custom_call" | custom-call | tf_op jit(solution)/shard_map/spread/pallas_call | solution.py:145
  15.0 4.3 %all-to-all-start = ((bf16[4,128,1280]{2,1,0:T(8,128)(2,1)}), bf16[4,128,1280]{2,1,0:T(8,128)(2,1)S(1)}, u32[]{:S(2)}, u32[]{:S(2)}) async-start(bf16[4,128,1280]{2,1,0:T(8,128)(2,1)} %spread.1), calls=%async_computation | async-start | bytes 2621440 | tf_op jit(solution)/shard_map/all_to_all | solution.py:298
  19.4 6.1 %collective-permute-done.1.second = bf16[320,640]{1,0:T(8,128)(2,1)S(1)} collective-permute-done((bf16[320,640]{1,0:T(8,128)(2,1)S(1)}, bf16[320,640]{1,0:T(8,128)(2,1)S(1)}, u32[]{:S(2)}, u32[]{:S(2)}) %collective-permute-start.1) | collective-permute-done | bytes 409632 | tf_op jit(solution)/shard_map/ppermute | solution.py:30
  25.5 1.4 collective-permute-done.first
  26.8 1.0 fusion
  27.9 3.4 %collective-permute-start.4 = (bf16[4,80,640]{2,1,0:T(8,128)(2,1)}, bf16[4,80,640]{2,1,0:T(8,128)(2,1)S(1)}, u32[]{:S(2)}, u32[]{:S(2)}) collective-permute-start(bf16[4,80,640]{2,1,0:T(8,128)(2,1)} %get-tuple-element.10), channel_id=1, source_target_pairs={{0,1},{1,2},{2,3},{3,0},{4,5},{5,6},{6,7},{7,4},{8,9},{9,10},{10,1... | collective-permute-start | bytes 1228808 | tf_op jit(solution)/shard_map/ppermute | solution.py:116
  31.3 4.6 %collective-permute-start.5 = (bf16[4,80,640]{2,1,0:T(8,128)(2,1)}, bf16[4,80,640]{2,1,0:T(8,128)(2,1)}, u32[]{:S(2)}, u32[]{:S(2)}) collective-permute-start(bf16[4,80,640]{2,1,0:T(8,128)(2,1)} %get-tuple-element.10), channel_id=1, source_target_pairs={{0,2},{1,3},{2,0},{3,1},{4,6},{5,7},{6,4},{7,5},{8,10},{9,11},{10,... | collective-permute-start | bytes 1228808 | tf_op jit(solution)/shard_map/ppermute | solution.py:116
  35.9 3.3 %collective-permute-start.6 = (bf16[4,80,640]{2,1,0:T(8,128)(2,1)}, bf16[4,80,640]{2,1,0:T(8,128)(2,1)}, u32[]{:S(2)}, u32[]{:S(2)}) collective-permute-start(bf16[4,80,640]{2,1,0:T(8,128)(2,1)} %get-tuple-element.10), channel_id=1, source_target_pairs={{0,3},{1,0},{2,1},{3,2},{4,7},{5,4},{6,5},{7,6},{8,11},{9,8},{10,9... | collective-permute-start | bytes 1228808 | tf_op jit(solution)/shard_map/ppermute | solution.py:116
  39.4 1.1 pad_maximum_fusion.1
  40.5 1.9 %collective-permute-start.3 = (bf16[3,240,640]{2,1,0:T(8,128)(2,1)}, bf16[3,240,640]{2,1,0:T(8,128)(2,1)}, u32[]{:S(2)}, u32[]{:S(2)}) collective-permute-start(bf16[3,240,640]{2,1,0:T(8,128)(2,1)} %pad_maximum_fusion.1), channel_id=1, source_target_pairs={{0,16},{16,0},{1,17},{17,1},{2,18},{18,2},{3,19},{19,3},{4,20},{20... | collective-permute-start | bytes 2764808 | tf_op jit(solution)/shard_map/ppermute | solution.py:26
  42.4 5.0 %collective-permute-done.4 = bf16[4,80,640]{2,1,0:T(8,128)(2,1)S(1)} collective-permute-done((bf16[4,80,640]{2,1,0:T(8,128)(2,1)}, bf16[4,80,640]{2,1,0:T(8,128)(2,1)S(1)}, u32[]{:S(2)}, u32[]{:S(2)}) %collective-permute-start.4) | collective-permute-done | bytes 409632 | tf_op jit(solution)/shard_map/ppermute | solution.py:116
  47.4 6.6 %collective-permute-done.5 = bf16[4,80,640]{2,1,0:T(8,128)(2,1)} collective-permute-done((bf16[4,80,640]{2,1,0:T(8,128)(2,1)}, bf16[4,80,640]{2,1,0:T(8,128)(2,1)}, u32[]{:S(2)}, u32[]{:S(2)}) %collective-permute-start.5) | collective-permute-done | bytes 409632 | tf_op jit(solution)/shard_map/ppermute | solution.py:116
  54.0 0.0 collective-permute-done.6
  54.0 1.6 pad_maximum_fusion.mine
  55.7 1.9 %collective-permute-start.7 = (bf16[4,4,80,640]{3,2,1,0:T(8,128)(2,1)S(1)}, bf16[4,4,80,640]{3,2,1,0:T(8,128)(2,1)}, u32[]{:S(2)}, u32[]{:S(2)}) collective-permute-start(bf16[4,4,80,640]{3,2,1,0:T(8,128)(2,1)S(1)} %pad_maximum_fusion.mine), channel_id=1, source_target_pairs={{0,16},{16,0},{1,17},{17,1},{2,18},{18,2},{3,19},{19,3},{4,20},{20... | collective-permute-start | bytes 4915208 | tf_op jit(solution)/shard_map/ppermute | solution.py:26
  57.6 2.0 %constant_dynamic-slice_fusion = bf16[1280,256]{1,0:T(8,128)(2,1)} fusion(bf16[5120,256]{1,0:T(8,128)(2,1)} %own.1, s32[]{:T(128)S(6)} %select_n.16), kind=kLoop, calls=%fused_computation.16 | loop fusion | bytes 1310724 | tf_op jit(solution)/shard_map/dynamic_slice | solution.py:308
  59.6 4.3 %collective-permute-start.8 = (bf16[1280,256]{1,0:T(8,128)(2,1)}, bf16[1280,256]{1,0:T(8,128)(2,1)}, u32[]{:S(2)}, u32[]{:S(2)}) collective-permute-start(bf16[1280,256]{1,0:T(8,128)(2,1)} %constant_dynamic-slice_fusion), channel_id=1, source_target_pairs={{0,4},{4,8},{8,12},{12,0},{1,5},{5,9},{9,13},{13,1},{2,6},{6,10},{... | collective-permute-start | bytes 1966088 | tf_op jit(solution)/shard_map/ppermute | solution.py:30
  63.9 2.7 %collective-permute-start.12 = (bf16[1280,256]{1,0:T(8,128)(2,1)}, bf16[1280,256]{1,0:T(8,128)(2,1)}, u32[]{:S(2)}, u32[]{:S(2)}) collective-permute-start(bf16[1280,256]{1,0:T(8,128)(2,1)} %constant_dynamic-slice_fusion), channel_id=1, source_target_pairs={{0,12},{4,0},{8,4},{12,8},{1,13},{5,1},{9,5},{13,9},{2,14},{6,2},{... | collective-permute-start | bytes 1966088 | tf_op jit(solution)/shard_map/ppermute | solution.py:30
  66.6 3.2 %collective-permute-start.16 = (bf16[1280,256]{1,0:T(8,128)(2,1)}, bf16[1280,256]{1,0:T(8,128)(2,1)}, u32[]{:S(2)}, u32[]{:S(2)}) collective-permute-start(bf16[1280,256]{1,0:T(8,128)(2,1)} %constant_dynamic-slice_fusion), channel_id=1, source_target_pairs={{0,8},{4,12},{8,0},{12,4},{1,9},{5,13},{9,1},{13,5},{2,10},{6,14},... | collective-permute-start | bytes 1966088 | tf_op jit(solution)/shard_map/ppermute | solution.py:30
  69.8 0.6 pad_add_fusion.1.place
  70.4 0.0 collective-permute-done.3.other
  70.4 1.1 copy-done.1
  71.5 6.4 %project_qkv.1 = bf16[4,240,512]{2,1,0:T(8,128)(2,1)} custom-call(s32[4]{0:T(128)} %pad_add_fusion.1.place, bf16[4,128,1280]{2,1,0:T(8,128)(2,1)} %copy-done.1, f32[1280]{0:T(1024)} %gain.2, bf16[240,1280]{1,0:T(8,128)(2,1)} %bitcast.34, bf16[320,640]{1,0:T(8,128)(2,1)} %copy-done.7, bf16[320,640]{1,0:T(8,128)(2,1)} %copy-done.6, ...), custom_call_target="tpu_custom_call" | custom-call | tf_op jit(solution)/shard_map/project_qkv/pallas_call | solution.py:174
  77.8 4.0 %all-to-all-start.1 = ((bf16[4,240,512]{2,1,0:T(8,128)(2,1)}), bf16[4,240,512]{2,1,0:T(8,128)(2,1)S(1)}, u32[]{:S(2)}, u32[]{:S(2)}) async-start(bf16[4,240,512]{2,1,0:T(8,128)(2,1)} %project_qkv.1), calls=%async_computation.1 | async-start | bytes 1966080 | tf_op jit(solution)/shard_map/all_to_all | solution.py:314
  81.9 0.3 reshape.19
  82.1 0.2 copy.14
  82.3 2.1 %broadcast_in_dim_reshape.8.seg_col = s32[2048,1]{1,0:T(8,128)} reshape(s32[16,4,32]{2,1,0:T(4,128)S(1)} %copy.14) | data formatting | bytes 16384 | tf_op jit(solution)/shard_map/broadcast_in_dim;reshape | solution.py:89
  84.4 0.7 broadcast_in_dim_reshape.7.seg_row
  85.1 0.2 slice_reduce_fusion.1
  85.3 0.2 convert_reduce_fusion.1
  85.5 0.0 collective-permute-done.8.rest_0_
  85.5 2.9 %collective-permute-start.9 = (bf16[1280,256]{1,0:T(8,128)(2,1)}, bf16[1280,256]{1,0:T(8,128)(2,1)}, u32[]{:S(2)}, u32[]{:S(2)}) collective-permute-start(bf16[1280,256]{1,0:T(8,128)(2,1)} %collective-permute-done.8.rest_0_), channel_id=1, source_target_pairs={{0,32},{32,64},{64,96},{96,128},{128,160},{160,192},{192,224},{224... | collective-permute-start | bytes 1966088 | tf_op jit(solution)/shard_map/ppermute | solution.py:120
  88.4 1.9 %collective-permute-start.10 = (bf16[1280,256]{1,0:T(8,128)(2,1)}, bf16[1280,256]{1,0:T(8,128)(2,1)}, u32[]{:S(2)}, u32[]{:S(2)}) collective-permute-start(bf16[1280,256]{1,0:T(8,128)(2,1)} %collective-permute-done.8.rest_0_), channel_id=1, source_target_pairs={{0,16},{16,0},{1,17},{17,1},{2,18},{18,2},{3,19},{19,3},{4,20},{20... | collective-permute-start | bytes 1966088 | tf_op jit(solution)/shard_map/ppermute | solution.py:26
  90.4 0.0 collective-permute-done.12.rest_4_
  90.4 2.9 %collective-permute-start.13 = (bf16[1280,256]{1,0:T(8,128)(2,1)}, bf16[1280,256]{1,0:T(8,128)(2,1)}, u32[]{:S(2)}, u32[]{:S(2)}) collective-permute-start(bf16[1280,256]{1,0:T(8,128)(2,1)} %collective-permute-done.12.rest_4_), channel_id=1, source_target_pairs={{0,480},{32,0},{64,32},{96,64},{128,96},{160,128},{192,160},{224,1... | collective-permute-start | bytes 1966088 | tf_op jit(solution)/shard_map/ppermute | solution.py:120
  93.3 2.2 %collective-permute-done.16.rest_8_ = bf16[1280,256]{1,0:T(8,128)(2,1)} collective-permute-done((bf16[1280,256]{1,0:T(8,128)(2,1)}, bf16[1280,256]{1,0:T(8,128)(2,1)}, u32[]{:S(2)}, u32[]{:S(2)}) %collective-permute-start.16) | collective-permute-done | bytes 655392 | tf_op jit(solution)/shard_map/ppermute | solution.py:30
  95.5 2.9 %collective-permute-start.17 = (bf16[1280,256]{1,0:T(8,128)(2,1)}, bf16[1280,256]{1,0:T(8,128)(2,1)}, u32[]{:S(2)}, u32[]{:S(2)}) collective-permute-start(bf16[1280,256]{1,0:T(8,128)(2,1)} %collective-permute-done.16.rest_8_), channel_id=1, source_target_pairs={{0,32},{32,64},{64,96},{96,128},{128,160},{160,192},{192,224},{224... | collective-permute-start | bytes 1966088 | tf_op jit(solution)/shard_map/ppermute | solution.py:120
  98.4 0.6 pad_add_fusion.bounds
  99.0 6.4 %all-to-all-done.1.qkv = bf16[4,240,512]{2,1,0:T(8,128)(2,1)S(1)} async-done(((bf16[4,240,512]{2,1,0:T(8,128)(2,1)}), bf16[4,240,512]{2,1,0:T(8,128)(2,1)S(1)}, u32[]{:S(2)}, u32[]{:S(2)}) %all-to-all-start.1) | async-done | bytes 983072 | tf_op jit(solution)/shard_map/all_to_all | solution.py:314
  105.4 1.0 copy-done.4
  106.4 11.2 %attention.1 = bf16[4,4,80,512]{3,2,1,0:T(8,128)(2,1)} custom-call(s32[2,4]{1,0:T(2,128)} %pad_add_fusion.bounds, bf16[4,240,512]{2,1,0:T(8,128)(2,1)} %copy-done.4, s32[2048,1]{1,0:T(8,128)} %broadcast_in_dim_reshape.8.seg_col, s32[1,2048]{1,0:T(1,128)} %broadcast_in_dim_reshape.7.seg_row), custom_call_target="tpu_custom_call" | custom-call | tf_op jit(solution)/shard_map/attention/pallas_call | solution.py:97
  117.6 8.6 %all-to-all-start.2 = ((bf16[16,80,512]{2,1,0:T(8,128)(2,1)}), bf16[16,80,512]{2,1,0:T(8,128)(2,1)S(1)}, u32[]{:S(2)}, u32[]{:S(2)}) async-start(bf16[16,80,512]{2,1,0:T(8,128)(2,1)} %bitcast.32), calls=%async_computation.2 | async-start | bytes 2621440 | tf_op jit(solution)/shard_map/all_to_all | solution.py:324
  126.2 0.0 collective-permute-done.9.rest_1_
  126.2 3.5 %collective-permute-start.14 = (bf16[1280,256]{1,0:T(8,128)(2,1)}, bf16[1280,256]{1,0:T(8,128)(2,1)}, u32[]{:S(2)}, u32[]{:S(2)}) collective-permute-start(bf16[1280,256]{1,0:T(8,128)(2,1)} %collective-permute-done.12.rest_4_), channel_id=1, source_target_pairs={{0,16},{16,0},{1,17},{17,1},{2,18},{18,2},{3,19},{19,3},{4,20},{20... | collective-permute-start | bytes 1966088 | tf_op jit(solution)/shard_map/ppermute | solution.py:26
  129.7 0.0 collective-permute-done.13.rest_5_
  129.7 1.9 %collective-permute-start.18 = (bf16[1280,256]{1,0:T(8,128)(2,1)}, bf16[1280,256]{1,0:T(8,128)(2,1)}, u32[]{:S(2)}, u32[]{:S(2)}) collective-permute-start(bf16[1280,256]{1,0:T(8,128)(2,1)} %collective-permute-done.16.rest_8_), channel_id=1, source_target_pairs={{0,16},{16,0},{1,17},{17,1},{2,18},{18,2},{3,19},{19,3},{4,20},{20... | collective-permute-start | bytes 1966088 | tf_op jit(solution)/shard_map/ppermute | solution.py:26
  131.7 0.0 collective-permute-done.17.rest_9_
  131.7 2.4 %collective-permute-start.11 = (bf16[1280,256]{1,0:T(8,128)(2,1)}, bf16[1280,256]{1,0:T(8,128)(2,1)}, u32[]{:S(2)}, u32[]{:S(2)}) collective-permute-start(bf16[1280,256]{1,0:T(8,128)(2,1)} %collective-permute-done.9.rest_1_), channel_id=1, source_target_pairs={{0,16},{16,0},{1,17},{17,1},{2,18},{18,2},{3,19},{19,3},{4,20},{20... | collective-permute-start | bytes 1966088 | tf_op jit(solution)/shard_map/ppermute | solution.py:26
  134.1 0.0 collective-permute-done.10.rest_2_
  134.1 1.9 %collective-permute-start.15 = (bf16[1280,256]{1,0:T(8,128)(2,1)}, bf16[1280,256]{1,0:T(8,128)(2,1)}, u32[]{:S(2)}, u32[]{:S(2)}) collective-permute-start(bf16[1280,256]{1,0:T(8,128)(2,1)} %collective-permute-done.13.rest_5_), channel_id=1, source_target_pairs={{0,16},{16,0},{1,17},{17,1},{2,18},{18,2},{3,19},{19,3},{4,20},{20... | collective-permute-start | bytes 1966088 | tf_op jit(solution)/shard_map/ppermute | solution.py:26
  136.0 0.0 collective-permute-done.7.other
  136.0 2.4 %collective-permute-start.19 = (bf16[1280,256]{1,0:T(8,128)(2,1)}, bf16[1280,256]{1,0:T(8,128)(2,1)S(1)}, u32[]{:S(2)}, u32[]{:S(2)}) collective-permute-start(bf16[1280,256]{1,0:T(8,128)(2,1)} %collective-permute-done.17.rest_9_), channel_id=1, source_target_pairs={{0,16},{16,0},{1,17},{17,1},{2,18},{18,2},{3,19},{19,3},{4,20},{20... | collective-permute-start | bytes 1966088 | tf_op jit(solution)/shard_map/ppermute | solution.py:26
  138.4 10.4 %all-to-all-done.2.back = bf16[16,80,512]{2,1,0:T(8,128)(2,1)S(1)} async-done(((bf16[16,80,512]{2,1,0:T(8,128)(2,1)}), bf16[16,80,512]{2,1,0:T(8,128)(2,1)S(1)}, u32[]{:S(2)}, u32[]{:S(2)}) %all-to-all-start.2) | async-done | bytes 1310752 | tf_op jit(solution)/shard_map/all_to_all | solution.py:324
  148.8 1.1 copy-done.3
  149.9 7.9 %merge_rows.1 = bf16[4,4,32,1280]{3,2,1,0:T(8,128)(2,1)} custom-call(s32[4]{0:T(128)} %pad_add_fusion.1.place, bf16[16,80,512]{2,1,0:T(8,128)(2,1)} %copy-done.3, bf16[4,128,1280]{2,1,0:T(8,128)(2,1)} %copy-done.1, bf16[4,4,80,640]{3,2,1,0:T(8,128)(2,1)} %copy-done.2, bf16[4,4,80,640]{3,2,1,0:T(8,128)(2,1)} %collective-permute-done.7.other, f32[1280]{0:T(1024)} %gain.3), custom_call_target="tpu_custom_call" | custom-call | tf_op jit(solution)/shard_map/merge_rows/pallas_call | solution.py:212
  157.8 0.0 collective-permute-done.14.rest_6_
  157.9 0.8 copy-done.8
  158.7 7.3 %merge.1 = bf16[128,1024]{1,0:T(8,128)(2,1)} custom-call(s32[4]{0:T(128)} %pad_add_fusion.1.place, bf16[4,128,1280]{2,1,0:T(8,128)(2,1)} %bitcast.33, bf16[5120,256]{1,0:T(8,128)(2,1)} %own.1, bf16[1280,256]{1,0:T(8,128)(2,1)} %collective-permute-done.8.rest_0_, bf16[1280,256]{1,0:T(8,128)(2,1)} %collective-permute-done.9.rest_1_, ...), custom_call_target="tpu_custom_call" | custom-call | tf_op jit(solution)/shard_map/merge/pallas_call | solution.py:248
  166.0 11.7 %all_to_all.20.got = bf16[4,32,1024]{2,1,0:T(8,128)(2,1)} all-to-all(bf16[4,32,1024]{2,1,0:T(8,128)(2,1)} %bitcast.35), channel_id=1, replica_groups=mesh['z'=16,'c'=2,'y'=4,'x'=4] {'x'}, dimensions={0} | all-to-all | bytes 524288 | tf_op jit(solution)/shard_map/all_to_all | solution.py:339
  177.7 2.3 %place_columns.1 = bf16[32,4096]{1,0:T(8,128)(2,1)} custom-call(s32[4]{0:T(128)} %pad_add_fusion.1.place, bf16[4,32,1024]{2,1,0:T(8,128)(2,1)} %all_to_all.20.got), custom_call_target="tpu_custom_call" | custom-call | tf_op jit(solution)/shard_map/place_columns/pallas_call | solution.py:276
  (34 shorter events, 0.2 us)
Async XLA Ops:
  0.0 1.0 copy-start
  1.1 18.2 %collective-permute-start.2 = (bf16[320,640]{1,0:T(8,128)(2,1)S(1)}, bf16[320,640]{1,0:T(8,128)(2,1)S(1)}, u32[]{:S(2)}, u32[]{:S(2)}) collective-permute-start(bf16[320,640]{1,0:T(8,128)(2,1)S(1)} %pad_maximum_fusion.2), channel_id=1, source_target_pairs={{0,4},{4,8},{8,12},{12,0},{1,5},{5,9},{9,13},{13,1},{2,6},{6,10},{... | collective-permute-start | bytes 1228808 | tf_op jit(solution)/shard_map/ppermute | solution.py:30
  4.6 20.8 %collective-permute-start.1 = (bf16[320,640]{1,0:T(8,128)(2,1)S(1)}, bf16[320,640]{1,0:T(8,128)(2,1)S(1)}, u32[]{:S(2)}, u32[]{:S(2)}) collective-permute-start(bf16[320,640]{1,0:T(8,128)(2,1)S(1)} %pad_maximum_fusion.2), channel_id=1, source_target_pairs={{0,8},{4,12},{8,0},{12,4},{1,9},{5,13},{9,1},{13,5},{2,10},{6,14},... | collective-permute-start | bytes 1228808 | tf_op jit(solution)/shard_map/ppermute | solution.py:30
  9.4 17.4 %collective-permute-start = (bf16[320,640]{1,0:T(8,128)(2,1)S(1)}, bf16[320,640]{1,0:T(8,128)(2,1)S(1)}, u32[]{:S(2)}, u32[]{:S(2)}) collective-permute-start(bf16[320,640]{1,0:T(8,128)(2,1)S(1)} %pad_maximum_fusion.2), channel_id=1, source_target_pairs={{0,12},{4,0},{8,4},{12,8},{1,13},{5,1},{9,5},{13,9},{2,14},{6,2},{... | collective-permute-start | bytes 1228808 | tf_op jit(solution)/shard_map/ppermute | solution.py:30
  15.0 55.4 %all-to-all-start = ((bf16[4,128,1280]{2,1,0:T(8,128)(2,1)}), bf16[4,128,1280]{2,1,0:T(8,128)(2,1)S(1)}, u32[]{:S(2)}, u32[]{:S(2)}) async-start(bf16[4,128,1280]{2,1,0:T(8,128)(2,1)} %spread.1), calls=%async_computation | async-start | bytes 2621440 | tf_op jit(solution)/shard_map/all_to_all | solution.py:298
  19.3 20.0 %copy-start.5 = (bf16[320,640]{1,0:T(8,128)(2,1)}, bf16[320,640]{1,0:T(8,128)(2,1)S(1)}, u32[]{:S(2)}) copy-start(bf16[320,640]{1,0:T(8,128)(2,1)S(1)} %collective-permute-done.2.third) | copy-start | bytes 1228804
  25.4 13.9 %copy-start.6 = (bf16[320,640]{1,0:T(8,128)(2,1)}, bf16[320,640]{1,0:T(8,128)(2,1)S(1)}, u32[]{:S(2)}) copy-start(bf16[320,640]{1,0:T(8,128)(2,1)S(1)} %collective-permute-done.1.second) | copy-start | bytes 1228804
  26.8 12.6 %copy-start.7 = (bf16[320,640]{1,0:T(8,128)(2,1)}, bf16[320,640]{1,0:T(8,128)(2,1)S(1)}, u32[]{:S(2)}) copy-start(bf16[320,640]{1,0:T(8,128)(2,1)S(1)} %collective-permute-done.first) | copy-start | bytes 1228804
  27.9 19.6 %collective-permute-start.4 = (bf16[4,80,640]{2,1,0:T(8,128)(2,1)}, bf16[4,80,640]{2,1,0:T(8,128)(2,1)S(1)}, u32[]{:S(2)}, u32[]{:S(2)}) collective-permute-start(bf16[4,80,640]{2,1,0:T(8,128)(2,1)} %get-tuple-element.10), channel_id=1, source_target_pairs={{0,1},{1,2},{2,3},{3,0},{4,5},{5,6},{6,7},{7,4},{8,9},{9,10},{10,1... | collective-permute-start | bytes 1228808 | tf_op jit(solution)/shard_map/ppermute | solution.py:116
  31.3 22.8 %collective-permute-start.5 = (bf16[4,80,640]{2,1,0:T(8,128)(2,1)}, bf16[4,80,640]{2,1,0:T(8,128)(2,1)}, u32[]{:S(2)}, u32[]{:S(2)}) collective-permute-start(bf16[4,80,640]{2,1,0:T(8,128)(2,1)} %get-tuple-element.10), channel_id=1, source_target_pairs={{0,2},{1,3},{2,0},{3,1},{4,6},{5,7},{6,4},{7,5},{8,10},{9,11},{10,... | collective-permute-start | bytes 1228808 | tf_op jit(solution)/shard_map/ppermute | solution.py:116
  35.9 18.1 %collective-permute-start.6 = (bf16[4,80,640]{2,1,0:T(8,128)(2,1)}, bf16[4,80,640]{2,1,0:T(8,128)(2,1)}, u32[]{:S(2)}, u32[]{:S(2)}) collective-permute-start(bf16[4,80,640]{2,1,0:T(8,128)(2,1)} %get-tuple-element.10), channel_id=1, source_target_pairs={{0,3},{1,0},{2,1},{3,2},{4,7},{5,4},{6,5},{7,6},{8,11},{9,8},{10,9... | collective-permute-start | bytes 1228808 | tf_op jit(solution)/shard_map/ppermute | solution.py:116
  40.5 29.9 %collective-permute-start.3 = (bf16[3,240,640]{2,1,0:T(8,128)(2,1)}, bf16[3,240,640]{2,1,0:T(8,128)(2,1)}, u32[]{:S(2)}, u32[]{:S(2)}) collective-permute-start(bf16[3,240,640]{2,1,0:T(8,128)(2,1)} %pad_maximum_fusion.1), channel_id=1, source_target_pairs={{0,16},{16,0},{1,17},{17,1},{2,18},{18,2},{3,19},{19,3},{4,20},{20... | collective-permute-start | bytes 2764808 | tf_op jit(solution)/shard_map/ppermute | solution.py:26
  47.4 6.6 %copy-start.9 = (bf16[4,80,640]{2,1,0:T(8,128)(2,1)}, bf16[4,80,640]{2,1,0:T(8,128)(2,1)S(1)}, u32[]{:S(2)}) copy-start(bf16[4,80,640]{2,1,0:T(8,128)(2,1)S(1)} %collective-permute-done.4) | copy-start | bytes 1228804
  55.7 28.7 %copy-start.2 = (bf16[4,4,80,640]{3,2,1,0:T(8,128)(2,1)}, bf16[4,4,80,640]{3,2,1,0:T(8,128)(2,1)S(1)}, u32[]{:S(2)}) copy-start(bf16[4,4,80,640]{3,2,1,0:T(8,128)(2,1)S(1)} %pad_maximum_fusion.mine) | copy-start | bytes 4915204
  55.7 80.4 %collective-permute-start.7 = (bf16[4,4,80,640]{3,2,1,0:T(8,128)(2,1)S(1)}, bf16[4,4,80,640]{3,2,1,0:T(8,128)(2,1)}, u32[]{:S(2)}, u32[]{:S(2)}) collective-permute-start(bf16[4,4,80,640]{3,2,1,0:T(8,128)(2,1)S(1)} %pad_maximum_fusion.mine), channel_id=1, source_target_pairs={{0,16},{16,0},{1,17},{17,1},{2,18},{18,2},{3,19},{19,3},{4,20},{20... | collective-permute-start | bytes 4915208 | tf_op jit(solution)/shard_map/ppermute | solution.py:26
  59.6 25.9 %collective-permute-start.8 = (bf16[1280,256]{1,0:T(8,128)(2,1)}, bf16[1280,256]{1,0:T(8,128)(2,1)}, u32[]{:S(2)}, u32[]{:S(2)}) collective-permute-start(bf16[1280,256]{1,0:T(8,128)(2,1)} %constant_dynamic-slice_fusion), channel_id=1, source_target_pairs={{0,4},{4,8},{8,12},{12,0},{1,5},{5,9},{9,13},{13,1},{2,6},{6,10},{... | collective-permute-start | bytes 1966088 | tf_op jit(solution)/shard_map/ppermute | solution.py:30
  63.9 26.5 %collective-permute-start.12 = (bf16[1280,256]{1,0:T(8,128)(2,1)}, bf16[1280,256]{1,0:T(8,128)(2,1)}, u32[]{:S(2)}, u32[]{:S(2)}) collective-permute-start(bf16[1280,256]{1,0:T(8,128)(2,1)} %constant_dynamic-slice_fusion), channel_id=1, source_target_pairs={{0,12},{4,0},{8,4},{12,8},{1,13},{5,1},{9,5},{13,9},{2,14},{6,2},{... | collective-permute-start | bytes 1966088 | tf_op jit(solution)/shard_map/ppermute | solution.py:30
  66.6 28.8 %collective-permute-start.16 = (bf16[1280,256]{1,0:T(8,128)(2,1)}, bf16[1280,256]{1,0:T(8,128)(2,1)}, u32[]{:S(2)}, u32[]{:S(2)}) collective-permute-start(bf16[1280,256]{1,0:T(8,128)(2,1)} %constant_dynamic-slice_fusion), channel_id=1, source_target_pairs={{0,8},{4,12},{8,0},{12,4},{1,9},{5,13},{9,1},{13,5},{2,10},{6,14},... | collective-permute-start | bytes 1966088 | tf_op jit(solution)/shard_map/ppermute | solution.py:30
  70.4 1.1 copy-start.1
  77.8 4.0 %copy-start.10 = (s32[2048]{0:T(1024)S(1)}, s32[2048]{0:T(1024)}, u32[]{:S(2)}) copy-start(s32[2048]{0:T(1024)} %param.8) | copy-start | bytes 24580
  77.8 27.6 %all-to-all-start.1 = ((bf16[4,240,512]{2,1,0:T(8,128)(2,1)}), bf16[4,240,512]{2,1,0:T(8,128)(2,1)S(1)}, u32[]{:S(2)}, u32[]{:S(2)}) async-start(bf16[4,240,512]{2,1,0:T(8,128)(2,1)} %project_qkv.1), calls=%async_computation.1 | async-start | bytes 1966080 | tf_op jit(solution)/shard_map/all_to_all | solution.py:314
  85.5 40.7 %collective-permute-start.9 = (bf16[1280,256]{1,0:T(8,128)(2,1)}, bf16[1280,256]{1,0:T(8,128)(2,1)}, u32[]{:S(2)}, u32[]{:S(2)}) collective-permute-start(bf16[1280,256]{1,0:T(8,128)(2,1)} %collective-permute-done.8.rest_0_), channel_id=1, source_target_pairs={{0,32},{32,64},{64,96},{96,128},{128,160},{160,192},{192,224},{224... | collective-permute-start | bytes 1966088 | tf_op jit(solution)/shard_map/ppermute | solution.py:120
  88.4 45.7 %collective-permute-start.10 = (bf16[1280,256]{1,0:T(8,128)(2,1)}, bf16[1280,256]{1,0:T(8,128)(2,1)}, u32[]{:S(2)}, u32[]{:S(2)}) collective-permute-start(bf16[1280,256]{1,0:T(8,128)(2,1)} %collective-permute-done.8.rest_0_), channel_id=1, source_target_pairs={{0,16},{16,0},{1,17},{17,1},{2,18},{18,2},{3,19},{19,3},{4,20},{20... | collective-permute-start | bytes 1966088 | tf_op jit(solution)/shard_map/ppermute | solution.py:26
  90.4 39.4 %collective-permute-start.13 = (bf16[1280,256]{1,0:T(8,128)(2,1)}, bf16[1280,256]{1,0:T(8,128)(2,1)}, u32[]{:S(2)}, u32[]{:S(2)}) collective-permute-start(bf16[1280,256]{1,0:T(8,128)(2,1)} %collective-permute-done.12.rest_4_), channel_id=1, source_target_pairs={{0,480},{32,0},{64,32},{96,64},{128,96},{160,128},{192,160},{224,1... | collective-permute-start | bytes 1966088 | tf_op jit(solution)/shard_map/ppermute | solution.py:120
  95.5 36.2 %collective-permute-start.17 = (bf16[1280,256]{1,0:T(8,128)(2,1)}, bf16[1280,256]{1,0:T(8,128)(2,1)}, u32[]{:S(2)}, u32[]{:S(2)}) collective-permute-start(bf16[1280,256]{1,0:T(8,128)(2,1)} %collective-permute-done.16.rest_8_), channel_id=1, source_target_pairs={{0,32},{32,64},{64,96},{96,128},{128,160},{160,192},{192,224},{224... | collective-permute-start | bytes 1966088 | tf_op jit(solution)/shard_map/ppermute | solution.py:120
  105.4 1.0 copy-start.4
  117.6 31.2 %all-to-all-start.2 = ((bf16[16,80,512]{2,1,0:T(8,128)(2,1)}), bf16[16,80,512]{2,1,0:T(8,128)(2,1)S(1)}, u32[]{:S(2)}, u32[]{:S(2)}) async-start(bf16[16,80,512]{2,1,0:T(8,128)(2,1)} %bitcast.32), calls=%async_computation.2 | async-start | bytes 2621440 | tf_op jit(solution)/shard_map/all_to_all | solution.py:324
  126.2 31.6 %collective-permute-start.14 = (bf16[1280,256]{1,0:T(8,128)(2,1)}, bf16[1280,256]{1,0:T(8,128)(2,1)}, u32[]{:S(2)}, u32[]{:S(2)}) collective-permute-start(bf16[1280,256]{1,0:T(8,128)(2,1)} %collective-permute-done.12.rest_4_), channel_id=1, source_target_pairs={{0,16},{16,0},{1,17},{17,1},{2,18},{18,2},{3,19},{19,3},{4,20},{20... | collective-permute-start | bytes 1966088 | tf_op jit(solution)/shard_map/ppermute | solution.py:26
  129.7 28.1 %collective-permute-start.18 = (bf16[1280,256]{1,0:T(8,128)(2,1)}, bf16[1280,256]{1,0:T(8,128)(2,1)}, u32[]{:S(2)}, u32[]{:S(2)}) collective-permute-start(bf16[1280,256]{1,0:T(8,128)(2,1)} %collective-permute-done.16.rest_8_), channel_id=1, source_target_pairs={{0,16},{16,0},{1,17},{17,1},{2,18},{18,2},{3,19},{19,3},{4,20},{20... | collective-permute-start | bytes 1966088 | tf_op jit(solution)/shard_map/ppermute | solution.py:26
  131.7 26.1 %collective-permute-start.11 = (bf16[1280,256]{1,0:T(8,128)(2,1)}, bf16[1280,256]{1,0:T(8,128)(2,1)}, u32[]{:S(2)}, u32[]{:S(2)}) collective-permute-start(bf16[1280,256]{1,0:T(8,128)(2,1)} %collective-permute-done.9.rest_1_), channel_id=1, source_target_pairs={{0,16},{16,0},{1,17},{17,1},{2,18},{18,2},{3,19},{19,3},{4,20},{20... | collective-permute-start | bytes 1966088 | tf_op jit(solution)/shard_map/ppermute | solution.py:26
  134.1 23.7 %collective-permute-start.15 = (bf16[1280,256]{1,0:T(8,128)(2,1)}, bf16[1280,256]{1,0:T(8,128)(2,1)}, u32[]{:S(2)}, u32[]{:S(2)}) collective-permute-start(bf16[1280,256]{1,0:T(8,128)(2,1)} %collective-permute-done.13.rest_5_), channel_id=1, source_target_pairs={{0,16},{16,0},{1,17},{17,1},{2,18},{18,2},{3,19},{19,3},{4,20},{20... | collective-permute-start | bytes 1966088 | tf_op jit(solution)/shard_map/ppermute | solution.py:26
  136.0 21.8 %collective-permute-start.19 = (bf16[1280,256]{1,0:T(8,128)(2,1)}, bf16[1280,256]{1,0:T(8,128)(2,1)S(1)}, u32[]{:S(2)}, u32[]{:S(2)}) collective-permute-start(bf16[1280,256]{1,0:T(8,128)(2,1)} %collective-permute-done.17.rest_9_), channel_id=1, source_target_pairs={{0,16},{16,0},{1,17},{17,1},{2,18},{18,2},{3,19},{19,3},{4,20},{20... | collective-permute-start | bytes 1966088 | tf_op jit(solution)/shard_map/ppermute | solution.py:26
  148.8 1.1 copy-start.3
  157.8 0.8 copy-start.8

commit v2 on v1

--- a/solution.py
+++ b/solution.py
@@ -227,58 +227,60 @@
     )(place, back, row_tokens, mine, other, gain)
 
 
-def merge_kernel(place, rows, own, *rest):
+def merge_kernel(place, mine, other, own, *rest):
     parts, out = rest[:-1], rest[-1]
     core, parity = place[1], place[3]
-    order = (parity * 2 + core, 2 - parity * 2 + core, parity * 2 + 1 - core, 3 - parity * 2 - core)
-    width = own.shape[1]
-    total = matmul(rows[0], own[0:D, :], 1, 0)
-    for spot in range(1, 4):
-        total = total + matmul(rows[spot], own[spot * D:(spot + 1) * D, :], 1, 0)
-    out[:, 0:width] = total.astype(jnp.bfloat16)
-    for block in range(len(parts) // 4):
-        total = matmul(rows[order[0]], parts[4 * block][...], 1, 0)
-        for index in range(1, 4):
-            total = total + matmul(rows[order[index]], parts[4 * block + index][...], 1, 0)
-        out[:, (block + 1) * width:(block + 2) * width] = total.astype(jnp.bfloat16)
-
-
-def merge(place, rows, own, parts):
-    width = own.shape[1] * (1 + len(parts) // 4)
+    lanes = parts[0].shape[1]
+    column = pl.multiple_of(core * lanes, lanes)
+    for source, target in ((mine, core), (other, 1 - core)):
+        near = jnp.concatenate([source[parity * 2], source[parity * 2 + 1]], axis=1)
+        far = jnp.concatenate([source[2 - parity * 2], source[3 - parity * 2]], axis=1)
+        flat = jnp.concatenate([source[spot] for spot in range(4)], axis=1)
+        out[target, :, 0:lanes] = matmul(flat, own[:, pl.ds(column, lanes)], 1, 0).astype(jnp.bfloat16)
+        for block in range(len(parts) // 2):
+            total = matmul(near, parts[2 * block][...], 1, 0) + matmul(far, parts[2 * block + 1][...], 1, 0)
+            out[target, :, (block + 1) * lanes:(block + 2) * lanes] = total.astype(jnp.bfloat16)
+
+
+def merge(place, mine, other, own, parts):
+    width = parts[0].shape[1] * (1 + len(parts) // 2)
     return pl.pallas_call(
         merge_kernel,
-        out_shape=jax.ShapeDtypeStruct((rows.shape[1], width), jnp.bfloat16),
+        out_shape=jax.ShapeDtypeStruct((2, mine.shape[1], width), jnp.bfloat16),
         grid_spec=pltpu.PrefetchScalarGridSpec(
             num_scalar_prefetch=1,
             grid=(1,),
-            in_specs=[whole(rows.shape), whole(own.shape)] + [whole(part.shape) for part in parts],
-            out_specs=whole((rows.shape[1], width)),
+            in_specs=[whole(mine.shape), whole(other.shape), whole(own.shape)]
+            + [whole(part.shape) for part in parts],
+            out_specs=whole((2, mine.shape[1], width)),
         ),
         name="merge",
-    )(place, rows, own, *parts)
+    )(place, mine, other, own, *parts)
 
 
 BACK_BY = (0, 1, 3, 2)
 
 
 def place_kernel(place, got, out):
-    cols, _, wide = got.shape
+    cores, cols, _, wide = got.shape
     rows = len(BACK_BY)
-    width = wide // rows
-    for at_col in range(cols):
-        for index, back_by in enumerate(BACK_BY):
-            at = (((place[0] + rows - back_by) % rows) * cols + at_col) * width
-            out[:, pl.ds(pl.multiple_of(at, width), width)] = got[at_col, :, index * width:(index + 1) * width]
+    lanes = wide // rows
+    for at_core in range(cores):
+        for at_col in range(cols):
+            for index, back_by in enumerate(BACK_BY):
+                at = ((((place[0] + rows - back_by) % rows) * cols + at_col) * cores + at_core) * lanes
+                out[:, pl.ds(pl.multiple_of(at, lanes), lanes)] = got[
+                    at_core, at_col, :, index * lanes:(index + 1) * lanes]
 
 
 def place_columns(place, got):
-    cols, count, wide = got.shape
+    cores, cols, count, wide = got.shape
     return pl.pallas_call(
         place_kernel,
-        out_shape=jax.ShapeDtypeStruct((count, cols * wide), jnp.bfloat16),
+        out_shape=jax.ShapeDtypeStruct((count, cores * cols * wide), jnp.bfloat16),
         grid_spec=pltpu.PrefetchScalarGridSpec(
             num_scalar_prefetch=1, grid=(1,), in_specs=[whole(got.shape)],
-            out_specs=whole((count, cols * wide))),
+            out_specs=whole((count, cores * cols * wide))),
         name="place_columns",
     )(place, got)
 
@@ -305,7 +307,8 @@
     ahead = [shift_rows(own, step, rows) for step in (3, 2, 1)]
     other_qkv = swap_cores(jnp.stack([part[:wide] for part in ahead]))
 
-    own_piece = lax.dynamic_slice_in_dim(w_merge, (parity * 2 + core) * D, D, 0)
+    piece = (w_merge.shape[0] // 2, w_merge.shape[1] // 2)
+    own_piece = lax.dynamic_slice(w_merge, (parity * piece[0], core * piece[1]), piece)
     first_y = shift_rows(own_piece, 1, rows)
     third_y = shift_rows(own_piece, 3, rows)
 
@@ -327,18 +330,15 @@
     second_z = shift_planes(second_y, 1, planes)
     mine_out = jnp.stack(out_parts)
     other_out = swap_cores(mine_out)
-    parts = []
-    for part_y, part_z in ((first_y, first_z), (third_y, third_z)):
-        parts += [part_y, part_z, swap_cores(part_y), swap_cores(part_z)]
-    parts += [second_y, second_z, swap_cores(second_y), swap_cores(second_z)]
-
     merged = merge_rows(
         place, back, row_tokens, mine_out, other_out, gain_merge)
+    merged = merged.reshape(4, cols * groups, D)
+    other_merged = swap_cores(merged)
     block = merge(
-        place, merged.reshape(4, cols * groups, D), w_merge, parts)
+        place, merged, other_merged, w_merge, (first_y, first_z, third_y, third_z, second_y, second_z))
     got = lax.all_to_all(
-        block.reshape(cols, groups, block.shape[1]), "x", split_axis=0, concat_axis=0, tiled=True)
-    return place_columns(place, got)
+        block.reshape(2 * cols, groups, block.shape[2]), ("c", "x"), split_axis=0, concat_axis=0, tiled=True)
+    return place_columns(place, got.reshape(2, cols, groups, block.shape[2]))
 
 
 def solution(mesh):

time: 181 us -> 195 us (1.077)
  the two profiles are of different devices: /device:TPU:320 before, /device:TPU:17 now
where the time goes in v2:
time: 195 us; the launch traced here: 193 us
  starting transfers between devices  65.3 us (33%)
  waiting for transfers between devices  45.4 us (23%)
  Pallas kernels  38.3 us (20%)
  blocking collectives  26.9 us (14%)
  local copies, waits for them, and re-layouts  12.4 us (6%)
  other arithmetic  4.86 us (2%)
    all_to_all x1, blocking collectives, block_step(): lax.all_to_all(block.reshape(2 * cols, groups, block.shape[2]), ('c', 'x'...  26.9 us
    ppermute x3, waiting for transfers between devices, shift_planes(): lax.ppermute(value, 'z', [(at, (at + step) % planes) for at in range(plan...  22 us
    ppermute x6, starting transfers between devices, shift_rows(): lax.ppermute(value, 'y', [(at, (at + step) % rows) for at in range(rows)])  16.4 us
    ppermute x3, starting transfers between devices, shift_planes(): lax.ppermute(value, 'z', [(at, (at + step) % planes) for at in range(plan...  15.7 us
    pallas_call x1, Pallas kernels, attention(): pl.pallas_call(attention_kernel, out_shape=jax.ShapeDtypeStruct((tiles, c...  11.3 us
    ppermute x3, starting transfers between devices, swap_cores(): return lax.ppermute(value, 'c', [(0, 1), (1, 0)])  11.1 us
    ppermute x3, starting transfers between devices, shift_cols(): lax.ppermute(value, 'x', [(at, (at + step) % cols) for at in range(cols)])  9.32 us
    ppermute x6, waiting for transfers between devices, shift_rows(): lax.ppermute(value, 'y', [(at, (at + step) % rows) for at in range(rows)])  8.72 us
  transfers between devices with their start and end apart: 18, of which 9 were waited for; matrix products, arithmetic and copies ran while one was open for 5% of the time, Pallas kernels for 14%

profile of v2, /device:TPU:17, one launch (start us, length us, event | category | flops | bytes accessed | tf_op | source)
XLA Modules:
  0.0 193.5 jit_solution(12757744769057239341)
XLA Ops:
  0.0 0.0 copy-start
  0.0 0.9 copy-done
  0.9 1.0 dynamic-slice_bitcast_fusion
  2.0 2.9 %collective-permute-start.2 = (bf16[320,640]{1,0:T(8,128)(2,1)S(1)}, bf16[320,640]{1,0:T(8,128)(2,1)S(1)}, u32[]{:S(2)}, u32[]{:S(2)}) collective-permute-start(bf16[320,640]{1,0:T(8,128)(2,1)S(1)} %pad_maximum_fusion.2), channel_id=1, source_target_pairs={{0,4},{4,8},{8,12},{12,0},{1,5},{5,9},{9,13},{13,1},{2,6},{6,10},{... | collective-permute-start | bytes 1228808 | tf_op jit(solution)/shard_map/ppermute | solution.py:30
  4.9 2.3 %collective-permute-start.1 = (bf16[320,640]{1,0:T(8,128)(2,1)S(1)}, bf16[320,640]{1,0:T(8,128)(2,1)S(1)}, u32[]{:S(2)}, u32[]{:S(2)}) collective-permute-start(bf16[320,640]{1,0:T(8,128)(2,1)S(1)} %pad_maximum_fusion.2), channel_id=1, source_target_pairs={{0,8},{4,12},{8,0},{12,4},{1,9},{5,13},{9,1},{13,5},{2,10},{6,14},... | collective-permute-start | bytes 1228808 | tf_op jit(solution)/shard_map/ppermute | solution.py:30
  7.2 2.8 %collective-permute-start = (bf16[320,640]{1,0:T(8,128)(2,1)S(1)}, bf16[320,640]{1,0:T(8,128)(2,1)S(1)}, u32[]{:S(2)}, u32[]{:S(2)}) collective-permute-start(bf16[320,640]{1,0:T(8,128)(2,1)S(1)} %pad_maximum_fusion.2), channel_id=1, source_target_pairs={{0,12},{4,0},{8,4},{12,8},{1,13},{5,1},{9,5},{13,9},{2,14},{6,2},{... | collective-permute-start | bytes 1228808 | tf_op jit(solution)/shard_map/ppermute | solution.py:30
  9.9 2.3 %spread.1 = bf16[4,128,1280]{2,1,0:T(8,128)(2,1)} custom-call(bf16[128,1280]{1,0:T(8,128)(2,1)} %tokens.1), custom_call_target="tpu_custom_call" | custom-call | tf_op jit(solution)/shard_map/spread/pallas_call | solution.py:145
  12.3 4.0 %all-to-all-start = ((bf16[4,128,1280]{2,1,0:T(8,128)(2,1)}), bf16[4,128,1280]{2,1,0:T(8,128)(2,1)S(1)}, u32[]{:S(2)}, u32[]{:S(2)}) async-start(bf16[4,128,1280]{2,1,0:T(8,128)(2,1)} %spread.1), calls=%async_computation | async-start | bytes 2621440 | tf_op jit(solution)/shard_map/all_to_all | solution.py:300
  16.3 1.5 collective-permute-done.2.third
  17.9 4.0 %collective-permute-done.1.second = bf16[320,640]{1,0:T(8,128)(2,1)S(1)} collective-permute-done((bf16[320,640]{1,0:T(8,128)(2,1)S(1)}, bf16[320,640]{1,0:T(8,128)(2,1)S(1)}, u32[]{:S(2)}, u32[]{:S(2)}) %collective-permute-start.1) | collective-permute-done | bytes 409632 | tf_op jit(solution)/shard_map/ppermute | solution.py:30
  21.9 3.2 %collective-permute-done.first = bf16[320,640]{1,0:T(8,128)(2,1)S(1)} collective-permute-done((bf16[320,640]{1,0:T(8,128)(2,1)S(1)}, bf16[320,640]{1,0:T(8,128)(2,1)S(1)}, u32[]{:S(2)}, u32[]{:S(2)}) %collective-permute-start) | collective-permute-done | bytes 409632 | tf_op jit(solution)/shard_map/ppermute | solution.py:30
  25.1 1.1 pad_maximum_fusion.1
  26.2 5.1 %collective-permute-start.3 = (bf16[3,240,640]{2,1,0:T(8,128)(2,1)}, bf16[3,240,640]{2,1,0:T(8,128)(2,1)}, u32[]{:S(2)}, u32[]{:S(2)}) collective-permute-start(bf16[3,240,640]{2,1,0:T(8,128)(2,1)} %pad_maximum_fusion.1), channel_id=1, source_target_pairs={{0,16},{16,0},{1,17},{17,1},{2,18},{18,2},{3,19},{19,3},{4,20},{20... | collective-permute-start | bytes 2764808 | tf_op jit(solution)/shard_map/ppermute | solution.py:26
  31.4 0.8 fusion
  32.2 4.4 %collective-permute-start.6 = (bf16[4,80,640]{2,1,0:T(8,128)(2,1)}, bf16[4,80,640]{2,1,0:T(8,128)(2,1)}, u32[]{:S(2)}, u32[]{:S(2)}) collective-permute-start(bf16[4,80,640]{2,1,0:T(8,128)(2,1)} %get-tuple-element.10), channel_id=1, source_target_pairs={{0,3},{1,0},{2,1},{3,2},{4,7},{5,4},{6,5},{7,6},{8,11},{9,8},{10,9... | collective-permute-start | bytes 1228808 | tf_op jit(solution)/shard_map/ppermute | solution.py:116
  36.6 2.4 %collective-permute-start.5 = (bf16[4,80,640]{2,1,0:T(8,128)(2,1)}, bf16[4,80,640]{2,1,0:T(8,128)(2,1)}, u32[]{:S(2)}, u32[]{:S(2)}) collective-permute-start(bf16[4,80,640]{2,1,0:T(8,128)(2,1)} %get-tuple-element.10), channel_id=1, source_target_pairs={{0,2},{1,3},{2,0},{3,1},{4,6},{5,7},{6,4},{7,5},{8,10},{9,11},{10,... | collective-permute-start | bytes 1228808 | tf_op jit(solution)/shard_map/ppermute | solution.py:116
  39.0 2.5 %collective-permute-start.4 = (bf16[4,80,640]{2,1,0:T(8,128)(2,1)}, bf16[4,80,640]{2,1,0:T(8,128)(2,1)}, u32[]{:S(2)}, u32[]{:S(2)}) collective-permute-start(bf16[4,80,640]{2,1,0:T(8,128)(2,1)} %get-tuple-element.10), channel_id=1, source_target_pairs={{0,1},{1,2},{2,3},{3,0},{4,5},{5,6},{6,7},{7,4},{8,9},{9,10},{10,1... | collective-permute-start | bytes 1228808 | tf_op jit(solution)/shard_map/ppermute | solution.py:116
  41.6 0.6 pad_add_fusion.1.place
  42.2 0.0 all-to-all-done.tokens.residual
  42.2 0.0 collective-permute-done.3.other
  42.2 1.1 copy-done.1
  43.2 6.4 %project_qkv.1 = bf16[4,240,512]{2,1,0:T(8,128)(2,1)} custom-call(s32[4]{0:T(128)} %pad_add_fusion.1.place, bf16[4,128,1280]{2,1,0:T(8,128)(2,1)} %copy-done.1, f32[1280]{0:T(1024)} %gain.2, bf16[240,1280]{1,0:T(8,128)(2,1)} %bitcast.36, bf16[320,640]{1,0:T(8,128)(2,1)} %copy-done.7, bf16[320,640]{1,0:T(8,128)(2,1)} %copy-done.6, ...), custom_call_target="tpu_custom_call" | custom-call | tf_op jit(solution)/shard_map/project_qkv/pallas_call | solution.py:174
  49.6 4.2 %all-to-all-start.1 = ((bf16[4,240,512]{2,1,0:T(8,128)(2,1)}), bf16[4,240,512]{2,1,0:T(8,128)(2,1)S(1)}, u32[]{:S(2)}, u32[]{:S(2)}) async-start(bf16[4,240,512]{2,1,0:T(8,128)(2,1)} %project_qkv.1), calls=%async_computation.1 | async-start | bytes 1966080 | tf_op jit(solution)/shard_map/all_to_all | solution.py:317
  53.9 0.5 collective-permute-done.6
  54.3 0.0 collective-permute-done.5
  54.3 6.1 %collective-permute-done.4 = bf16[4,80,640]{2,1,0:T(8,128)(2,1)} collective-permute-done((bf16[4,80,640]{2,1,0:T(8,128)(2,1)}, bf16[4,80,640]{2,1,0:T(8,128)(2,1)}, u32[]{:S(2)}, u32[]{:S(2)}) %collective-permute-start.4) | collective-permute-done | bytes 409632 | tf_op jit(solution)/shard_map/ppermute | solution.py:116
  60.5 1.5 pad_maximum_fusion.mine
  62.0 2.4 %collective-permute-start.7 = (bf16[4,4,80,640]{3,2,1,0:T(8,128)(2,1)S(1)}, bf16[4,4,80,640]{3,2,1,0:T(8,128)(2,1)}, u32[]{:S(2)}, u32[]{:S(2)}) collective-permute-start(bf16[4,4,80,640]{3,2,1,0:T(8,128)(2,1)S(1)} %pad_maximum_fusion.mine), channel_id=1, source_target_pairs={{0,16},{16,0},{1,17},{17,1},{2,18},{18,2},{3,19},{19,3},{4,20},{20... | collective-permute-start | bytes 4915208 | tf_op jit(solution)/shard_map/ppermute | solution.py:26
  64.4 0.3 reshape.22
  64.7 0.2 copy.14
  64.9 2.1 %broadcast_in_dim_reshape.8.seg_col = s32[2048,1]{1,0:T(8,128)} reshape(s32[16,4,32]{2,1,0:T(4,128)S(1)} %copy.14) | data formatting | bytes 16384 | tf_op jit(solution)/shard_map/broadcast_in_dim;reshape | solution.py:89
  66.9 0.7 broadcast_in_dim_reshape.7.seg_row
  67.6 0.2 slice_reduce_fusion.1
  67.8 0.2 convert_reduce_fusion.1
  68.0 0.6 pad_add_fusion.bounds
  68.6 0.0 all-to-all-done.1.qkv
  68.6 1.0 copy-done.4
  69.6 11.3 %attention.1 = bf16[4,4,80,512]{3,2,1,0:T(8,128)(2,1)} custom-call(s32[2,4]{1,0:T(2,128)} %pad_add_fusion.bounds, bf16[4,240,512]{2,1,0:T(8,128)(2,1)} %copy-done.4, s32[2048,1]{1,0:T(8,128)} %broadcast_in_dim_reshape.8.seg_col, s32[1,2048]{1,0:T(1,128)} %broadcast_in_dim_reshape.7.seg_row), custom_call_target="tpu_custom_call" | custom-call | tf_op jit(solution)/shard_map/attention/pallas_call | solution.py:97
  80.8 4.5 %all-to-all-start.2 = ((bf16[16,80,512]{2,1,0:T(8,128)(2,1)}), bf16[16,80,512]{2,1,0:T(8,128)(2,1)S(1)}, u32[]{:S(2)}, u32[]{:S(2)}) async-start(bf16[16,80,512]{2,1,0:T(8,128)(2,1)} %bitcast.33), calls=%async_computation.2 | async-start | bytes 2621440 | tf_op jit(solution)/shard_map/all_to_all | solution.py:327
  85.4 2.0 %dynamic_slice.11 = bf16[2560,128]{1,0:T(8,128)(2,1)} dynamic-slice(bf16[5120,256]{1,0:T(8,128)(2,1)} %own.1, s32[]{:T(128)S(6)} %select_n.19, s32[]{:T(128)S(6)} %select_n.20), dynamic_slice_sizes={2560,128} | dynamic-slice | bytes 1310724 | tf_op jit(solution)/shard_map/dynamic_slice | solution.py:311
  87.3 2.8 %collective-permute-start.9 = (bf16[2560,128]{1,0:T(8,128)(2,1)}, bf16[2560,128]{1,0:T(8,128)(2,1)}, u32[]{:S(2)}, u32[]{:S(2)}) collective-permute-start(bf16[2560,128]{1,0:T(8,128)(2,1)} %dynamic_slice.11), channel_id=1, source_target_pairs={{0,4},{4,8},{8,12},{12,0},{1,5},{5,9},{9,13},{13,1},{2,6},{6,10},{... | collective-permute-start | bytes 1966088 | tf_op jit(solution)/shard_map/ppermute | solution.py:30
  90.1 2.5 %collective-permute-start.11 = (bf16[2560,128]{1,0:T(8,128)(2,1)}, bf16[2560,128]{1,0:T(8,128)(2,1)}, u32[]{:S(2)}, u32[]{:S(2)}) collective-permute-start(bf16[2560,128]{1,0:T(8,128)(2,1)} %dynamic_slice.11), channel_id=1, source_target_pairs={{0,12},{4,0},{8,4},{12,8},{1,13},{5,1},{9,5},{13,9},{2,14},{6,2},{... | collective-permute-start | bytes 1966088 | tf_op jit(solution)/shard_map/ppermute | solution.py:30
  92.6 3.2 %collective-permute-start.13 = (bf16[2560,128]{1,0:T(8,128)(2,1)}, bf16[2560,128]{1,0:T(8,128)(2,1)}, u32[]{:S(2)}, u32[]{:S(2)}) collective-permute-start(bf16[2560,128]{1,0:T(8,128)(2,1)} %dynamic_slice.11), channel_id=1, source_target_pairs={{0,8},{4,12},{8,0},{12,4},{1,9},{5,13},{9,1},{13,5},{2,10},{6,14},... | collective-permute-start | bytes 1966088 | tf_op jit(solution)/shard_map/ppermute | solution.py:30
  95.9 0.0 collective-permute-done.7.other
  95.9 8.1 %all-to-all-done.2.back = bf16[16,80,512]{2,1,0:T(8,128)(2,1)S(1)} async-done(((bf16[16,80,512]{2,1,0:T(8,128)(2,1)}), bf16[16,80,512]{2,1,0:T(8,128)(2,1)S(1)}, u32[]{:S(2)}, u32[]{:S(2)}) %all-to-all-start.2) | async-done | bytes 1310752 | tf_op jit(solution)/shard_map/all_to_all | solution.py:327
  104.0 1.1 copy-done.3
  105.1 7.9 %merge_rows.1 = bf16[4,4,32,1280]{3,2,1,0:T(8,128)(2,1)} custom-call(s32[4]{0:T(128)} %pad_add_fusion.1.place, bf16[16,80,512]{2,1,0:T(8,128)(2,1)} %copy-done.3, bf16[4,128,1280]{2,1,0:T(8,128)(2,1)} %copy-done.1, bf16[4,4,80,640]{3,2,1,0:T(8,128)(2,1)} %copy-done.2, bf16[4,4,80,640]{3,2,1,0:T(8,128)(2,1)} %collective-permute-done.7.other, f32[1280]{0:T(1024)} %gain.3), custom_call_target="tpu_custom_call" | custom-call | tf_op jit(solution)/shard_map/merge_rows/pallas_call | solution.py:212
  113.0 3.6 %collective-permute-start.8 = (bf16[4,128,1280]{2,1,0:T(8,128)(2,1)}, bf16[4,128,1280]{2,1,0:T(8,128)(2,1)S(1)}, u32[]{:S(2)}, u32[]{:S(2)}) collective-permute-start(bf16[4,128,1280]{2,1,0:T(8,128)(2,1)} %bitcast.34), channel_id=1, source_target_pairs={{0,16},{16,0},{1,17},{17,1},{2,18},{18,2},{3,19},{19,3},{4,20},{20... | collective-permute-start | bytes 3932168 | tf_op jit(solution)/shard_map/ppermute | solution.py:26
  116.6 0.0 collective-permute-done.9.rest_0_
  116.6 3.5 %collective-permute-start.10 = (bf16[2560,128]{1,0:T(8,128)(2,1)}, bf16[2560,128]{1,0:T(8,128)(2,1)S(1)}, u32[]{:S(2)}, u32[]{:S(2)}) collective-permute-start(bf16[2560,128]{1,0:T(8,128)(2,1)} %collective-permute-done.9.rest_0_), channel_id=1, source_target_pairs={{0,32},{32,64},{64,96},{96,128},{128,160},{160,192},{192,224},{224... | collective-permute-start | bytes 1966088 | tf_op jit(solution)/shard_map/ppermute | solution.py:120
  120.1 0.0 collective-permute-done.11.rest_2_
  120.1 9.5 %collective-permute-start.12 = (bf16[2560,128]{1,0:T(8,128)(2,1)}, bf16[2560,128]{1,0:T(8,128)(2,1)S(1)}, u32[]{:S(2)}, u32[]{:S(2)}) collective-permute-start(bf16[2560,128]{1,0:T(8,128)(2,1)} %collective-permute-done.11.rest_2_), channel_id=1, source_target_pairs={{0,480},{32,0},{64,32},{96,64},{128,96},{160,128},{192,160},{224,1... | collective-permute-start | bytes 1966088 | tf_op jit(solution)/shard_map/ppermute | solution.py:120
  129.6 0.0 collective-permute-done.13.rest_4_
  129.7 2.6 %collective-permute-start.14 = (bf16[2560,128]{1,0:T(8,128)(2,1)}, bf16[2560,128]{1,0:T(8,128)(2,1)S(1)}, u32[]{:S(2)}, u32[]{:S(2)}) collective-permute-start(bf16[2560,128]{1,0:T(8,128)(2,1)} %collective-permute-done.13.rest_4_), channel_id=1, source_target_pairs={{0,32},{32,64},{64,96},{96,128},{128,160},{160,192},{192,224},{224... | collective-permute-start | bytes 1966088 | tf_op jit(solution)/shard_map/ppermute | solution.py:120
  132.3 3.6 %collective-permute-done.10.rest_1_ = bf16[2560,128]{1,0:T(8,128)(2,1)S(1)} collective-permute-done((bf16[2560,128]{1,0:T(8,128)(2,1)}, bf16[2560,128]{1,0:T(8,128)(2,1)S(1)}, u32[]{:S(2)}, u32[]{:S(2)}) %collective-permute-start.10) | collective-permute-done | bytes 655392 | tf_op jit(solution)/shard_map/ppermute | solution.py:120
  135.9 1.6 collective-permute-done.12.rest_3_
  137.5 16.8 %collective-permute-done.14.rest_5_ = bf16[2560,128]{1,0:T(8,128)(2,1)S(1)} collective-permute-done((bf16[2560,128]{1,0:T(8,128)(2,1)}, bf16[2560,128]{1,0:T(8,128)(2,1)S(1)}, u32[]{:S(2)}, u32[]{:S(2)}) %collective-permute-start.14) | collective-permute-done | bytes 655392 | tf_op jit(solution)/shard_map/ppermute | solution.py:120
  154.3 0.0 collective-permute-done.8.other
  154.3 0.0 copy-done.9
  154.3 0.8 copy-done.11
  155.1 1.1 copy-done.8
  156.2 8.1 %merge.1 = bf16[2,128,512]{2,1,0:T(8,128)(2,1)} custom-call(s32[4]{0:T(128)} %pad_add_fusion.1.place, bf16[4,128,1280]{2,1,0:T(8,128)(2,1)} %bitcast.35, bf16[4,128,1280]{2,1,0:T(8,128)(2,1)} %copy-done.8, bf16[5120,256]{1,0:T(8,128)(2,1)} %own.1, bf16[2560,128]{1,0:T(8,128)(2,1)} %collective-permute-done.9.rest_0_, bf16[2560,128]{1,0:T(8,128)(2,1)} %copy-done.9, ...), custom_call_target="tpu_custom_call" | custom-call | tf_op jit(solution)/shard_map/merge/pallas_call | solution.py:247
  164.3 26.9 %all_to_all.20 = bf16[8,32,512]{2,1,0:T(8,128)(2,1)} all-to-all(bf16[8,32,512]{2,1,0:T(8,128)(2,1)} %bitcast.37), channel_id=1, replica_groups=mesh['z'=16,'c'=2,'y'=4,'x'=4] {'c','x'}, dimensions={0} | all-to-all | bytes 524288 | tf_op jit(solution)/shard_map/all_to_all | solution.py:339
  191.1 2.4 %place_columns.1 = bf16[32,4096]{1,0:T(8,128)(2,1)} custom-call(s32[4]{0:T(128)} %pad_add_fusion.1.place, bf16[2,4,32,512]{3,2,1,0:T(8,128)(2,1)} %bitcast.38), custom_call_target="tpu_custom_call" | custom-call | tf_op jit(solution)/shard_map/place_columns/pallas_call | solution.py:278
  (28 shorter events, 0.2 us)
Async XLA Ops:
  0.0 0.9 copy-start
  2.0 15.8 %collective-permute-start.2 = (bf16[320,640]{1,0:T(8,128)(2,1)S(1)}, bf16[320,640]{1,0:T(8,128)(2,1)S(1)}, u32[]{:S(2)}, u32[]{:S(2)}) collective-permute-start(bf16[320,640]{1,0:T(8,128)(2,1)S(1)} %pad_maximum_fusion.2), channel_id=1, source_target_pairs={{0,4},{4,8},{8,12},{12,0},{1,5},{5,9},{9,13},{13,1},{2,6},{6,10},{... | collective-permute-start | bytes 1228808 | tf_op jit(solution)/shard_map/ppermute | solution.py:30
  4.9 16.9 %collective-permute-start.1 = (bf16[320,640]{1,0:T(8,128)(2,1)S(1)}, bf16[320,640]{1,0:T(8,128)(2,1)S(1)}, u32[]{:S(2)}, u32[]{:S(2)}) collective-permute-start(bf16[320,640]{1,0:T(8,128)(2,1)S(1)} %pad_maximum_fusion.2), channel_id=1, source_target_pairs={{0,8},{4,12},{8,0},{12,4},{1,9},{5,13},{9,1},{13,5},{2,10},{6,14},... | collective-permute-start | bytes 1228808 | tf_op jit(solution)/shard_map/ppermute | solution.py:30
  7.2 17.9 %collective-permute-start = (bf16[320,640]{1,0:T(8,128)(2,1)S(1)}, bf16[320,640]{1,0:T(8,128)(2,1)S(1)}, u32[]{:S(2)}, u32[]{:S(2)}) collective-permute-start(bf16[320,640]{1,0:T(8,128)(2,1)S(1)} %pad_maximum_fusion.2), channel_id=1, source_target_pairs={{0,12},{4,0},{8,4},{12,8},{1,13},{5,1},{9,5},{13,9},{2,14},{6,2},{... | collective-permute-start | bytes 1228808 | tf_op jit(solution)/shard_map/ppermute | solution.py:30
  12.3 29.9 %all-to-all-start = ((bf16[4,128,1280]{2,1,0:T(8,128)(2,1)}), bf16[4,128,1280]{2,1,0:T(8,128)(2,1)S(1)}, u32[]{:S(2)}, u32[]{:S(2)}) async-start(bf16[4,128,1280]{2,1,0:T(8,128)(2,1)} %spread.1), calls=%async_computation | async-start | bytes 2621440 | tf_op jit(solution)/shard_map/all_to_all | solution.py:300
  17.8 13.5 %copy-start.5 = (bf16[320,640]{1,0:T(8,128)(2,1)}, bf16[320,640]{1,0:T(8,128)(2,1)S(1)}, u32[]{:S(2)}) copy-start(bf16[320,640]{1,0:T(8,128)(2,1)S(1)} %collective-permute-done.2.third) | copy-start | bytes 1228804
  21.9 9.5 %copy-start.6 = (bf16[320,640]{1,0:T(8,128)(2,1)}, bf16[320,640]{1,0:T(8,128)(2,1)S(1)}, u32[]{:S(2)}) copy-start(bf16[320,640]{1,0:T(8,128)(2,1)S(1)} %collective-permute-done.1.second) | copy-start | bytes 1228804
  25.1 7.1 %copy-start.7 = (bf16[320,640]{1,0:T(8,128)(2,1)}, bf16[320,640]{1,0:T(8,128)(2,1)S(1)}, u32[]{:S(2)}) copy-start(bf16[320,640]{1,0:T(8,128)(2,1)S(1)} %collective-permute-done.first) | copy-start | bytes 1228804
  26.2 16.0 %collective-permute-start.3 = (bf16[3,240,640]{2,1,0:T(8,128)(2,1)}, bf16[3,240,640]{2,1,0:T(8,128)(2,1)}, u32[]{:S(2)}, u32[]{:S(2)}) collective-permute-start(bf16[3,240,640]{2,1,0:T(8,128)(2,1)} %pad_maximum_fusion.1), channel_id=1, source_target_pairs={{0,16},{16,0},{1,17},{17,1},{2,18},{18,2},{3,19},{19,3},{4,20},{20... | collective-permute-start | bytes 2764808 | tf_op jit(solution)/shard_map/ppermute | solution.py:26
  32.2 22.1 %collective-permute-start.6 = (bf16[4,80,640]{2,1,0:T(8,128)(2,1)}, bf16[4,80,640]{2,1,0:T(8,128)(2,1)}, u32[]{:S(2)}, u32[]{:S(2)}) collective-permute-start(bf16[4,80,640]{2,1,0:T(8,128)(2,1)} %get-tuple-element.10), channel_id=1, source_target_pairs={{0,3},{1,0},{2,1},{3,2},{4,7},{5,4},{6,5},{7,6},{8,11},{9,8},{10,9... | collective-permute-start | bytes 1228808 | tf_op jit(solution)/shard_map/ppermute | solution.py:116
  36.6 17.7 %collective-permute-start.5 = (bf16[4,80,640]{2,1,0:T(8,128)(2,1)}, bf16[4,80,640]{2,1,0:T(8,128)(2,1)}, u32[]{:S(2)}, u32[]{:S(2)}) collective-permute-start(bf16[4,80,640]{2,1,0:T(8,128)(2,1)} %get-tuple-element.10), channel_id=1, source_target_pairs={{0,2},{1,3},{2,0},{3,1},{4,6},{5,7},{6,4},{7,5},{8,10},{9,11},{10,... | collective-permute-start | bytes 1228808 | tf_op jit(solution)/shard_map/ppermute | solution.py:116
  39.0 21.4 %collective-permute-start.4 = (bf16[4,80,640]{2,1,0:T(8,128)(2,1)}, bf16[4,80,640]{2,1,0:T(8,128)(2,1)}, u32[]{:S(2)}, u32[]{:S(2)}) collective-permute-start(bf16[4,80,640]{2,1,0:T(8,128)(2,1)} %get-tuple-element.10), channel_id=1, source_target_pairs={{0,1},{1,2},{2,3},{3,0},{4,5},{5,6},{6,7},{7,4},{8,9},{9,10},{10,1... | collective-permute-start | bytes 1228808 | tf_op jit(solution)/shard_map/ppermute | solution.py:116
  42.2 1.1 copy-start.1
  49.6 19.0 %all-to-all-start.1 = ((bf16[4,240,512]{2,1,0:T(8,128)(2,1)}), bf16[4,240,512]{2,1,0:T(8,128)(2,1)S(1)}, u32[]{:S(2)}, u32[]{:S(2)}) async-start(bf16[4,240,512]{2,1,0:T(8,128)(2,1)} %project_qkv.1), calls=%async_computation.1 | async-start | bytes 1966080 | tf_op jit(solution)/shard_map/all_to_all | solution.py:317
  60.5 3.9 %copy-start.12 = (s32[2048]{0:T(1024)S(1)}, s32[2048]{0:T(1024)}, u32[]{:S(2)}) copy-start(s32[2048]{0:T(1024)} %param.8) | copy-start | bytes 24580
  62.0 18.9 %copy-start.2 = (bf16[4,4,80,640]{3,2,1,0:T(8,128)(2,1)}, bf16[4,4,80,640]{3,2,1,0:T(8,128)(2,1)S(1)}, u32[]{:S(2)}) copy-start(bf16[4,4,80,640]{3,2,1,0:T(8,128)(2,1)S(1)} %pad_maximum_fusion.mine) | copy-start | bytes 4915204
  62.0 33.9 %collective-permute-start.7 = (bf16[4,4,80,640]{3,2,1,0:T(8,128)(2,1)S(1)}, bf16[4,4,80,640]{3,2,1,0:T(8,128)(2,1)}, u32[]{:S(2)}, u32[]{:S(2)}) collective-permute-start(bf16[4,4,80,640]{3,2,1,0:T(8,128)(2,1)S(1)} %pad_maximum_fusion.mine), channel_id=1, source_target_pairs={{0,16},{16,0},{1,17},{17,1},{2,18},{18,2},{3,19},{19,3},{4,20},{20... | collective-permute-start | bytes 4915208 | tf_op jit(solution)/shard_map/ppermute | solution.py:26
  68.6 1.0 copy-start.4
  80.8 23.1 %all-to-all-start.2 = ((bf16[16,80,512]{2,1,0:T(8,128)(2,1)}), bf16[16,80,512]{2,1,0:T(8,128)(2,1)S(1)}, u32[]{:S(2)}, u32[]{:S(2)}) async-start(bf16[16,80,512]{2,1,0:T(8,128)(2,1)} %bitcast.33), calls=%async_computation.2 | async-start | bytes 2621440 | tf_op jit(solution)/shard_map/all_to_all | solution.py:327
  87.3 29.2 %collective-permute-start.9 = (bf16[2560,128]{1,0:T(8,128)(2,1)}, bf16[2560,128]{1,0:T(8,128)(2,1)}, u32[]{:S(2)}, u32[]{:S(2)}) collective-permute-start(bf16[2560,128]{1,0:T(8,128)(2,1)} %dynamic_slice.11), channel_id=1, source_target_pairs={{0,4},{4,8},{8,12},{12,0},{1,5},{5,9},{9,13},{13,1},{2,6},{6,10},{... | collective-permute-start | bytes 1966088 | tf_op jit(solution)/shard_map/ppermute | solution.py:30
  90.1 30.0 %collective-permute-start.11 = (bf16[2560,128]{1,0:T(8,128)(2,1)}, bf16[2560,128]{1,0:T(8,128)(2,1)}, u32[]{:S(2)}, u32[]{:S(2)}) collective-permute-start(bf16[2560,128]{1,0:T(8,128)(2,1)} %dynamic_slice.11), channel_id=1, source_target_pairs={{0,12},{4,0},{8,4},{12,8},{1,13},{5,1},{9,5},{13,9},{2,14},{6,2},{... | collective-permute-start | bytes 1966088 | tf_op jit(solution)/shard_map/ppermute | solution.py:30
  92.6 37.0 %collective-permute-start.13 = (bf16[2560,128]{1,0:T(8,128)(2,1)}, bf16[2560,128]{1,0:T(8,128)(2,1)}, u32[]{:S(2)}, u32[]{:S(2)}) collective-permute-start(bf16[2560,128]{1,0:T(8,128)(2,1)} %dynamic_slice.11), channel_id=1, source_target_pairs={{0,8},{4,12},{8,0},{12,4},{1,9},{5,13},{9,1},{13,5},{2,10},{6,14},... | collective-permute-start | bytes 1966088 | tf_op jit(solution)/shard_map/ppermute | solution.py:30
  104.0 1.1 copy-start.3
  113.0 41.3 %collective-permute-start.8 = (bf16[4,128,1280]{2,1,0:T(8,128)(2,1)}, bf16[4,128,1280]{2,1,0:T(8,128)(2,1)S(1)}, u32[]{:S(2)}, u32[]{:S(2)}) collective-permute-start(bf16[4,128,1280]{2,1,0:T(8,128)(2,1)} %bitcast.34), channel_id=1, source_target_pairs={{0,16},{16,0},{1,17},{17,1},{2,18},{18,2},{3,19},{19,3},{4,20},{20... | collective-permute-start | bytes 3932168 | tf_op jit(solution)/shard_map/ppermute | solution.py:26
  116.6 19.3 %collective-permute-start.10 = (bf16[2560,128]{1,0:T(8,128)(2,1)}, bf16[2560,128]{1,0:T(8,128)(2,1)S(1)}, u32[]{:S(2)}, u32[]{:S(2)}) collective-permute-start(bf16[2560,128]{1,0:T(8,128)(2,1)} %collective-permute-done.9.rest_0_), channel_id=1, source_target_pairs={{0,32},{32,64},{64,96},{96,128},{128,160},{160,192},{192,224},{224... | collective-permute-start | bytes 1966088 | tf_op jit(solution)/shard_map/ppermute | solution.py:120
  120.1 17.4 %collective-permute-start.12 = (bf16[2560,128]{1,0:T(8,128)(2,1)}, bf16[2560,128]{1,0:T(8,128)(2,1)S(1)}, u32[]{:S(2)}, u32[]{:S(2)}) collective-permute-start(bf16[2560,128]{1,0:T(8,128)(2,1)} %collective-permute-done.11.rest_2_), channel_id=1, source_target_pairs={{0,480},{32,0},{64,32},{96,64},{128,96},{160,128},{192,160},{224,1... | collective-permute-start | bytes 1966088 | tf_op jit(solution)/shard_map/ppermute | solution.py:120
  129.7 24.6 %collective-permute-start.14 = (bf16[2560,128]{1,0:T(8,128)(2,1)}, bf16[2560,128]{1,0:T(8,128)(2,1)S(1)}, u32[]{:S(2)}, u32[]{:S(2)}) collective-permute-start(bf16[2560,128]{1,0:T(8,128)(2,1)} %collective-permute-done.13.rest_4_), channel_id=1, source_target_pairs={{0,32},{32,64},{64,96},{96,128},{128,160},{160,192},{192,224},{224... | collective-permute-start | bytes 1966088 | tf_op jit(solution)/shard_map/ppermute | solution.py:120
  135.9 18.4 %copy-start.9 = (bf16[2560,128]{1,0:T(8,128)(2,1)}, bf16[2560,128]{1,0:T(8,128)(2,1)S(1)}, u32[]{:S(2)}) copy-start(bf16[2560,128]{1,0:T(8,128)(2,1)S(1)} %collective-permute-done.10.rest_1_) | copy-start | bytes 1966084
  137.5 16.8 %copy-start.10 = (bf16[2560,128]{1,0:T(8,128)(2,1)}, bf16[2560,128]{1,0:T(8,128)(2,1)S(1)}, u32[]{:S(2)}) copy-start(bf16[2560,128]{1,0:T(8,128)(2,1)S(1)} %collective-permute-done.12.rest_3_) | copy-start | bytes 1966084
  154.3 0.9 copy-start.11
  155.1 1.1 copy-start.8

commit v3 on v2

--- a/solution.py
+++ b/solution.py
@@ -237,13 +237,21 @@
         far = jnp.concatenate([source[2 - parity * 2], source[3 - parity * 2]], axis=1)
         flat = jnp.concatenate([source[spot] for spot in range(4)], axis=1)
         out[target, :, 0:lanes] = matmul(flat, own[:, pl.ds(column, lanes)], 1, 0).astype(jnp.bfloat16)
-        for block in range(len(parts) // 2):
-            total = matmul(near, parts[2 * block][...], 1, 0) + matmul(far, parts[2 * block + 1][...], 1, 0)
+        for block in range(3):
+            total = 0.0
+            for value, pieces in zip((near, far), (parts[block * 2:], parts[block * 2 + 1:])):
+                if block < 2:
+                    total = total + matmul(value, pieces[0][...], 1, 0)
+                else:
+                    for index, part in enumerate((pieces[0], pieces[2])):
+                        total = total + matmul(value[:, index * D:(index + 1) * D], part[...], 1, 0)
             out[target, :, (block + 1) * lanes:(block + 2) * lanes] = total.astype(jnp.bfloat16)
 
 
 def merge(place, mine, other, own, parts):
-    width = parts[0].shape[1] * (1 + len(parts) // 2)
+    first_y, first_z, third_y, third_z, second_y, second_z = parts
+    parts = first_y + first_z + third_y + third_z + [second_y[0], second_z[0], second_y[1], second_z[1]]
+    width = 4 * parts[0].shape[1]
     return pl.pallas_call(
         merge_kernel,
         out_shape=jax.ShapeDtypeStruct((2, mine.shape[1], width), jnp.bfloat16),
@@ -304,7 +312,10 @@
     own = jnp.concatenate([
         lax.dynamic_slice_in_dim(weights, core * half, half, 1),
         lax.dynamic_slice_in_dim(w_out, core * half, half, 1)], axis=0)
-    ahead = [shift_rows(own, step, rows) for step in (3, 2, 1)]
+    up, down = shift_rows(own, 1, rows), shift_rows(own, 3, rows)
+    cut = own.shape[0] // 2
+    across = [shift_rows(up[:cut], 1, rows), shift_rows(down[cut:], 3, rows)]
+    ahead = [down, jnp.concatenate(across, axis=0), up]
     other_qkv = swap_cores(jnp.stack([part[:wide] for part in ahead]))
 
     piece = (w_merge.shape[0] // 2, w_merge.shape[1] // 2)
@@ -321,13 +332,14 @@
     out_parts = [out_rows, next_out] + [shift_cols(out_rows, step, cols) for step in (2, 3)]
     first_z = shift_planes(first_y, 1, planes)
     third_z = shift_planes(third_y, planes - 1, planes)
-    second_y = shift_rows(own_piece, 2, rows)
+    cut = piece[0] // 2
+    second_y = [shift_rows(first_y[:cut], 1, rows), shift_rows(third_y[cut:], 3, rows)]
 
     attended = attention(by_head, layout, cols)
     back = lax.all_to_all(
         attended.reshape(rows * cols, HEAD_DIM, row_count), ("y", "x"),
         split_axis=0, concat_axis=0, tiled=True)
-    second_z = shift_planes(second_y, 1, planes)
+    second_z = [shift_planes(second_y[0], 1, planes), shift_planes(second_y[1], planes - 1, planes)]
     mine_out = jnp.stack(out_parts)
     other_out = swap_cores(mine_out)
     merged = merge_rows(
@@ -335,7 +347,7 @@
     merged = merged.reshape(4, cols * groups, D)
     other_merged = swap_cores(merged)
     block = merge(
-        place, merged, other_merged, w_merge, (first_y, first_z, third_y, third_z, second_y, second_z))
+        place, merged, other_merged, w_merge, ([first_y], [first_z], [third_y], [third_z], second_y, second_z))
     got = lax.all_to_all(
         block.reshape(2 * cols, groups, block.shape[2]), ("c", "x"), split_axis=0, concat_axis=0, tiled=True)
     return place_columns(place, got.reshape(2, cols, groups, block.shape[2]))

time: 195 us -> 184 us (0.944)
  the two profiles are of different devices: /device:TPU:17 before, /device:TPU:1 now
where the time goes in v3:
time: 184 us; the launch traced here: 182 us
  starting transfers between devices  78.7 us (43%)
  Pallas kernels  38.3 us (21%)
  waiting for transfers between devices  32.5 us (18%)
  local copies, waits for them, and re-layouts  14.5 us (8%)
  blocking collectives  12.8 us (7%)
  other arithmetic  4.92 us (3%)
    ppermute x8, starting transfers between devices, shift_rows(): lax.ppermute(value, 'y', [(at, (at + step) % rows) for at in range(rows)])  26.9 us
    ppermute x3, starting transfers between devices, swap_cores(): return lax.ppermute(value, 'c', [(0, 1), (1, 0)])  14.8 us
    ppermute x4, starting transfers between devices, shift_planes(): lax.ppermute(value, 'z', [(at, (at + step) % planes) for at in range(plan...  13.6 us
    all_to_all x1, blocking collectives, block_step(): lax.all_to_all(block.reshape(2 * cols, groups, block.shape[2]), ('c', 'x'...  12.8 us
    all_to_all x1, waiting for transfers between devices, block_step(): lax.all_to_all(attended.reshape(rows * cols, HEAD_DIM, row_count), ('y',...  12.7 us
    pallas_call x1, Pallas kernels, attention(): pl.pallas_call(attention_kernel, out_shape=jax.ShapeDtypeStruct((tiles, c...  11.2 us
    ppermute x3, starting transfers between devices, shift_cols(): lax.ppermute(value, 'x', [(at, (at + step) % cols) for at in range(cols)])  9.78 us
    pallas_call x1, Pallas kernels, merge(): pl.pallas_call(merge_kernel, out_shape=jax.ShapeDtypeStruct((2, mine.shap...  8.03 us
  transfers between devices with their start and end apart: 21, of which 7 were waited for; matrix products, arithmetic and copies ran while one was open for 7% of the time, Pallas kernels for 15%

profile of v3, /device:TPU:1, one launch (start us, length us, event | category | flops | bytes accessed | tf_op | source)
XLA Modules:
  0.0 182.3 jit_solution(1488181945995401825)
XLA Ops:
  0.0 0.9 copy-done
  0.9 1.0 dynamic-slice_bitcast_fusion
  2.0 4.0 %collective-permute-start.1 = (bf16[320,640]{1,0:T(8,128)(2,1)S(1)}, bf16[320,640]{1,0:T(8,128)(2,1)S(1)}, u32[]{:S(2)}, u32[]{:S(2)}) collective-permute-start(bf16[320,640]{1,0:T(8,128)(2,1)S(1)} %pad_maximum_fusion.2), channel_id=1, source_target_pairs={{0,4},{4,8},{8,12},{12,0},{1,5},{5,9},{9,13},{13,1},{2,6},{6,10},{... | collective-permute-start | bytes 1228808 | tf_op jit(solution)/shard_map/ppermute | solution.py:30
  6.0 3.4 %collective-permute-start = (bf16[320,640]{1,0:T(8,128)(2,1)S(1)}, bf16[320,640]{1,0:T(8,128)(2,1)S(1)}, u32[]{:S(2)}, u32[]{:S(2)}) collective-permute-start(bf16[320,640]{1,0:T(8,128)(2,1)S(1)} %pad_maximum_fusion.2), channel_id=1, source_target_pairs={{0,12},{4,0},{8,4},{12,8},{1,13},{5,1},{9,5},{13,9},{2,14},{6,2},{... | collective-permute-start | bytes 1228808 | tf_op jit(solution)/shard_map/ppermute | solution.py:30
  9.4 2.4 %spread.1 = bf16[4,128,1280]{2,1,0:T(8,128)(2,1)} custom-call(bf16[128,1280]{1,0:T(8,128)(2,1)} %tokens.1), custom_call_target="tpu_custom_call" | custom-call | tf_op jit(solution)/shard_map/spread/pallas_call | solution.py:145
  11.7 4.0 %all-to-all-start = ((bf16[4,128,1280]{2,1,0:T(8,128)(2,1)}), bf16[4,128,1280]{2,1,0:T(8,128)(2,1)S(1)}, u32[]{:S(2)}, u32[]{:S(2)}) async-start(bf16[4,128,1280]{2,1,0:T(8,128)(2,1)} %spread.1), calls=%async_computation | async-start | bytes 2621440 | tf_op jit(solution)/shard_map/all_to_all | solution.py:308
  15.8 0.0 collective-permute-done.1.third
  15.8 1.9 %collective-permute-start.2 = (bf16[160,640]{1,0:T(8,128)(2,1)S(1)}, bf16[160,640]{1,0:T(8,128)(2,1)S(1)}, u32[]{:S(2)}, u32[]{:S(2)}) collective-permute-start(bf16[160,640]{1,0:T(8,128)(2,1)S(1)} %slice.52), channel_id=1, source_target_pairs={{0,4},{4,8},{8,12},{12,0},{1,5},{5,9},{9,13},{13,1},{2,6},{6,10},{... | collective-permute-start | bytes 614408 | tf_op jit(solution)/shard_map/ppermute | solution.py:30
  17.7 0.0 collective-permute-done.first
  17.8 4.6 %collective-permute-start.3 = (bf16[160,640]{1,0:T(8,128)(2,1)S(1)}, bf16[160,640]{1,0:T(8,128)(2,1)S(1)}, u32[]{:S(2)}, u32[]{:S(2)}) collective-permute-start(bf16[160,640]{1,0:T(8,128)(2,1)S(1)} %slice.53), channel_id=1, source_target_pairs={{0,12},{4,0},{8,4},{12,8},{1,13},{5,1},{9,5},{13,9},{2,14},{6,2},{... | collective-permute-start | bytes 614408 | tf_op jit(solution)/shard_map/ppermute | solution.py:30
  22.4 1.1 collective-permute-done.2
  23.5 1.5 collective-permute-done.3
  25.1 1.1 pad_maximum_fusion.1
  26.2 9.1 %collective-permute-start.4 = (bf16[3,240,640]{2,1,0:T(8,128)(2,1)}, bf16[3,240,640]{2,1,0:T(8,128)(2,1)}, u32[]{:S(2)}, u32[]{:S(2)}) collective-permute-start(bf16[3,240,640]{2,1,0:T(8,128)(2,1)} %pad_maximum_fusion.1), channel_id=1, source_target_pairs={{0,16},{16,0},{1,17},{17,1},{2,18},{18,2},{3,19},{19,3},{4,20},{20... | collective-permute-start | bytes 2764808 | tf_op jit(solution)/shard_map/ppermute | solution.py:26
  35.4 0.8 fusion
  36.2 4.8 %collective-permute-start.7 = (bf16[4,80,640]{2,1,0:T(8,128)(2,1)}, bf16[4,80,640]{2,1,0:T(8,128)(2,1)}, u32[]{:S(2)}, u32[]{:S(2)}) collective-permute-start(bf16[4,80,640]{2,1,0:T(8,128)(2,1)} %get-tuple-element.10), channel_id=1, source_target_pairs={{0,3},{1,0},{2,1},{3,2},{4,7},{5,4},{6,5},{7,6},{8,11},{9,8},{10,9... | collective-permute-start | bytes 1228808 | tf_op jit(solution)/shard_map/ppermute | solution.py:116
  41.0 2.5 %collective-permute-start.6 = (bf16[4,80,640]{2,1,0:T(8,128)(2,1)}, bf16[4,80,640]{2,1,0:T(8,128)(2,1)}, u32[]{:S(2)}, u32[]{:S(2)}) collective-permute-start(bf16[4,80,640]{2,1,0:T(8,128)(2,1)} %get-tuple-element.10), channel_id=1, source_target_pairs={{0,2},{1,3},{2,0},{3,1},{4,6},{5,7},{6,4},{7,5},{8,10},{9,11},{10,... | collective-permute-start | bytes 1228808 | tf_op jit(solution)/shard_map/ppermute | solution.py:116
  43.5 2.5 %collective-permute-start.5 = (bf16[4,80,640]{2,1,0:T(8,128)(2,1)}, bf16[4,80,640]{2,1,0:T(8,128)(2,1)}, u32[]{:S(2)}, u32[]{:S(2)}) collective-permute-start(bf16[4,80,640]{2,1,0:T(8,128)(2,1)} %get-tuple-element.10), channel_id=1, source_target_pairs={{0,1},{1,2},{2,3},{3,0},{4,5},{5,6},{6,7},{7,4},{8,9},{9,10},{10,1... | collective-permute-start | bytes 1228808 | tf_op jit(solution)/shard_map/ppermute | solution.py:116
  46.0 0.7 pad_add_fusion.1.place
  46.7 1.1 copy-done.1
  47.8 6.4 %project_qkv.1 = bf16[4,240,512]{2,1,0:T(8,128)(2,1)} custom-call(s32[4]{0:T(128)} %pad_add_fusion.1.place, bf16[4,128,1280]{2,1,0:T(8,128)(2,1)} %copy-done.1, f32[1280]{0:T(1024)} %gain.2, bf16[240,1280]{1,0:T(8,128)(2,1)} %bitcast.36, bf16[320,640]{1,0:T(8,128)(2,1)} %copy-done.6, bf16[320,640]{1,0:T(8,128)(2,1)} %copy-done.7, ...), custom_call_target="tpu_custom_call" | custom-call | tf_op jit(solution)/shard_map/project_qkv/pallas_call | solution.py:174
  54.1 4.7 %all-to-all-start.1 = ((bf16[4,240,512]{2,1,0:T(8,128)(2,1)}), bf16[4,240,512]{2,1,0:T(8,128)(2,1)S(1)}, u32[]{:S(2)}, u32[]{:S(2)}) async-start(bf16[4,240,512]{2,1,0:T(8,128)(2,1)} %project_qkv.1), calls=%async_computation.1 | async-start | bytes 1966080 | tf_op jit(solution)/shard_map/all_to_all | solution.py:328
  58.8 0.0 collective-permute-done.7
  58.8 0.0 collective-permute-done.6
  58.8 6.1 %collective-permute-done.5 = bf16[4,80,640]{2,1,0:T(8,128)(2,1)} collective-permute-done((bf16[4,80,640]{2,1,0:T(8,128)(2,1)}, bf16[4,80,640]{2,1,0:T(8,128)(2,1)}, u32[]{:S(2)}, u32[]{:S(2)}) %collective-permute-start.5) | collective-permute-done | bytes 409632 | tf_op jit(solution)/shard_map/ppermute | solution.py:116
  64.9 1.5 pad_maximum_fusion.mine
  66.4 2.4 %collective-permute-start.8 = (bf16[4,4,80,640]{3,2,1,0:T(8,128)(2,1)S(1)}, bf16[4,4,80,640]{3,2,1,0:T(8,128)(2,1)}, u32[]{:S(2)}, u32[]{:S(2)}) collective-permute-start(bf16[4,4,80,640]{3,2,1,0:T(8,128)(2,1)S(1)} %pad_maximum_fusion.mine), channel_id=1, source_target_pairs={{0,16},{16,0},{1,17},{17,1},{2,18},{18,2},{3,19},{19,3},{4,20},{20... | collective-permute-start | bytes 4915208 | tf_op jit(solution)/shard_map/ppermute | solution.py:26
  68.8 0.3 reshape.22
  69.1 0.2 copy.14
  69.3 2.1 %broadcast_in_dim_reshape.8.seg_col = s32[2048,1]{1,0:T(8,128)} reshape(s32[16,4,32]{2,1,0:T(4,128)S(1)} %copy.14) | data formatting | bytes 16384 | tf_op jit(solution)/shard_map/broadcast_in_dim;reshape | solution.py:89
  71.4 0.7 broadcast_in_dim_reshape.7.seg_row
  72.1 0.2 slice_reduce_fusion.1
  72.2 0.2 convert_reduce_fusion.1
  72.5 0.6 pad_add_fusion.bounds
  73.1 0.0 all-to-all-done.1.qkv
  73.1 1.0 copy-done.4
  74.0 11.2 %attention.1 = bf16[4,4,80,512]{3,2,1,0:T(8,128)(2,1)} custom-call(s32[2,4]{1,0:T(2,128)} %pad_add_fusion.bounds, bf16[4,240,512]{2,1,0:T(8,128)(2,1)} %copy-done.4, s32[2048,1]{1,0:T(8,128)} %broadcast_in_dim_reshape.8.seg_col, s32[1,2048]{1,0:T(1,128)} %broadcast_in_dim_reshape.7.seg_row), custom_call_target="tpu_custom_call" | custom-call | tf_op jit(solution)/shard_map/attention/pallas_call | solution.py:97
  85.3 5.1 %all-to-all-start.2 = ((bf16[16,80,512]{2,1,0:T(8,128)(2,1)}), bf16[16,80,512]{2,1,0:T(8,128)(2,1)S(1)}, u32[]{:S(2)}, u32[]{:S(2)}) async-start(bf16[16,80,512]{2,1,0:T(8,128)(2,1)} %bitcast.35), calls=%async_computation.2 | async-start | bytes 2621440 | tf_op jit(solution)/shard_map/all_to_all | solution.py:339
  90.4 2.0 %dynamic_slice.11 = bf16[2560,128]{1,0:T(8,128)(2,1)} dynamic-slice(bf16[5120,256]{1,0:T(8,128)(2,1)} %own.1, s32[]{:T(128)S(6)} %select_n.19, s32[]{:T(128)S(6)} %select_n.20), dynamic_slice_sizes={2560,128} | dynamic-slice | bytes 1310724 | tf_op jit(solution)/shard_map/dynamic_slice | solution.py:322
  92.4 3.2 %collective-permute-start.10 = (bf16[2560,128]{1,0:T(8,128)(2,1)}, bf16[2560,128]{1,0:T(8,128)(2,1)}, u32[]{:S(2)}, u32[]{:S(2)}) collective-permute-start(bf16[2560,128]{1,0:T(8,128)(2,1)} %dynamic_slice.11), channel_id=1, source_target_pairs={{0,4},{4,8},{8,12},{12,0},{1,5},{5,9},{9,13},{13,1},{2,6},{6,10},{... | collective-permute-start | bytes 1966088 | tf_op jit(solution)/shard_map/ppermute | solution.py:30
  95.6 3.2 %collective-permute-start.12 = (bf16[2560,128]{1,0:T(8,128)(2,1)}, bf16[2560,128]{1,0:T(8,128)(2,1)}, u32[]{:S(2)}, u32[]{:S(2)}) collective-permute-start(bf16[2560,128]{1,0:T(8,128)(2,1)} %dynamic_slice.11), channel_id=1, source_target_pairs={{0,12},{4,0},{8,4},{12,8},{1,13},{5,1},{9,5},{13,9},{2,14},{6,2},{... | collective-permute-start | bytes 1966088 | tf_op jit(solution)/shard_map/ppermute | solution.py:30
  98.9 0.0 collective-permute-done.8.other
  98.9 12.7 %all-to-all-done.2.back = bf16[16,80,512]{2,1,0:T(8,128)(2,1)S(1)} async-done(((bf16[16,80,512]{2,1,0:T(8,128)(2,1)}), bf16[16,80,512]{2,1,0:T(8,128)(2,1)S(1)}, u32[]{:S(2)}, u32[]{:S(2)}) %all-to-all-start.2) | async-done | bytes 1310752 | tf_op jit(solution)/shard_map/all_to_all | solution.py:339
  111.7 1.1 copy-done.3
  112.7 7.9 %merge_rows.1 = bf16[4,4,32,1280]{3,2,1,0:T(8,128)(2,1)} custom-call(s32[4]{0:T(128)} %pad_add_fusion.1.place, bf16[16,80,512]{2,1,0:T(8,128)(2,1)} %copy-done.3, bf16[4,128,1280]{2,1,0:T(8,128)(2,1)} %copy-done.1, bf16[4,4,80,640]{3,2,1,0:T(8,128)(2,1)} %copy-done.2, bf16[4,4,80,640]{3,2,1,0:T(8,128)(2,1)} %collective-permute-done.8.other, f32[1280]{0:T(1024)} %gain.3), custom_call_target="tpu_custom_call" | custom-call | tf_op jit(solution)/shard_map/merge_rows/pallas_call | solution.py:212
  120.6 3.3 %collective-permute-start.9 = (bf16[4,128,1280]{2,1,0:T(8,128)(2,1)}, bf16[4,128,1280]{2,1,0:T(8,128)(2,1)S(1)}, u32[]{:S(2)}, u32[]{:S(2)}) collective-permute-start(bf16[4,128,1280]{2,1,0:T(8,128)(2,1)} %bitcast.33), channel_id=1, source_target_pairs={{0,16},{16,0},{1,17},{17,1},{2,18},{18,2},{3,19},{19,3},{4,20},{20... | collective-permute-start | bytes 3932168 | tf_op jit(solution)/shard_map/ppermute | solution.py:26
  123.9 0.0 collective-permute-done.10.rest_0_
  123.9 1.0 slice.60
  124.9 1.9 %collective-permute-start.14 = (bf16[1280,128]{1,0:T(8,128)(2,1)S(1)}, bf16[1280,128]{1,0:T(8,128)(2,1)S(1)}, u32[]{:S(2)}, u32[]{:S(2)}) collective-permute-start(bf16[1280,128]{1,0:T(8,128)(2,1)S(1)} %slice.60), channel_id=1, source_target_pairs={{0,4},{4,8},{8,12},{12,0},{1,5},{5,9},{9,13},{13,1},{2,6},{6,10},{... | collective-permute-start | bytes 983048 | tf_op jit(solution)/shard_map/ppermute | solution.py:30
  126.9 1.9 %collective-permute-start.11 = (bf16[2560,128]{1,0:T(8,128)(2,1)}, bf16[2560,128]{1,0:T(8,128)(2,1)S(1)}, u32[]{:S(2)}, u32[]{:S(2)}) collective-permute-start(bf16[2560,128]{1,0:T(8,128)(2,1)} %collective-permute-done.10.rest_0_), channel_id=1, source_target_pairs={{0,32},{32,64},{64,96},{96,128},{128,160},{160,192},{192,224},{224... | collective-permute-start | bytes 1966088 | tf_op jit(solution)/shard_map/ppermute | solution.py:120
  128.8 0.0 collective-permute-done.12.rest_2_
  128.8 6.6 %collective-permute-start.13 = (bf16[2560,128]{1,0:T(8,128)(2,1)}, bf16[2560,128]{1,0:T(8,128)(2,1)S(1)}, u32[]{:S(2)}, u32[]{:S(2)}) collective-permute-start(bf16[2560,128]{1,0:T(8,128)(2,1)} %collective-permute-done.12.rest_2_), channel_id=1, source_target_pairs={{0,480},{32,0},{64,32},{96,64},{128,96},{160,128},{192,160},{224,1... | collective-permute-start | bytes 1966088 | tf_op jit(solution)/shard_map/ppermute | solution.py:120
  135.4 1.0 slice.61
  136.5 4.6 %collective-permute-start.16 = (bf16[1280,128]{1,0:T(8,128)(2,1)S(1)}, bf16[1280,128]{1,0:T(8,128)(2,1)S(1)}, u32[]{:S(2)}, u32[]{:S(2)}) collective-permute-start(bf16[1280,128]{1,0:T(8,128)(2,1)S(1)} %slice.61), channel_id=1, source_target_pairs={{0,12},{4,0},{8,4},{12,8},{1,13},{5,1},{9,5},{13,9},{2,14},{6,2},{... | collective-permute-start | bytes 983048 | tf_op jit(solution)/shard_map/ppermute | solution.py:30
  141.1 1.9 %collective-permute-start.15 = (bf16[1280,128]{1,0:T(8,128)(2,1)S(1)}, bf16[1280,128]{1,0:T(8,128)(2,1)S(1)}, u32[]{:S(2)}, u32[]{:S(2)}) collective-permute-start(bf16[1280,128]{1,0:T(8,128)(2,1)S(1)} %collective-permute-done.14.rest_4_), channel_id=1, source_target_pairs={{0,32},{32,64},{64,96},{96,128},{128,160},{160,192},{192,224},{224... | collective-permute-start | bytes 983048 | tf_op jit(solution)/shard_map/ppermute | solution.py:120
  143.0 4.5 %collective-permute-done.16.rest_6_ = bf16[1280,128]{1,0:T(8,128)(2,1)S(1)} collective-permute-done((bf16[1280,128]{1,0:T(8,128)(2,1)S(1)}, bf16[1280,128]{1,0:T(8,128)(2,1)S(1)}, u32[]{:S(2)}, u32[]{:S(2)}) %collective-permute-start.16) | collective-permute-done | bytes 327712 | tf_op jit(solution)/shard_map/ppermute | solution.py:30
  147.5 3.1 %collective-permute-start.17 = (bf16[1280,128]{1,0:T(8,128)(2,1)S(1)}, bf16[1280,128]{1,0:T(8,128)(2,1)S(1)}, u32[]{:S(2)}, u32[]{:S(2)}) collective-permute-start(bf16[1280,128]{1,0:T(8,128)(2,1)S(1)} %collective-permute-done.16.rest_6_), channel_id=1, source_target_pairs={{0,480},{32,0},{64,32},{96,64},{128,96},{160,128},{192,160},{224,1... | collective-permute-start | bytes 983048 | tf_op jit(solution)/shard_map/ppermute | solution.py:120
  150.6 5.1 %collective-permute-done.15.rest_5_ = bf16[1280,128]{1,0:T(8,128)(2,1)S(1)} collective-permute-done((bf16[1280,128]{1,0:T(8,128)(2,1)S(1)}, bf16[1280,128]{1,0:T(8,128)(2,1)S(1)}, u32[]{:S(2)}, u32[]{:S(2)}) %collective-permute-start.15) | collective-permute-done | bytes 327712 | tf_op jit(solution)/shard_map/ppermute | solution.py:120
  155.7 1.5 collective-permute-done.17.rest_7_
  157.2 0.7 copy-done.14
  158.0 1.1 copy-done.8
  159.1 8.0 %merge.1 = bf16[2,128,512]{2,1,0:T(8,128)(2,1)} custom-call(s32[4]{0:T(128)} %pad_add_fusion.1.place, bf16[4,128,1280]{2,1,0:T(8,128)(2,1)} %bitcast.34, bf16[4,128,1280]{2,1,0:T(8,128)(2,1)} %copy-done.8, bf16[5120,256]{1,0:T(8,128)(2,1)} %own.1, bf16[2560,128]{1,0:T(8,128)(2,1)} %collective-permute-done.10.rest_0_, bf16[2560,128]{1,0:T(8,128)(2,1)} %copy-done.9, ...), custom_call_target="tpu_custom_call" | custom-call | tf_op jit(solution)/shard_map/merge/pallas_call | solution.py:255
  167.1 12.8 %all_to_all.20 = bf16[8,32,512]{2,1,0:T(8,128)(2,1)} all-to-all(bf16[8,32,512]{2,1,0:T(8,128)(2,1)} %bitcast.37), channel_id=1, replica_groups=mesh['z'=16,'c'=2,'y'=4,'x'=4] {'c','x'}, dimensions={0} | all-to-all | bytes 524288 | tf_op jit(solution)/shard_map/all_to_all | solution.py:351
  179.9 2.4 %place_columns.1 = bf16[32,4096]{1,0:T(8,128)(2,1)} custom-call(s32[4]{0:T(128)} %pad_add_fusion.1.place, bf16[2,4,32,512]{3,2,1,0:T(8,128)(2,1)} %bitcast.38), custom_call_target="tpu_custom_call" | custom-call | tf_op jit(solution)/shard_map/place_columns/pallas_call | solution.py:286
  (46 shorter events, 0.3 us)
Async XLA Ops:
  0.0 0.9 copy-start
  2.0 13.8 %collective-permute-start.1 = (bf16[320,640]{1,0:T(8,128)(2,1)S(1)}, bf16[320,640]{1,0:T(8,128)(2,1)S(1)}, u32[]{:S(2)}, u32[]{:S(2)}) collective-permute-start(bf16[320,640]{1,0:T(8,128)(2,1)S(1)} %pad_maximum_fusion.2), channel_id=1, source_target_pairs={{0,4},{4,8},{8,12},{12,0},{1,5},{5,9},{9,13},{13,1},{2,6},{6,10},{... | collective-permute-start | bytes 1228808 | tf_op jit(solution)/shard_map/ppermute | solution.py:30
  6.0 11.7 %collective-permute-start = (bf16[320,640]{1,0:T(8,128)(2,1)S(1)}, bf16[320,640]{1,0:T(8,128)(2,1)S(1)}, u32[]{:S(2)}, u32[]{:S(2)}) collective-permute-start(bf16[320,640]{1,0:T(8,128)(2,1)S(1)} %pad_maximum_fusion.2), channel_id=1, source_target_pairs={{0,12},{4,0},{8,4},{12,8},{1,13},{5,1},{9,5},{13,9},{2,14},{6,2},{... | collective-permute-start | bytes 1228808 | tf_op jit(solution)/shard_map/ppermute | solution.py:30
  11.7 34.9 %all-to-all-start = ((bf16[4,128,1280]{2,1,0:T(8,128)(2,1)}), bf16[4,128,1280]{2,1,0:T(8,128)(2,1)S(1)}, u32[]{:S(2)}, u32[]{:S(2)}) async-start(bf16[4,128,1280]{2,1,0:T(8,128)(2,1)} %spread.1), calls=%async_computation | async-start | bytes 2621440 | tf_op jit(solution)/shard_map/all_to_all | solution.py:308
  15.8 19.5 %copy-start.5 = (bf16[320,640]{1,0:T(8,128)(2,1)}, bf16[320,640]{1,0:T(8,128)(2,1)S(1)}, u32[]{:S(2)}) copy-start(bf16[320,640]{1,0:T(8,128)(2,1)S(1)} %collective-permute-done.1.third) | copy-start | bytes 1228804
  15.8 7.7 %collective-permute-start.2 = (bf16[160,640]{1,0:T(8,128)(2,1)S(1)}, bf16[160,640]{1,0:T(8,128)(2,1)S(1)}, u32[]{:S(2)}, u32[]{:S(2)}) collective-permute-start(bf16[160,640]{1,0:T(8,128)(2,1)S(1)} %slice.52), channel_id=1, source_target_pairs={{0,4},{4,8},{8,12},{12,0},{1,5},{5,9},{9,13},{13,1},{2,6},{6,10},{... | collective-permute-start | bytes 614408 | tf_op jit(solution)/shard_map/ppermute | solution.py:30
  17.8 17.6 %copy-start.6 = (bf16[320,640]{1,0:T(8,128)(2,1)}, bf16[320,640]{1,0:T(8,128)(2,1)S(1)}, u32[]{:S(2)}) copy-start(bf16[320,640]{1,0:T(8,128)(2,1)S(1)} %collective-permute-done.first) | copy-start | bytes 1228804
  17.8 7.3 %collective-permute-start.3 = (bf16[160,640]{1,0:T(8,128)(2,1)S(1)}, bf16[160,640]{1,0:T(8,128)(2,1)S(1)}, u32[]{:S(2)}, u32[]{:S(2)}) collective-permute-start(bf16[160,640]{1,0:T(8,128)(2,1)S(1)} %slice.53), channel_id=1, source_target_pairs={{0,12},{4,0},{8,4},{12,8},{1,13},{5,1},{9,5},{13,9},{2,14},{6,2},{... | collective-permute-start | bytes 614408 | tf_op jit(solution)/shard_map/ppermute | solution.py:30
  25.1 11.1 %copy-start.7 = (bf16[320,640]{1,0:T(8,128)(2,1)}, bf16[320,640]{1,0:T(8,128)(2,1)S(1)}, u32[]{:S(2)}) copy-start(bf16[320,640]{1,0:T(8,128)(2,1)S(1)} %constant_dynamic-update-slice_fusion.second) | copy-start | bytes 1228804
  26.2 20.5 %collective-permute-start.4 = (bf16[3,240,640]{2,1,0:T(8,128)(2,1)}, bf16[3,240,640]{2,1,0:T(8,128)(2,1)}, u32[]{:S(2)}, u32[]{:S(2)}) collective-permute-start(bf16[3,240,640]{2,1,0:T(8,128)(2,1)} %pad_maximum_fusion.1), channel_id=1, source_target_pairs={{0,16},{16,0},{1,17},{17,1},{2,18},{18,2},{3,19},{19,3},{4,20},{20... | collective-permute-start | bytes 2764808 | tf_op jit(solution)/shard_map/ppermute | solution.py:26
  36.2 22.6 %collective-permute-start.7 = (bf16[4,80,640]{2,1,0:T(8,128)(2,1)}, bf16[4,80,640]{2,1,0:T(8,128)(2,1)}, u32[]{:S(2)}, u32[]{:S(2)}) collective-permute-start(bf16[4,80,640]{2,1,0:T(8,128)(2,1)} %get-tuple-element.10), channel_id=1, source_target_pairs={{0,3},{1,0},{2,1},{3,2},{4,7},{5,4},{6,5},{7,6},{8,11},{9,8},{10,9... | collective-permute-start | bytes 1228808 | tf_op jit(solution)/shard_map/ppermute | solution.py:116
  41.0 17.8 %collective-permute-start.6 = (bf16[4,80,640]{2,1,0:T(8,128)(2,1)}, bf16[4,80,640]{2,1,0:T(8,128)(2,1)}, u32[]{:S(2)}, u32[]{:S(2)}) collective-permute-start(bf16[4,80,640]{2,1,0:T(8,128)(2,1)} %get-tuple-element.10), channel_id=1, source_target_pairs={{0,2},{1,3},{2,0},{3,1},{4,6},{5,7},{6,4},{7,5},{8,10},{9,11},{10,... | collective-permute-start | bytes 1228808 | tf_op jit(solution)/shard_map/ppermute | solution.py:116
  43.5 21.4 %collective-permute-start.5 = (bf16[4,80,640]{2,1,0:T(8,128)(2,1)}, bf16[4,80,640]{2,1,0:T(8,128)(2,1)}, u32[]{:S(2)}, u32[]{:S(2)}) collective-permute-start(bf16[4,80,640]{2,1,0:T(8,128)(2,1)} %get-tuple-element.10), channel_id=1, source_target_pairs={{0,1},{1,2},{2,3},{3,0},{4,5},{5,6},{6,7},{7,4},{8,9},{9,10},{10,1... | collective-permute-start | bytes 1228808 | tf_op jit(solution)/shard_map/ppermute | solution.py:116
  46.7 1.1 copy-start.1
  54.1 18.9 %all-to-all-start.1 = ((bf16[4,240,512]{2,1,0:T(8,128)(2,1)}), bf16[4,240,512]{2,1,0:T(8,128)(2,1)S(1)}, u32[]{:S(2)}, u32[]{:S(2)}) async-start(bf16[4,240,512]{2,1,0:T(8,128)(2,1)} %project_qkv.1), calls=%async_computation.1 | async-start | bytes 1966080 | tf_op jit(solution)/shard_map/all_to_all | solution.py:328
  64.9 3.9 %copy-start.15 = (s32[2048]{0:T(1024)S(1)}, s32[2048]{0:T(1024)}, u32[]{:S(2)}) copy-start(s32[2048]{0:T(1024)} %param.8) | copy-start | bytes 24580
  66.4 18.9 %copy-start.2 = (bf16[4,4,80,640]{3,2,1,0:T(8,128)(2,1)}, bf16[4,4,80,640]{3,2,1,0:T(8,128)(2,1)S(1)}, u32[]{:S(2)}) copy-start(bf16[4,4,80,640]{3,2,1,0:T(8,128)(2,1)S(1)} %pad_maximum_fusion.mine) | copy-start | bytes 4915204
  66.4 32.5 %collective-permute-start.8 = (bf16[4,4,80,640]{3,2,1,0:T(8,128)(2,1)S(1)}, bf16[4,4,80,640]{3,2,1,0:T(8,128)(2,1)}, u32[]{:S(2)}, u32[]{:S(2)}) collective-permute-start(bf16[4,4,80,640]{3,2,1,0:T(8,128)(2,1)S(1)} %pad_maximum_fusion.mine), channel_id=1, source_target_pairs={{0,16},{16,0},{1,17},{17,1},{2,18},{18,2},{3,19},{19,3},{4,20},{20... | collective-permute-start | bytes 4915208 | tf_op jit(solution)/shard_map/ppermute | solution.py:26
  73.1 1.0 copy-start.4
  85.3 26.4 %all-to-all-start.2 = ((bf16[16,80,512]{2,1,0:T(8,128)(2,1)}), bf16[16,80,512]{2,1,0:T(8,128)(2,1)S(1)}, u32[]{:S(2)}, u32[]{:S(2)}) async-start(bf16[16,80,512]{2,1,0:T(8,128)(2,1)} %bitcast.35), calls=%async_computation.2 | async-start | bytes 2621440 | tf_op jit(solution)/shard_map/all_to_all | solution.py:339
  92.4 31.5 %collective-permute-start.10 = (bf16[2560,128]{1,0:T(8,128)(2,1)}, bf16[2560,128]{1,0:T(8,128)(2,1)}, u32[]{:S(2)}, u32[]{:S(2)}) collective-permute-start(bf16[2560,128]{1,0:T(8,128)(2,1)} %dynamic_slice.11), channel_id=1, source_target_pairs={{0,4},{4,8},{8,12},{12,0},{1,5},{5,9},{9,13},{13,1},{2,6},{6,10},{... | collective-permute-start | bytes 1966088 | tf_op jit(solution)/shard_map/ppermute | solution.py:30
  95.6 33.1 %collective-permute-start.12 = (bf16[2560,128]{1,0:T(8,128)(2,1)}, bf16[2560,128]{1,0:T(8,128)(2,1)}, u32[]{:S(2)}, u32[]{:S(2)}) collective-permute-start(bf16[2560,128]{1,0:T(8,128)(2,1)} %dynamic_slice.11), channel_id=1, source_target_pairs={{0,12},{4,0},{8,4},{12,8},{1,13},{5,1},{9,5},{13,9},{2,14},{6,2},{... | collective-permute-start | bytes 1966088 | tf_op jit(solution)/shard_map/ppermute | solution.py:30
  111.6 1.1 copy-start.3
  120.6 37.3 %collective-permute-start.9 = (bf16[4,128,1280]{2,1,0:T(8,128)(2,1)}, bf16[4,128,1280]{2,1,0:T(8,128)(2,1)S(1)}, u32[]{:S(2)}, u32[]{:S(2)}) collective-permute-start(bf16[4,128,1280]{2,1,0:T(8,128)(2,1)} %bitcast.33), channel_id=1, source_target_pairs={{0,16},{16,0},{1,17},{17,1},{2,18},{18,2},{3,19},{19,3},{4,20},{20... | collective-permute-start | bytes 3932168 | tf_op jit(solution)/shard_map/ppermute | solution.py:26
  124.9 16.1 %collective-permute-start.14 = (bf16[1280,128]{1,0:T(8,128)(2,1)S(1)}, bf16[1280,128]{1,0:T(8,128)(2,1)S(1)}, u32[]{:S(2)}, u32[]{:S(2)}) collective-permute-start(bf16[1280,128]{1,0:T(8,128)(2,1)S(1)} %slice.60), channel_id=1, source_target_pairs={{0,4},{4,8},{8,12},{12,0},{1,5},{5,9},{9,13},{13,1},{2,6},{6,10},{... | collective-permute-start | bytes 983048 | tf_op jit(solution)/shard_map/ppermute | solution.py:30
  126.9 23.7 %collective-permute-start.11 = (bf16[2560,128]{1,0:T(8,128)(2,1)}, bf16[2560,128]{1,0:T(8,128)(2,1)S(1)}, u32[]{:S(2)}, u32[]{:S(2)}) collective-permute-start(bf16[2560,128]{1,0:T(8,128)(2,1)} %collective-permute-done.10.rest_0_), channel_id=1, source_target_pairs={{0,32},{32,64},{64,96},{96,128},{128,160},{160,192},{192,224},{224... | collective-permute-start | bytes 1966088 | tf_op jit(solution)/shard_map/ppermute | solution.py:120
  128.8 21.8 %collective-permute-start.13 = (bf16[2560,128]{1,0:T(8,128)(2,1)}, bf16[2560,128]{1,0:T(8,128)(2,1)S(1)}, u32[]{:S(2)}, u32[]{:S(2)}) collective-permute-start(bf16[2560,128]{1,0:T(8,128)(2,1)} %collective-permute-done.12.rest_2_), channel_id=1, source_target_pairs={{0,480},{32,0},{64,32},{96,64},{128,96},{160,128},{192,160},{224,1... | collective-permute-start | bytes 1966088 | tf_op jit(solution)/shard_map/ppermute | solution.py:120
  136.5 11.1 %collective-permute-start.16 = (bf16[1280,128]{1,0:T(8,128)(2,1)S(1)}, bf16[1280,128]{1,0:T(8,128)(2,1)S(1)}, u32[]{:S(2)}, u32[]{:S(2)}) collective-permute-start(bf16[1280,128]{1,0:T(8,128)(2,1)S(1)} %slice.61), channel_id=1, source_target_pairs={{0,12},{4,0},{8,4},{12,8},{1,13},{5,1},{9,5},{13,9},{2,14},{6,2},{... | collective-permute-start | bytes 983048 | tf_op jit(solution)/shard_map/ppermute | solution.py:30
  141.0 16.9 %copy-start.11 = (bf16[1280,128]{1,0:T(8,128)(2,1)}, bf16[1280,128]{1,0:T(8,128)(2,1)S(1)}, u32[]{:S(2)}) copy-start(bf16[1280,128]{1,0:T(8,128)(2,1)S(1)} %collective-permute-done.14.rest_4_) | copy-start | bytes 983044
  141.1 14.7 %collective-permute-start.15 = (bf16[1280,128]{1,0:T(8,128)(2,1)S(1)}, bf16[1280,128]{1,0:T(8,128)(2,1)S(1)}, u32[]{:S(2)}, u32[]{:S(2)}) collective-permute-start(bf16[1280,128]{1,0:T(8,128)(2,1)S(1)} %collective-permute-done.14.rest_4_), channel_id=1, source_target_pairs={{0,32},{32,64},{64,96},{96,128},{128,160},{160,192},{192,224},{224... | collective-permute-start | bytes 983048 | tf_op jit(solution)/shard_map/ppermute | solution.py:120
  147.5 10.5 %copy-start.12 = (bf16[1280,128]{1,0:T(8,128)(2,1)}, bf16[1280,128]{1,0:T(8,128)(2,1)S(1)}, u32[]{:S(2)}) copy-start(bf16[1280,128]{1,0:T(8,128)(2,1)S(1)} %collective-permute-done.16.rest_6_) | copy-start | bytes 983044
  147.5 9.7 %collective-permute-start.17 = (bf16[1280,128]{1,0:T(8,128)(2,1)S(1)}, bf16[1280,128]{1,0:T(8,128)(2,1)S(1)}, u32[]{:S(2)}, u32[]{:S(2)}) collective-permute-start(bf16[1280,128]{1,0:T(8,128)(2,1)S(1)} %collective-permute-done.16.rest_6_), channel_id=1, source_target_pairs={{0,480},{32,0},{64,32},{96,64},{128,96},{160,128},{192,160},{224,1... | collective-permute-start | bytes 983048 | tf_op jit(solution)/shard_map/ppermute | solution.py:120
  150.6 7.4 %copy-start.9 = (bf16[2560,128]{1,0:T(8,128)(2,1)}, bf16[2560,128]{1,0:T(8,128)(2,1)S(1)}, u32[]{:S(2)}) copy-start(bf16[2560,128]{1,0:T(8,128)(2,1)S(1)} %collective-permute-done.11.rest_1_) | copy-start | bytes 1966084
  150.6 7.4 %copy-start.10 = (bf16[2560,128]{1,0:T(8,128)(2,1)}, bf16[2560,128]{1,0:T(8,128)(2,1)S(1)}, u32[]{:S(2)}) copy-start(bf16[2560,128]{1,0:T(8,128)(2,1)S(1)} %collective-permute-done.13.rest_3_) | copy-start | bytes 1966084
  155.7 1.5 copy-start.13
  157.2 0.7 copy-start.14
  158.0 1.1 copy-start.8

commit v4 on v2

--- a/solution.py
+++ b/solution.py
@@ -116,10 +116,6 @@
     return lax.ppermute(value, "x", [(at, (at + step) % cols) for at in range(cols)])
 
 
-def shift_planes(value, step, planes):
-    return lax.ppermute(value, "z", [(at, (at + step) % planes) for at in range(planes)])
-
-
 def matmul(left, right, left_dim, right_dim):
     return lax.dot_general(
         left, right, (((left_dim,), (right_dim,)), ((), ())), preferred_element_type=jnp.float32)
@@ -227,74 +223,73 @@
     )(place, back, row_tokens, mine, other, gain)
 
 
-def merge_kernel(place, mine, other, own, *rest):
-    parts, out = rest[:-1], rest[-1]
-    core, parity = place[1], place[3]
-    lanes = parts[0].shape[1]
-    column = pl.multiple_of(core * lanes, lanes)
-    for source, target in ((mine, core), (other, 1 - core)):
-        near = jnp.concatenate([source[parity * 2], source[parity * 2 + 1]], axis=1)
-        far = jnp.concatenate([source[2 - parity * 2], source[3 - parity * 2]], axis=1)
-        flat = jnp.concatenate([source[spot] for spot in range(4)], axis=1)
-        out[target, :, 0:lanes] = matmul(flat, own[:, pl.ds(column, lanes)], 1, 0).astype(jnp.bfloat16)
-        for block in range(len(parts) // 2):
-            total = matmul(near, parts[2 * block][...], 1, 0) + matmul(far, parts[2 * block + 1][...], 1, 0)
-            out[target, :, (block + 1) * lanes:(block + 2) * lanes] = total.astype(jnp.bfloat16)
-
-
-def merge(place, mine, other, own, parts):
-    width = parts[0].shape[1] * (1 + len(parts) // 2)
+def merge_kernel(place, mine, other, weights, out, flat):
+    core = place[1]
+    count = mine.shape[1]
+
+    @pl.when(pl.program_id(0) == 0)
+    def _():
+        for spot in range(4):
+            flat[0:count, spot * D:(spot + 1) * D] = mine[spot]
+            flat[count:2 * count, spot * D:(spot + 1) * D] = other[spot]
+
+    wide = jnp.concatenate([weights[0], weights[1]], axis=1)
+    value = matmul(flat[...], wide, 1, 0).astype(jnp.bfloat16)
+    out[core] = value[0:count, :]
+    out[1 - core] = value[count:2 * count, :]
+
+
+def merge(place, mine, other, weights):
+    blocks, depth, lanes = weights.shape
+    count = mine.shape[1]
     return pl.pallas_call(
         merge_kernel,
-        out_shape=jax.ShapeDtypeStruct((2, mine.shape[1], width), jnp.bfloat16),
+        out_shape=jax.ShapeDtypeStruct((2, count, blocks * lanes), jnp.bfloat16),
         grid_spec=pltpu.PrefetchScalarGridSpec(
             num_scalar_prefetch=1,
-            grid=(1,),
-            in_specs=[whole(mine.shape), whole(other.shape), whole(own.shape)]
-            + [whole(part.shape) for part in parts],
-            out_specs=whole((2, mine.shape[1], width)),
+            grid=(blocks // 2,),
+            in_specs=[whole(mine.shape), whole(other.shape),
+                      pl.BlockSpec((2, depth, lanes), lambda i, p: (i, 0, 0))],
+            out_specs=pl.BlockSpec((2, count, 2 * lanes), lambda i, p: (0, 0, i)),
+            scratch_shapes=[pltpu.VMEM((2 * count, depth), jnp.bfloat16)],
         ),
         name="merge",
-    )(place, mine, other, own, *parts)
-
-
-BACK_BY = (0, 1, 3, 2)
-
-
-def place_kernel(place, got, out):
+    )(place, mine, other, weights)
+
+
+def place_kernel(got, out):
     cores, cols, _, wide = got.shape
-    rows = len(BACK_BY)
+    rows = out.shape[1] // (cores * cols * 128)
     lanes = wide // rows
     for at_core in range(cores):
         for at_col in range(cols):
-            for index, back_by in enumerate(BACK_BY):
-                at = ((((place[0] + rows - back_by) % rows) * cols + at_col) * cores + at_core) * lanes
-                out[:, pl.ds(pl.multiple_of(at, lanes), lanes)] = got[
-                    at_core, at_col, :, index * lanes:(index + 1) * lanes]
-
-
-def place_columns(place, got):
+            for at_row in range(rows):
+                at = ((at_row * cols + at_col) * cores + at_core) * lanes
+                out[:, at:at + lanes] = got[at_core, at_col, :, at_row * lanes:(at_row + 1) * lanes]
+
+
+def place_columns(got):
     cores, cols, count, wide = got.shape
     return pl.pallas_call(
         place_kernel,
         out_shape=jax.ShapeDtypeStruct((count, cores * cols * wide), jnp.bfloat16),
-        grid_spec=pltpu.PrefetchScalarGridSpec(
-            num_scalar_prefetch=1, grid=(1,), in_specs=[whole(got.shape)],
-            out_specs=whole((count, cores * cols * wide))),
+        grid=(1,), in_specs=[whole(got.shape)],
+        out_specs=whole((count, cores * cols * wide)),
         name="place_columns",
-    )(place, got)
+    )(got)
 
 
 def block_step(tokens, segment_ids, w_qkv, w_out, w_merge, gain_attn, gain_merge):
-    rows, cols, planes = lax.axis_size("y"), lax.axis_size("x"), lax.axis_size("z")
+    rows, cols = lax.axis_size("y"), lax.axis_size("x")
     row, col, core = lax.axis_index("y"), lax.axis_index("x"), lax.axis_index("c")
-    parity = lax.axis_index("z") % 2
     tok_local = tokens.shape[0]
     groups = tok_local // 4
     row_count = cols * tok_local
     half = D // 2
     wide = w_qkv.shape[1]
-    place = jnp.stack([row, core, col, parity]).astype(jnp.int32)
+    lanes = w_merge.shape[1] // 2
+    all_merge = lax.all_gather(lax.dynamic_slice_in_dim(w_merge, core * lanes, lanes, 1), "y", axis=0)
+    place = jnp.stack([row, core, col]).astype(jnp.int32)
     segments = segment_ids.reshape(rows * cols, groups, 4).transpose(0, 2, 1).reshape(-1)
     layout = attention_inputs(segments, segment_ids)
     row_tokens = lax.all_to_all(
@@ -307,11 +302,6 @@
     ahead = [shift_rows(own, step, rows) for step in (3, 2, 1)]
     other_qkv = swap_cores(jnp.stack([part[:wide] for part in ahead]))
 
-    piece = (w_merge.shape[0] // 2, w_merge.shape[1] // 2)
-    own_piece = lax.dynamic_slice(w_merge, (parity * piece[0], core * piece[1]), piece)
-    first_y = shift_rows(own_piece, 1, rows)
-    third_y = shift_rows(own_piece, 3, rows)
-
     qkv = project_qkv(
         place, row_tokens, gain_attn, weights, ahead, other_qkv, rows)
     by_head = lax.all_to_all(qkv, "y", split_axis=0, concat_axis=0, tiled=True)
@@ -319,26 +309,20 @@
     out_rows = jnp.stack([own[wide:]] + [part[wide:] for part in ahead])
     next_out = shift_cols(out_rows, 1, cols)
     out_parts = [out_rows, next_out] + [shift_cols(out_rows, step, cols) for step in (2, 3)]
-    first_z = shift_planes(first_y, 1, planes)
-    third_z = shift_planes(third_y, planes - 1, planes)
-    second_y = shift_rows(own_piece, 2, rows)
-
     attended = attention(by_head, layout, cols)
     back = lax.all_to_all(
         attended.reshape(rows * cols, HEAD_DIM, row_count), ("y", "x"),
         split_axis=0, concat_axis=0, tiled=True)
-    second_z = shift_planes(second_y, 1, planes)
     mine_out = jnp.stack(out_parts)
     other_out = swap_cores(mine_out)
     merged = merge_rows(
         place, back, row_tokens, mine_out, other_out, gain_merge)
     merged = merged.reshape(4, cols * groups, D)
     other_merged = swap_cores(merged)
-    block = merge(
-        place, merged, other_merged, w_merge, (first_y, first_z, third_y, third_z, second_y, second_z))
+    block = merge(place, merged, other_merged, all_merge)
     got = lax.all_to_all(
         block.reshape(2 * cols, groups, block.shape[2]), ("c", "x"), split_axis=0, concat_axis=0, tiled=True)
-    return place_columns(place, got.reshape(2, cols, groups, block.shape[2]))
+    return place_columns(got.reshape(2, cols, groups, block.shape[2]))
 
 
 def solution(mesh):

time: 195 us -> 169 us (0.87)
  the two profiles are of different devices: /device:TPU:17 before, /device:TPU:321 now
where the time goes in v4:
time: 169 us; the launch traced here: 168 us
  starting transfers between devices  46.8 us (28%)
  waiting for transfers between devices  42.8 us (25%)
  Pallas kernels  37.8 us (22%)
  between operations  13.6 us (8%)
  blocking collectives  10.7 us (6%)
  local copies, waits for them, and re-layouts  9.7 us (6%)
  other arithmetic  6.75 us (4%)
    all_to_all x1, waiting for transfers between devices, block_step(): lax.all_to_all(attended.reshape(rows * cols, HEAD_DIM, row_count), ('y',...  20.9 us
    pallas_call x1, Pallas kernels, attention(): pl.pallas_call(attention_kernel, out_shape=jax.ShapeDtypeStruct((tiles, c...  13.7 us
    ppermute x3, waiting for transfers between devices, shift_rows(): lax.ppermute(value, 'y', [(at, (at + step) % rows) for at in range(rows)])  11.9 us
    ppermute x3, starting transfers between devices, shift_rows(): lax.ppermute(value, 'y', [(at, (at + step) % rows) for at in range(rows)])  10.7 us
    all_to_all x1, blocking collectives, block_step(): lax.all_to_all(block.reshape(2 * cols, groups, block.shape[2]), ('c', 'x'...  10.7 us
    ppermute x3, starting transfers between devices, shift_cols(): lax.ppermute(value, 'x', [(at, (at + step) % cols) for at in range(cols)])  10.6 us
    ppermute x3, starting transfers between devices, swap_cores(): return lax.ppermute(value, 'c', [(0, 1), (1, 0)])  8.98 us
    pallas_call x1, Pallas kernels, merge_rows(): pl.pallas_call(hidden_kernel, out_shape=jax.ShapeDtypeStruct((4, cols, co...  7.93 us
  transfers between devices with their start and end apart: 13, of which 7 were waited for; matrix products, arithmetic and copies ran while one was open for 8% of the time, Pallas kernels for 18%

profile of v4, /device:TPU:321, one launch (start us, length us, event | category | flops | bytes accessed | tf_op | source)
XLA Modules:
  0.0 168.2 jit_solution(13733151122878179140)
XLA Ops:
  6.5 0.0 copy-start
  6.5 0.0 all-gather.3.cloned.1.call-start
  6.5 1.7 %copy-done = bf16[5120,256]{1,0:T(8,128)(2,1)S(1)} copy-done((bf16[5120,256]{1,0:T(8,128)(2,1)S(1)}, bf16[5120,256]{1,0:T(8,128)(2,1)}, u32[]{:S(2)}) %copy-start) | copy-done | bytes 2621464
  8.3 0.0 copy-start.4
  8.3 0.0 copy-start.3
  8.3 1.2 constant_dynamic-slice_fusion
  9.5 0.0 all-gather.3.cloned.1.call-update
  9.5 0.0 copy-done.4
  9.6 0.4 copy-done.3
  9.9 0.8 pad_maximum_fusion.2
  10.7 3.2 %collective-permute-start.2 = (bf16[320,640]{1,0:T(8,128)(2,1)}, bf16[320,640]{1,0:T(8,128)(2,1)S(1)}, u32[]{:S(2)}, u32[]{:S(2)}) collective-permute-start(bf16[320,640]{1,0:T(8,128)(2,1)} %pad_maximum_fusion.2), channel_id=1, source_target_pairs={{0,4},{4,8},{8,12},{12,0},{1,5},{5,9},{9,13},{13,1},{2,6},{6,10},{... | collective-permute-start | bytes 1228808 | tf_op jit(solution)/shard_map/ppermute | solution.py:30
  13.9 4.5 %collective-permute-start.1 = (bf16[320,640]{1,0:T(8,128)(2,1)}, bf16[320,640]{1,0:T(8,128)(2,1)S(1)}, u32[]{:S(2)}, u32[]{:S(2)}) collective-permute-start(bf16[320,640]{1,0:T(8,128)(2,1)} %pad_maximum_fusion.2), channel_id=1, source_target_pairs={{0,8},{4,12},{8,0},{12,4},{1,9},{5,13},{9,1},{13,5},{2,10},{6,14},... | collective-permute-start | bytes 1228808 | tf_op jit(solution)/shard_map/ppermute | solution.py:30
  18.5 3.0 %collective-permute-start = (bf16[320,640]{1,0:T(8,128)(2,1)}, bf16[320,640]{1,0:T(8,128)(2,1)}, u32[]{:S(2)}, u32[]{:S(2)}) collective-permute-start(bf16[320,640]{1,0:T(8,128)(2,1)} %pad_maximum_fusion.2), channel_id=1, source_target_pairs={{0,12},{4,0},{8,4},{12,8},{1,13},{5,1},{9,5},{13,9},{2,14},{6,2},{... | collective-permute-start | bytes 1228808 | tf_op jit(solution)/shard_map/ppermute | solution.py:30
  21.5 2.4 %spread.1 = bf16[4,128,1280]{2,1,0:T(8,128)(2,1)} custom-call(bf16[128,1280]{1,0:T(8,128)(2,1)} %tokens.1), custom_call_target="tpu_custom_call" | custom-call | tf_op jit(solution)/shard_map/spread/pallas_call | solution.py:141
  23.8 4.3 %all-to-all-start = ((bf16[4,128,1280]{2,1,0:T(8,128)(2,1)}), bf16[4,128,1280]{2,1,0:T(8,128)(2,1)}, u32[]{:S(2)}, u32[]{:S(2)}) async-start(bf16[4,128,1280]{2,1,0:T(8,128)(2,1)} %spread.1), calls=%async_computation | async-start | bytes 2621440 | tf_op jit(solution)/shard_map/all_to_all | solution.py:295
  28.1 0.9 fusion.1
  29.1 0.0 collective-permute-done.2.third
  29.1 0.0 copy-start.1
  29.1 6.4 %collective-permute-done.1.second = bf16[320,640]{1,0:T(8,128)(2,1)S(1)} collective-permute-done((bf16[320,640]{1,0:T(8,128)(2,1)}, bf16[320,640]{1,0:T(8,128)(2,1)S(1)}, u32[]{:S(2)}, u32[]{:S(2)}) %collective-permute-start.1) | collective-permute-done | bytes 409632 | tf_op jit(solution)/shard_map/ppermute | solution.py:30
  35.6 0.0 copy-start.2
  35.6 5.4 %collective-permute-done.first = bf16[320,640]{1,0:T(8,128)(2,1)} collective-permute-done((bf16[320,640]{1,0:T(8,128)(2,1)}, bf16[320,640]{1,0:T(8,128)(2,1)}, u32[]{:S(2)}, u32[]{:S(2)}) %collective-permute-start) | collective-permute-done | bytes 409632 | tf_op jit(solution)/shard_map/ppermute | solution.py:30
  41.0 1.0 slice_bitcast_fusion.2
  42.0 1.1 pad_maximum_fusion.1
  43.2 4.0 %collective-permute-start.3 = (bf16[3,240,640]{2,1,0:T(8,128)(2,1)}, bf16[3,240,640]{2,1,0:T(8,128)(2,1)}, u32[]{:S(2)}, u32[]{:S(2)}) collective-permute-start(bf16[3,240,640]{2,1,0:T(8,128)(2,1)} %pad_maximum_fusion.1), channel_id=1, source_target_pairs={{0,16},{16,0},{1,17},{17,1},{2,18},{18,2},{3,19},{19,3},{4,20},{20... | collective-permute-start | bytes 2764808 | tf_op jit(solution)/shard_map/ppermute | solution.py:26
  47.2 0.0 copy-done.1
  47.2 0.0 copy-done.2
  47.2 0.9 slice_bitcast_fusion.5
  48.2 0.9 fusion
  49.0 3.1 %collective-permute-start.4 = (bf16[4,80,640]{2,1,0:T(8,128)(2,1)}, bf16[4,80,640]{2,1,0:T(8,128)(2,1)S(1)}, u32[]{:S(2)}, u32[]{:S(2)}) collective-permute-start(bf16[4,80,640]{2,1,0:T(8,128)(2,1)} %get-tuple-element.10), channel_id=1, source_target_pairs={{0,1},{1,2},{2,3},{3,0},{4,5},{5,6},{6,7},{7,4},{8,9},{9,10},{10,1... | collective-permute-start | bytes 1228808 | tf_op jit(solution)/shard_map/ppermute | solution.py:116
  52.1 4.4 %collective-permute-start.5 = (bf16[4,80,640]{2,1,0:T(8,128)(2,1)}, bf16[4,80,640]{2,1,0:T(8,128)(2,1)}, u32[]{:S(2)}, u32[]{:S(2)}) collective-permute-start(bf16[4,80,640]{2,1,0:T(8,128)(2,1)} %get-tuple-element.10), channel_id=1, source_target_pairs={{0,2},{1,3},{2,0},{3,1},{4,6},{5,7},{6,4},{7,5},{8,10},{9,11},{10,... | collective-permute-start | bytes 1228808 | tf_op jit(solution)/shard_map/ppermute | solution.py:116
  56.6 3.0 %collective-permute-start.6 = (bf16[4,80,640]{2,1,0:T(8,128)(2,1)}, bf16[4,80,640]{2,1,0:T(8,128)(2,1)}, u32[]{:S(2)}, u32[]{:S(2)}) collective-permute-start(bf16[4,80,640]{2,1,0:T(8,128)(2,1)} %get-tuple-element.10), channel_id=1, source_target_pairs={{0,3},{1,0},{2,1},{3,2},{4,7},{5,4},{6,5},{7,6},{8,11},{9,8},{10,9... | collective-permute-start | bytes 1228808 | tf_op jit(solution)/shard_map/ppermute | solution.py:116
  59.6 0.6 pad_add_fusion.1.place
  60.2 0.0 all-to-all-done.tokens.residual
  60.2 0.0 collective-permute-done.3.other
  60.2 6.4 %project_qkv.1 = bf16[4,240,512]{2,1,0:T(8,128)(2,1)} custom-call(s32[3]{0:T(128)} %pad_add_fusion.1.place, bf16[4,128,1280]{2,1,0:T(8,128)(2,1)} %all-to-all-done.tokens.residual, f32[1280]{0:T(1024)} %gain.2, bf16[240,1280]{1,0:T(8,128)(2,1)} %bitcast.37, bf16[320,640]{1,0:T(8,128)(2,1)} %collective-permute-done.first, bf16[320,640]{1,0:T(8,128)(2,1)} %copy-done.2, ...), custom_call_target="tpu_custom_call" | custom-call | tf_op jit(solution)/shard_map/project_qkv/pallas_call | solution.py:170
  66.6 4.6 %all-to-all-start.1 = ((bf16[4,240,512]{2,1,0:T(8,128)(2,1)}), bf16[4,240,512]{2,1,0:T(8,128)(2,1)}, u32[]{:S(2)}, u32[]{:S(2)}) async-start(bf16[4,240,512]{2,1,0:T(8,128)(2,1)} %project_qkv.1), calls=%async_computation.1 | async-start | bytes 1966080 | tf_op jit(solution)/shard_map/all_to_all | solution.py:307
  71.2 0.0 collective-permute-done.4
  71.2 2.0 %collective-permute-done.5 = bf16[4,80,640]{2,1,0:T(8,128)(2,1)} collective-permute-done((bf16[4,80,640]{2,1,0:T(8,128)(2,1)}, bf16[4,80,640]{2,1,0:T(8,128)(2,1)}, u32[]{:S(2)}, u32[]{:S(2)}) %collective-permute-start.5) | collective-permute-done | bytes 409632 | tf_op jit(solution)/shard_map/ppermute | solution.py:116
  73.3 1.2 collective-permute-done.6
  74.5 0.0 copy-start.5
  74.5 2.6 %pad_maximum_fusion.mine = bf16[4,4,80,640]{3,2,1,0:T(8,128)(2,1)} fusion(bf16[1,4,80,640]{3,2,1,0:T(8,128)(2,1)} %bitcast.19, bf16[1,4,80,640]{3,2,1,0:T(8,128)(2,1)} %bitcast.18, bf16[1,4,80,640]{3,2,1,0:T(8,128)(2,1)S(1)} %bitcast.41, bf16[1,4,80,640]{3,2,1,0:T(8,128)(2,1)S(1)} %get-tuple-element.9), kind=kLoop, calls=%fused_computation | loop fusion | flops 2457600 | bytes 3276800 | tf_op jit(solution)/shard_map/stack | solution.py:316
  77.0 3.0 %collective-permute-start.7 = (bf16[4,4,80,640]{3,2,1,0:T(8,128)(2,1)}, bf16[4,4,80,640]{3,2,1,0:T(8,128)(2,1)}, u32[]{:S(2)}, u32[]{:S(2)}) collective-permute-start(bf16[4,4,80,640]{3,2,1,0:T(8,128)(2,1)} %pad_maximum_fusion.mine), channel_id=1, source_target_pairs={{0,16},{16,0},{1,17},{17,1},{2,18},{18,2},{3,19},{19,3},{4,20},{20... | collective-permute-start | bytes 4915208 | tf_op jit(solution)/shard_map/ppermute | solution.py:26
  80.1 0.0 copy-done.5
  80.1 0.3 reshape.22
  80.4 0.2 copy.14
  80.5 2.1 %broadcast_in_dim_reshape.8.seg_col = s32[2048,1]{1,0:T(8,128)} reshape(s32[16,4,32]{2,1,0:T(4,128)S(1)} %copy.14) | data formatting | bytes 16384 | tf_op jit(solution)/shard_map/broadcast_in_dim;reshape | solution.py:89
  82.7 0.7 broadcast_in_dim_reshape.7.seg_row
  83.4 0.2 slice_reduce_fusion.1
  83.5 0.2 convert_reduce_fusion.1
  83.8 0.6 pad_add_fusion.bounds
  84.4 3.5 %all-to-all-done.1.qkv = bf16[4,240,512]{2,1,0:T(8,128)(2,1)} async-done(((bf16[4,240,512]{2,1,0:T(8,128)(2,1)}), bf16[4,240,512]{2,1,0:T(8,128)(2,1)}, u32[]{:S(2)}, u32[]{:S(2)}) %all-to-all-start.1) | async-done | bytes 983072 | tf_op jit(solution)/shard_map/all_to_all | solution.py:307
  87.8 13.7 %attention.1 = bf16[4,4,80,512]{3,2,1,0:T(8,128)(2,1)} custom-call(s32[2,4]{1,0:T(2,128)} %pad_add_fusion.bounds, bf16[4,240,512]{2,1,0:T(8,128)(2,1)} %all-to-all-done.1.qkv, s32[2048,1]{1,0:T(8,128)} %broadcast_in_dim_reshape.8.seg_col, s32[1,2048]{1,0:T(1,128)} %broadcast_in_dim_reshape.7.seg_row), custom_call_target="tpu_custom_call" | custom-call | tf_op jit(solution)/shard_map/attention/pallas_call | solution.py:97
  101.5 7.7 %all-to-all-start.2 = ((bf16[16,80,512]{2,1,0:T(8,128)(2,1)}), bf16[16,80,512]{2,1,0:T(8,128)(2,1)}, u32[]{:S(2)}, u32[]{:S(2)}) async-start(bf16[16,80,512]{2,1,0:T(8,128)(2,1)} %bitcast.35), calls=%async_computation.2 | async-start | bytes 2621440 | tf_op jit(solution)/shard_map/all_to_all | solution.py:313
  109.2 0.0 collective-permute-done.7.other
  109.2 20.9 %all-to-all-done.2.back = bf16[16,80,512]{2,1,0:T(8,128)(2,1)} async-done(((bf16[16,80,512]{2,1,0:T(8,128)(2,1)}), bf16[16,80,512]{2,1,0:T(8,128)(2,1)}, u32[]{:S(2)}, u32[]{:S(2)}) %all-to-all-start.2) | async-done | bytes 1310752 | tf_op jit(solution)/shard_map/all_to_all | solution.py:313
  130.1 7.9 %merge_rows.1 = bf16[4,4,32,1280]{3,2,1,0:T(8,128)(2,1)} custom-call(s32[3]{0:T(128)} %pad_add_fusion.1.place, bf16[16,80,512]{2,1,0:T(8,128)(2,1)} %all-to-all-done.2.back, bf16[4,128,1280]{2,1,0:T(8,128)(2,1)} %all-to-all-done.tokens.residual, bf16[4,4,80,640]{3,2,1,0:T(8,128)(2,1)} %pad_maximum_fusion.mine, ...), custom_call_target="tpu_custom_call" | custom-call | tf_op jit(solution)/shard_map/merge_rows/pallas_call | solution.py:208
  138.0 1.9 %collective-permute-start.8 = (bf16[4,128,1280]{2,1,0:T(8,128)(2,1)}, bf16[4,128,1280]{2,1,0:T(8,128)(2,1)}, u32[]{:S(2)}, u32[]{:S(2)}) collective-permute-start(bf16[4,128,1280]{2,1,0:T(8,128)(2,1)} %bitcast.33), channel_id=1, source_target_pairs={{0,16},{16,0},{1,17},{17,1},{2,18},{18,2},{3,19},{19,3},{4,20},{20... | collective-permute-start | bytes 3932168 | tf_op jit(solution)/shard_map/ppermute | solution.py:26
  139.9 3.3 %collective-permute-done.8.other = bf16[4,128,1280]{2,1,0:T(8,128)(2,1)} collective-permute-done((bf16[4,128,1280]{2,1,0:T(8,128)(2,1)}, bf16[4,128,1280]{2,1,0:T(8,128)(2,1)}, u32[]{:S(2)}, u32[]{:S(2)}) %collective-permute-start.8) | collective-permute-done | bytes 1310752 | tf_op jit(solution)/shard_map/ppermute | solution.py:26
  143.2 0.0 all-gather.3.cloned.1.call-done
  143.2 5.7 %merge.1 = bf16[2,128,512]{2,1,0:T(8,128)(2,1)} custom-call(s32[3]{0:T(128)} %pad_add_fusion.1.place, bf16[4,128,1280]{2,1,0:T(8,128)(2,1)} %bitcast.34, bf16[4,128,1280]{2,1,0:T(8,128)(2,1)} %collective-permute-done.8.other, bf16[4,5120,128]{2,1,0:T(8,128)(2,1)} %bitcast.36), custom_call_target="tpu_custom_call" | custom-call | tf_op jit(solution)/shard_map/merge/pallas_call | solution.py:245
  149.0 10.7 %all_to_all.20 = bf16[8,32,512]{2,1,0:T(8,128)(2,1)} all-to-all(bf16[8,32,512]{2,1,0:T(8,128)(2,1)} %bitcast.38), channel_id=1, replica_groups=mesh['z'=16,'c'=2,'y'=4,'x'=4] {'c','x'}, dimensions={0} | all-to-all | bytes 524288 | tf_op jit(solution)/shard_map/all_to_all | solution.py:323
  159.6 1.7 %place_columns.1 = bf16[32,4096]{1,0:T(8,128)(2,1)} custom-call(bf16[2,4,32,512]{3,2,1,0:T(8,128)(2,1)} %bitcast.39), custom_call_target="tpu_custom_call" | custom-call | tf_op jit(solution)/shard_map/place_columns/pallas_call | solution.py:273
  (7 shorter events, 0.1 us)
Async XLA Ops:
  6.5 1.7 %copy-start = (bf16[5120,256]{1,0:T(8,128)(2,1)S(1)}, bf16[5120,256]{1,0:T(8,128)(2,1)}, u32[]{:S(2)}) copy-start(bf16[5120,256]{1,0:T(8,128)(2,1)} %param.11) | copy-start | bytes 7864324
  6.5 136.7 %all-gather.3.cloned.1.call-start = ((), (), s32[]{:S(2)}) async-start(), calls=%async_computation.4 | async-start | bytes 6553600 | tf_op jit(solution)/shard_map/all_gather | solution.py:291
  8.3 1.2 copy-start.4
  8.3 1.6 copy-start.3
  10.7 18.3 %collective-permute-start.2 = (bf16[320,640]{1,0:T(8,128)(2,1)}, bf16[320,640]{1,0:T(8,128)(2,1)S(1)}, u32[]{:S(2)}, u32[]{:S(2)}) collective-permute-start(bf16[320,640]{1,0:T(8,128)(2,1)} %pad_maximum_fusion.2), channel_id=1, source_target_pairs={{0,4},{4,8},{8,12},{12,0},{1,5},{5,9},{9,13},{13,1},{2,6},{6,10},{... | collective-permute-start | bytes 1228808 | tf_op jit(solution)/shard_map/ppermute | solution.py:30
  13.9 21.6 %collective-permute-start.1 = (bf16[320,640]{1,0:T(8,128)(2,1)}, bf16[320,640]{1,0:T(8,128)(2,1)S(1)}, u32[]{:S(2)}, u32[]{:S(2)}) collective-permute-start(bf16[320,640]{1,0:T(8,128)(2,1)} %pad_maximum_fusion.2), channel_id=1, source_target_pairs={{0,8},{4,12},{8,0},{12,4},{1,9},{5,13},{9,1},{13,5},{2,10},{6,14},... | collective-permute-start | bytes 1228808 | tf_op jit(solution)/shard_map/ppermute | solution.py:30
  18.5 22.6 %collective-permute-start = (bf16[320,640]{1,0:T(8,128)(2,1)}, bf16[320,640]{1,0:T(8,128)(2,1)}, u32[]{:S(2)}, u32[]{:S(2)}) collective-permute-start(bf16[320,640]{1,0:T(8,128)(2,1)} %pad_maximum_fusion.2), channel_id=1, source_target_pairs={{0,12},{4,0},{8,4},{12,8},{1,13},{5,1},{9,5},{13,9},{2,14},{6,2},{... | collective-permute-start | bytes 1228808 | tf_op jit(solution)/shard_map/ppermute | solution.py:30
  23.8 36.4 %all-to-all-start = ((bf16[4,128,1280]{2,1,0:T(8,128)(2,1)}), bf16[4,128,1280]{2,1,0:T(8,128)(2,1)}, u32[]{:S(2)}, u32[]{:S(2)}) async-start(bf16[4,128,1280]{2,1,0:T(8,128)(2,1)} %spread.1), calls=%async_computation | async-start | bytes 2621440 | tf_op jit(solution)/shard_map/all_to_all | solution.py:295
  29.1 18.1 %copy-start.1 = (bf16[320,640]{1,0:T(8,128)(2,1)}, bf16[320,640]{1,0:T(8,128)(2,1)S(1)}, u32[]{:S(2)}) copy-start(bf16[320,640]{1,0:T(8,128)(2,1)S(1)} %collective-permute-done.2.third) | copy-start | bytes 1228804
  35.6 11.7 %copy-start.2 = (bf16[320,640]{1,0:T(8,128)(2,1)}, bf16[320,640]{1,0:T(8,128)(2,1)S(1)}, u32[]{:S(2)}) copy-start(bf16[320,640]{1,0:T(8,128)(2,1)S(1)} %collective-permute-done.1.second) | copy-start | bytes 1228804
  43.2 17.1 %collective-permute-start.3 = (bf16[3,240,640]{2,1,0:T(8,128)(2,1)}, bf16[3,240,640]{2,1,0:T(8,128)(2,1)}, u32[]{:S(2)}, u32[]{:S(2)}) collective-permute-start(bf16[3,240,640]{2,1,0:T(8,128)(2,1)} %pad_maximum_fusion.1), channel_id=1, source_target_pairs={{0,16},{16,0},{1,17},{17,1},{2,18},{18,2},{3,19},{19,3},{4,20},{20... | collective-permute-start | bytes 2764808 | tf_op jit(solution)/shard_map/ppermute | solution.py:26
  49.0 22.2 %collective-permute-start.4 = (bf16[4,80,640]{2,1,0:T(8,128)(2,1)}, bf16[4,80,640]{2,1,0:T(8,128)(2,1)S(1)}, u32[]{:S(2)}, u32[]{:S(2)}) collective-permute-start(bf16[4,80,640]{2,1,0:T(8,128)(2,1)} %get-tuple-element.10), channel_id=1, source_target_pairs={{0,1},{1,2},{2,3},{3,0},{4,5},{5,6},{6,7},{7,4},{8,9},{9,10},{10,1... | collective-permute-start | bytes 1228808 | tf_op jit(solution)/shard_map/ppermute | solution.py:116
  52.1 21.1 %collective-permute-start.5 = (bf16[4,80,640]{2,1,0:T(8,128)(2,1)}, bf16[4,80,640]{2,1,0:T(8,128)(2,1)}, u32[]{:S(2)}, u32[]{:S(2)}) collective-permute-start(bf16[4,80,640]{2,1,0:T(8,128)(2,1)} %get-tuple-element.10), channel_id=1, source_target_pairs={{0,2},{1,3},{2,0},{3,1},{4,6},{5,7},{6,4},{7,5},{8,10},{9,11},{10,... | collective-permute-start | bytes 1228808 | tf_op jit(solution)/shard_map/ppermute | solution.py:116
  56.6 17.9 %collective-permute-start.6 = (bf16[4,80,640]{2,1,0:T(8,128)(2,1)}, bf16[4,80,640]{2,1,0:T(8,128)(2,1)}, u32[]{:S(2)}, u32[]{:S(2)}) collective-permute-start(bf16[4,80,640]{2,1,0:T(8,128)(2,1)} %get-tuple-element.10), channel_id=1, source_target_pairs={{0,3},{1,0},{2,1},{3,2},{4,7},{5,4},{6,5},{7,6},{8,11},{9,8},{10,9... | collective-permute-start | bytes 1228808 | tf_op jit(solution)/shard_map/ppermute | solution.py:116
  66.6 21.2 %all-to-all-start.1 = ((bf16[4,240,512]{2,1,0:T(8,128)(2,1)}), bf16[4,240,512]{2,1,0:T(8,128)(2,1)}, u32[]{:S(2)}, u32[]{:S(2)}) async-start(bf16[4,240,512]{2,1,0:T(8,128)(2,1)} %project_qkv.1), calls=%async_computation.1 | async-start | bytes 1966080 | tf_op jit(solution)/shard_map/all_to_all | solution.py:307
  74.5 5.6 %copy-start.5 = (s32[2048]{0:T(1024)S(1)}, s32[2048]{0:T(1024)}, u32[]{:S(2)}) copy-start(s32[2048]{0:T(1024)} %param.8) | copy-start | bytes 24580
  77.0 32.1 %collective-permute-start.7 = (bf16[4,4,80,640]{3,2,1,0:T(8,128)(2,1)}, bf16[4,4,80,640]{3,2,1,0:T(8,128)(2,1)}, u32[]{:S(2)}, u32[]{:S(2)}) collective-permute-start(bf16[4,4,80,640]{3,2,1,0:T(8,128)(2,1)} %pad_maximum_fusion.mine), channel_id=1, source_target_pairs={{0,16},{16,0},{1,17},{17,1},{2,18},{18,2},{3,19},{19,3},{4,20},{20... | collective-permute-start | bytes 4915208 | tf_op jit(solution)/shard_map/ppermute | solution.py:26
  101.5 28.6 %all-to-all-start.2 = ((bf16[16,80,512]{2,1,0:T(8,128)(2,1)}), bf16[16,80,512]{2,1,0:T(8,128)(2,1)}, u32[]{:S(2)}, u32[]{:S(2)}) async-start(bf16[16,80,512]{2,1,0:T(8,128)(2,1)} %bitcast.35), calls=%async_computation.2 | async-start | bytes 2621440 | tf_op jit(solution)/shard_map/all_to_all | solution.py:313
  138.0 5.3 %collective-permute-start.8 = (bf16[4,128,1280]{2,1,0:T(8,128)(2,1)}, bf16[4,128,1280]{2,1,0:T(8,128)(2,1)}, u32[]{:S(2)}, u32[]{:S(2)}) collective-permute-start(bf16[4,128,1280]{2,1,0:T(8,128)(2,1)} %bitcast.33), channel_id=1, source_target_pairs={{0,16},{16,0},{1,17},{17,1},{2,18},{18,2},{3,19},{19,3},{4,20},{20... | collective-permute-start | bytes 3932168 | tf_op jit(solution)/shard_map/ppermute | solution.py:26
Sparse Core Ops, SparseCore 0:
  9.6 73.7 all-gather.2

commit v5 on v2

--- a/solution.py
+++ b/solution.py
@@ -202,9 +202,11 @@
         turned, other[...].reshape(D, half), 1, 0)
     total = residual[...].reshape(count, D).astype(jnp.float32) + hidden[...]
     value = layer_norm(total, gain[...]).astype(jnp.bfloat16)
-    group = count // 4
-    for spot in range(4):
-        out[spot, 0] = value[spot * group:(spot + 1) * group, :]
+    group = out.shape[2]
+    for index in range(out.shape[1]):
+        for spot in range(4):
+            at = (index * 4 + spot) * group
+            out[spot, index] = value[at:at + group, :]
 
 
 def merge_rows(place, back, row_tokens, mine, other, gain):
@@ -214,32 +216,37 @@
         out_shape=jax.ShapeDtypeStruct((4, cols, count // 4, D), jnp.bfloat16),
         grid_spec=pltpu.PrefetchScalarGridSpec(
             num_scalar_prefetch=1,
-            grid=(cols,),
+            grid=(cols // 2,),
             in_specs=[
-                pl.BlockSpec((HEADS, HEAD_DIM, count), lambda i, p: (0, 0, i)),
-                pl.BlockSpec((1, count, D), lambda i, p: (i, 0, 0)),
+                pl.BlockSpec((HEADS, HEAD_DIM, 2 * count), lambda i, p: (0, 0, i)),
+                pl.BlockSpec((2, count, D), lambda i, p: (i, 0, 0)),
                 whole(mine.shape), whole(other.shape), whole((D,)),
             ],
-            out_specs=pl.BlockSpec((4, 1, count // 4, D), lambda i, p: (0, i, 0, 0)),
-            scratch_shapes=[pltpu.VMEM((D, count), jnp.bfloat16), pltpu.VMEM((count, D), jnp.float32)],
+            out_specs=pl.BlockSpec((4, 2, count // 4, D), lambda i, p: (0, i, 0, 0)),
+            scratch_shapes=[pltpu.VMEM((D, 2 * count), jnp.bfloat16), pltpu.VMEM((2 * count, D), jnp.float32)],
         ),
         name="merge_rows",
     )(place, back, row_tokens, mine, other, gain)
 
 
 def merge_kernel(place, mine, other, own, *rest):
-    parts, out = rest[:-1], rest[-1]
+    parts, out, near, far = rest[:-3], rest[-3], rest[-2], rest[-1]
     core, parity = place[1], place[3]
     lanes = parts[0].shape[1]
-    column = pl.multiple_of(core * lanes, lanes)
-    for source, target in ((mine, core), (other, 1 - core)):
-        near = jnp.concatenate([source[parity * 2], source[parity * 2 + 1]], axis=1)
-        far = jnp.concatenate([source[2 - parity * 2], source[3 - parity * 2]], axis=1)
-        flat = jnp.concatenate([source[spot] for spot in range(4)], axis=1)
-        out[target, :, 0:lanes] = matmul(flat, own[:, pl.ds(column, lanes)], 1, 0).astype(jnp.bfloat16)
-        for block in range(len(parts) // 2):
-            total = matmul(near, parts[2 * block][...], 1, 0) + matmul(far, parts[2 * block + 1][...], 1, 0)
-            out[target, :, (block + 1) * lanes:(block + 2) * lanes] = total.astype(jnp.bfloat16)
+    count, depth = mine.shape[1], 2 * D
+    for index, source in enumerate((mine, other)):
+        for spot in range(2):
+            at = (slice(index * count, (index + 1) * count), slice(spot * D, (spot + 1) * D))
+            near[at] = source[parity * 2 + spot]
+            far[at] = source[2 - parity * 2 + spot]
+    column = pl.ds(pl.multiple_of(core * lanes, lanes), lanes)
+    near_own = own[pl.ds(pl.multiple_of(parity * depth, depth), depth), column]
+    far_own = own[pl.ds(pl.multiple_of((1 - parity) * depth, depth), depth), column]
+    near_wide = jnp.concatenate([near_own] + [part[...] for part in parts[0::2]], axis=1)
+    far_wide = jnp.concatenate([far_own] + [part[...] for part in parts[1::2]], axis=1)
+    value = matmul(near[...], near_wide, 1, 0) + matmul(far[...], far_wide, 1, 0)
+    out[core] = value[0:count, :].astype(jnp.bfloat16)
+    out[1 - core] = value[count:2 * count, :].astype(jnp.bfloat16)
 
 
 def merge(place, mine, other, own, parts):
@@ -253,6 +260,7 @@
             in_specs=[whole(mine.shape), whole(other.shape), whole(own.shape)]
             + [whole(part.shape) for part in parts],
             out_specs=whole((2, mine.shape[1], width)),
+            scratch_shapes=[pltpu.VMEM((2 * mine.shape[1], 2 * D), jnp.bfloat16)] * 2,
         ),
         name="merge",
     )(place, mine, other, own, *parts)
@@ -321,7 +329,7 @@
     out_parts = [out_rows, next_out] + [shift_cols(out_rows, step, cols) for step in (2, 3)]
     first_z = shift_planes(first_y, 1, planes)
     third_z = shift_planes(third_y, planes - 1, planes)
-    second_y = shift_rows(own_piece, 2, rows)
+    second_y = shift_rows(first_y, 1, rows)
 
     attended = attention(by_head, layout, cols)
     back = lax.all_to_all(

time: 195 us -> 195 us (level)
  the two profiles are of different devices: /device:TPU:17 before, /device:TPU:1 now
where the time goes in v5:
time: 195 us; the launch traced here: 194 us
  starting transfers between devices  66.3 us (34%)
  waiting for transfers between devices  62.2 us (32%)
  Pallas kernels  36.2 us (19%)
  local copies, waits for them, and re-layouts  12.5 us (6%)
  blocking collectives  11.4 us (6%)
  other arithmetic  4.95 us (3%)
    ppermute x6, waiting for transfers between devices, shift_rows(): lax.ppermute(value, 'y', [(at, (at + step) % rows) for at in range(rows)])  30 us
    ppermute x3, waiting for transfers between devices, shift_planes(): lax.ppermute(value, 'z', [(at, (at + step) % planes) for at in range(plan...  25.5 us
    ppermute x6, starting transfers between devices, shift_rows(): lax.ppermute(value, 'y', [(at, (at + step) % rows) for at in range(rows)])  19.9 us
    ppermute x3, starting transfers between devices, shift_planes(): lax.ppermute(value, 'z', [(at, (at + step) % planes) for at in range(plan...  15 us
    all_to_all x1, blocking collectives, block_step(): lax.all_to_all(block.reshape(2 * cols, groups, block.shape[2]), ('c', 'x'...  11.4 us
    pallas_call x1, Pallas kernels, attention(): pl.pallas_call(attention_kernel, out_shape=jax.ShapeDtypeStruct((tiles, c...  11.3 us
    ppermute x3, starting transfers between devices, swap_cores(): return lax.ppermute(value, 'c', [(0, 1), (1, 0)])  9.48 us
    ppermute x3, starting transfers between devices, shift_cols(): lax.ppermute(value, 'x', [(at, (at + step) % cols) for at in range(cols)])  9.32 us
  transfers between devices with their start and end apart: 18, of which 7 were waited for; matrix products, arithmetic and copies ran while one was open for 5% of the time, Pallas kernels for 14%

profile of v5, /device:TPU:1, one launch (start us, length us, event | category | flops | bytes accessed | tf_op | source)
XLA Modules:
  0.0 193.8 jit_solution(16832738002280370120)
XLA Ops:
  0.0 0.9 copy-done
  0.9 1.0 dynamic-slice_bitcast_fusion
  2.0 4.0 %collective-permute-start.2 = (bf16[320,640]{1,0:T(8,128)(2,1)S(1)}, bf16[320,640]{1,0:T(8,128)(2,1)S(1)}, u32[]{:S(2)}, u32[]{:S(2)}) collective-permute-start(bf16[320,640]{1,0:T(8,128)(2,1)S(1)} %pad_maximum_fusion.2), channel_id=1, source_target_pairs={{0,4},{4,8},{8,12},{12,0},{1,5},{5,9},{9,13},{13,1},{2,6},{6,10},{... | collective-permute-start | bytes 1228808 | tf_op jit(solution)/shard_map/ppermute | solution.py:30
  6.0 4.5 %collective-permute-start.1 = (bf16[320,640]{1,0:T(8,128)(2,1)S(1)}, bf16[320,640]{1,0:T(8,128)(2,1)S(1)}, u32[]{:S(2)}, u32[]{:S(2)}) collective-permute-start(bf16[320,640]{1,0:T(8,128)(2,1)S(1)} %pad_maximum_fusion.2), channel_id=1, source_target_pairs={{0,8},{4,12},{8,0},{12,4},{1,9},{5,13},{9,1},{13,5},{2,10},{6,14},... | collective-permute-start | bytes 1228808 | tf_op jit(solution)/shard_map/ppermute | solution.py:30
  10.6 3.0 %collective-permute-start = (bf16[320,640]{1,0:T(8,128)(2,1)S(1)}, bf16[320,640]{1,0:T(8,128)(2,1)S(1)}, u32[]{:S(2)}, u32[]{:S(2)}) collective-permute-start(bf16[320,640]{1,0:T(8,128)(2,1)S(1)} %pad_maximum_fusion.2), channel_id=1, source_target_pairs={{0,12},{4,0},{8,4},{12,8},{1,13},{5,1},{9,5},{13,9},{2,14},{6,2},{... | collective-permute-start | bytes 1228808 | tf_op jit(solution)/shard_map/ppermute | solution.py:30
  13.5 2.3 %spread.1 = bf16[4,128,1280]{2,1,0:T(8,128)(2,1)} custom-call(bf16[128,1280]{1,0:T(8,128)(2,1)} %tokens.1), custom_call_target="tpu_custom_call" | custom-call | tf_op jit(solution)/shard_map/spread/pallas_call | solution.py:145
  15.9 4.0 %all-to-all-start = ((bf16[4,128,1280]{2,1,0:T(8,128)(2,1)}), bf16[4,128,1280]{2,1,0:T(8,128)(2,1)S(1)}, u32[]{:S(2)}, u32[]{:S(2)}) async-start(bf16[4,128,1280]{2,1,0:T(8,128)(2,1)} %spread.1), calls=%async_computation | async-start | bytes 2621440 | tf_op jit(solution)/shard_map/all_to_all | solution.py:308
  19.9 0.0 collective-permute-done.2.third
  20.0 6.4 %collective-permute-done.1.second = bf16[320,640]{1,0:T(8,128)(2,1)S(1)} collective-permute-done((bf16[320,640]{1,0:T(8,128)(2,1)S(1)}, bf16[320,640]{1,0:T(8,128)(2,1)S(1)}, u32[]{:S(2)}, u32[]{:S(2)}) %collective-permute-start.1) | collective-permute-done | bytes 409632 | tf_op jit(solution)/shard_map/ppermute | solution.py:30
  26.4 0.0 collective-permute-done.first
  26.4 1.2 pad_maximum_fusion.1
  27.6 4.6 %collective-permute-start.3 = (bf16[3,240,640]{2,1,0:T(8,128)(2,1)}, bf16[3,240,640]{2,1,0:T(8,128)(2,1)}, u32[]{:S(2)}, u32[]{:S(2)}) collective-permute-start(bf16[3,240,640]{2,1,0:T(8,128)(2,1)} %pad_maximum_fusion.1), channel_id=1, source_target_pairs={{0,16},{16,0},{1,17},{17,1},{2,18},{18,2},{3,19},{19,3},{4,20},{20... | collective-permute-start | bytes 2764808 | tf_op jit(solution)/shard_map/ppermute | solution.py:26
  32.3 0.8 fusion
  33.1 4.4 %collective-permute-start.6 = (bf16[4,80,640]{2,1,0:T(8,128)(2,1)}, bf16[4,80,640]{2,1,0:T(8,128)(2,1)}, u32[]{:S(2)}, u32[]{:S(2)}) collective-permute-start(bf16[4,80,640]{2,1,0:T(8,128)(2,1)} %get-tuple-element.10), channel_id=1, source_target_pairs={{0,3},{1,0},{2,1},{3,2},{4,7},{5,4},{6,5},{7,6},{8,11},{9,8},{10,9... | collective-permute-start | bytes 1228808 | tf_op jit(solution)/shard_map/ppermute | solution.py:116
  37.5 2.4 %collective-permute-start.5 = (bf16[4,80,640]{2,1,0:T(8,128)(2,1)}, bf16[4,80,640]{2,1,0:T(8,128)(2,1)}, u32[]{:S(2)}, u32[]{:S(2)}) collective-permute-start(bf16[4,80,640]{2,1,0:T(8,128)(2,1)} %get-tuple-element.10), channel_id=1, source_target_pairs={{0,2},{1,3},{2,0},{3,1},{4,6},{5,7},{6,4},{7,5},{8,10},{9,11},{10,... | collective-permute-start | bytes 1228808 | tf_op jit(solution)/shard_map/ppermute | solution.py:116
  39.9 2.5 %collective-permute-start.4 = (bf16[4,80,640]{2,1,0:T(8,128)(2,1)}, bf16[4,80,640]{2,1,0:T(8,128)(2,1)}, u32[]{:S(2)}, u32[]{:S(2)}) collective-permute-start(bf16[4,80,640]{2,1,0:T(8,128)(2,1)} %get-tuple-element.10), channel_id=1, source_target_pairs={{0,1},{1,2},{2,3},{3,0},{4,5},{5,6},{6,7},{7,4},{8,9},{9,10},{10,1... | collective-permute-start | bytes 1228808 | tf_op jit(solution)/shard_map/ppermute | solution.py:116
  42.5 0.6 pad_add_fusion.1.place
  43.1 0.0 all-to-all-done.tokens.residual
  43.1 0.0 collective-permute-done.3.other
  43.1 1.1 copy-done.1
  44.1 6.4 %project_qkv.1 = bf16[4,240,512]{2,1,0:T(8,128)(2,1)} custom-call(s32[4]{0:T(128)} %pad_add_fusion.1.place, bf16[4,128,1280]{2,1,0:T(8,128)(2,1)} %copy-done.1, f32[1280]{0:T(1024)} %gain.2, bf16[240,1280]{1,0:T(8,128)(2,1)} %bitcast.36, bf16[320,640]{1,0:T(8,128)(2,1)} %copy-done.7, bf16[320,640]{1,0:T(8,128)(2,1)} %copy-done.6, ...), custom_call_target="tpu_custom_call" | custom-call | tf_op jit(solution)/shard_map/project_qkv/pallas_call | solution.py:174
  50.5 4.1 %all-to-all-start.1 = ((bf16[4,240,512]{2,1,0:T(8,128)(2,1)}), bf16[4,240,512]{2,1,0:T(8,128)(2,1)S(1)}, u32[]{:S(2)}, u32[]{:S(2)}) async-start(bf16[4,240,512]{2,1,0:T(8,128)(2,1)} %project_qkv.1), calls=%async_computation.1 | async-start | bytes 1966080 | tf_op jit(solution)/shard_map/all_to_all | solution.py:325
  54.6 0.6 collective-permute-done.6
  55.2 0.0 collective-permute-done.5
  55.2 6.1 %collective-permute-done.4 = bf16[4,80,640]{2,1,0:T(8,128)(2,1)} collective-permute-done((bf16[4,80,640]{2,1,0:T(8,128)(2,1)}, bf16[4,80,640]{2,1,0:T(8,128)(2,1)}, u32[]{:S(2)}, u32[]{:S(2)}) %collective-permute-start.4) | collective-permute-done | bytes 409632 | tf_op jit(solution)/shard_map/ppermute | solution.py:116
  61.4 1.5 pad_maximum_fusion.mine
  62.9 0.0 copy-start.2
  62.9 2.4 %collective-permute-start.7 = (bf16[4,4,80,640]{3,2,1,0:T(8,128)(2,1)S(1)}, bf16[4,4,80,640]{3,2,1,0:T(8,128)(2,1)}, u32[]{:S(2)}, u32[]{:S(2)}) collective-permute-start(bf16[4,4,80,640]{3,2,1,0:T(8,128)(2,1)S(1)} %pad_maximum_fusion.mine), channel_id=1, source_target_pairs={{0,16},{16,0},{1,17},{17,1},{2,18},{18,2},{3,19},{19,3},{4,20},{20... | collective-permute-start | bytes 4915208 | tf_op jit(solution)/shard_map/ppermute | solution.py:26
  65.3 0.3 reshape.22
  65.6 0.2 copy.14
  65.7 2.1 %broadcast_in_dim_reshape.8.seg_col = s32[2048,1]{1,0:T(8,128)} reshape(s32[16,4,32]{2,1,0:T(4,128)S(1)} %copy.14) | data formatting | bytes 16384 | tf_op jit(solution)/shard_map/broadcast_in_dim;reshape | solution.py:89
  67.8 0.7 broadcast_in_dim_reshape.7.seg_row
  68.5 0.2 slice_reduce_fusion.1
  68.7 0.2 convert_reduce_fusion.1
  68.9 0.6 pad_add_fusion.bounds
  69.5 0.0 all-to-all-done.1.qkv
  69.5 1.0 copy-done.4
  70.5 11.3 %attention.1 = bf16[4,4,80,512]{3,2,1,0:T(8,128)(2,1)} custom-call(s32[2,4]{1,0:T(2,128)} %pad_add_fusion.bounds, bf16[4,240,512]{2,1,0:T(8,128)(2,1)} %copy-done.4, s32[2048,1]{1,0:T(8,128)} %broadcast_in_dim_reshape.8.seg_col, s32[1,2048]{1,0:T(1,128)} %broadcast_in_dim_reshape.7.seg_row), custom_call_target="tpu_custom_call" | custom-call | tf_op jit(solution)/shard_map/attention/pallas_call | solution.py:97
  81.7 4.5 %all-to-all-start.2 = ((bf16[16,80,512]{2,1,0:T(8,128)(2,1)}), bf16[16,80,512]{2,1,0:T(8,128)(2,1)S(1)}, u32[]{:S(2)}, u32[]{:S(2)}) async-start(bf16[16,80,512]{2,1,0:T(8,128)(2,1)} %bitcast.33), calls=%async_computation.2 | async-start | bytes 2621440 | tf_op jit(solution)/shard_map/all_to_all | solution.py:335
  86.2 2.0 %dynamic_slice.11 = bf16[2560,128]{1,0:T(8,128)(2,1)} dynamic-slice(bf16[5120,256]{1,0:T(8,128)(2,1)} %own.1, s32[]{:T(128)S(6)} %select_n.19, s32[]{:T(128)S(6)} %select_n.20), dynamic_slice_sizes={2560,128} | dynamic-slice | bytes 1310724 | tf_op jit(solution)/shard_map/dynamic_slice | solution.py:319
  88.2 3.2 %collective-permute-start.9 = (bf16[2560,128]{1,0:T(8,128)(2,1)}, bf16[2560,128]{1,0:T(8,128)(2,1)}, u32[]{:S(2)}, u32[]{:S(2)}) collective-permute-start(bf16[2560,128]{1,0:T(8,128)(2,1)} %dynamic_slice.11), channel_id=1, source_target_pairs={{0,4},{4,8},{8,12},{12,0},{1,5},{5,9},{9,13},{13,1},{2,6},{6,10},{... | collective-permute-start | bytes 1966088 | tf_op jit(solution)/shard_map/ppermute | solution.py:30
  91.5 3.2 %collective-permute-start.11 = (bf16[2560,128]{1,0:T(8,128)(2,1)}, bf16[2560,128]{1,0:T(8,128)(2,1)}, u32[]{:S(2)}, u32[]{:S(2)}) collective-permute-start(bf16[2560,128]{1,0:T(8,128)(2,1)} %dynamic_slice.11), channel_id=1, source_target_pairs={{0,12},{4,0},{8,4},{12,8},{1,13},{5,1},{9,5},{13,9},{2,14},{6,2},{... | collective-permute-start | bytes 1966088 | tf_op jit(solution)/shard_map/ppermute | solution.py:30
  94.7 23.6 %collective-permute-done.9.rest_0_ = bf16[2560,128]{1,0:T(8,128)(2,1)} collective-permute-done((bf16[2560,128]{1,0:T(8,128)(2,1)}, bf16[2560,128]{1,0:T(8,128)(2,1)}, u32[]{:S(2)}, u32[]{:S(2)}) %collective-permute-start.9) | collective-permute-done | bytes 655392 | tf_op jit(solution)/shard_map/ppermute | solution.py:30
  118.4 1.9 collective-permute-start.13
  120.3 0.0 collective-permute-done.7.other
  120.3 0.0 all-to-all-done.2.back
  120.3 1.1 copy-done.3
  121.4 7.3 %merge_rows.1 = bf16[4,4,32,1280]{3,2,1,0:T(8,128)(2,1)} custom-call(s32[4]{0:T(128)} %pad_add_fusion.1.place, bf16[16,80,512]{2,1,0:T(8,128)(2,1)} %copy-done.3, bf16[4,128,1280]{2,1,0:T(8,128)(2,1)} %copy-done.1, bf16[4,4,80,640]{3,2,1,0:T(8,128)(2,1)} %copy-done.2, bf16[4,4,80,640]{3,2,1,0:T(8,128)(2,1)} %collective-permute-done.7.other, f32[1280]{0:T(1024)} %gain.3), custom_call_target="tpu_custom_call" | custom-call | tf_op jit(solution)/shard_map/merge_rows/pallas_call | solution.py:214
  128.7 2.5 %collective-permute-start.8 = (bf16[4,128,1280]{2,1,0:T(8,128)(2,1)}, bf16[4,128,1280]{2,1,0:T(8,128)(2,1)S(1)}, u32[]{:S(2)}, u32[]{:S(2)}) collective-permute-start(bf16[4,128,1280]{2,1,0:T(8,128)(2,1)} %bitcast.34), channel_id=1, source_target_pairs={{0,16},{16,0},{1,17},{17,1},{2,18},{18,2},{3,19},{19,3},{4,20},{20... | collective-permute-start | bytes 3932168 | tf_op jit(solution)/shard_map/ppermute | solution.py:26
  131.1 3.5 %collective-permute-start.10 = (bf16[2560,128]{1,0:T(8,128)(2,1)}, bf16[2560,128]{1,0:T(8,128)(2,1)S(1)}, u32[]{:S(2)}, u32[]{:S(2)}) collective-permute-start(bf16[2560,128]{1,0:T(8,128)(2,1)} %collective-permute-done.9.rest_0_), channel_id=1, source_target_pairs={{0,32},{32,64},{64,96},{96,128},{128,160},{160,192},{192,224},{224... | collective-permute-start | bytes 1966088 | tf_op jit(solution)/shard_map/ppermute | solution.py:120
  134.7 0.0 collective-permute-done.11.rest_2_
  134.7 9.5 %collective-permute-start.12 = (bf16[2560,128]{1,0:T(8,128)(2,1)}, bf16[2560,128]{1,0:T(8,128)(2,1)S(1)}, u32[]{:S(2)}, u32[]{:S(2)}) collective-permute-start(bf16[2560,128]{1,0:T(8,128)(2,1)} %collective-permute-done.11.rest_2_), channel_id=1, source_target_pairs={{0,480},{32,0},{64,32},{96,64},{128,96},{160,128},{192,160},{224,1... | collective-permute-start | bytes 1966088 | tf_op jit(solution)/shard_map/ppermute | solution.py:120
  144.2 0.0 collective-permute-done.13.rest_4_
  144.2 1.9 collective-permute-start.14
  146.2 11.4 %collective-permute-done.10.rest_1_ = bf16[2560,128]{1,0:T(8,128)(2,1)S(1)} collective-permute-done((bf16[2560,128]{1,0:T(8,128)(2,1)}, bf16[2560,128]{1,0:T(8,128)(2,1)S(1)}, u32[]{:S(2)}, u32[]{:S(2)}) %collective-permute-start.10) | collective-permute-done | bytes 655392 | tf_op jit(solution)/shard_map/ppermute | solution.py:120
  157.6 1.0 collective-permute-done.12.rest_3_
  158.6 13.0 %collective-permute-done.14.rest_5_ = bf16[2560,128]{1,0:T(8,128)(2,1)S(1)} collective-permute-done((bf16[2560,128]{1,0:T(8,128)(2,1)}, bf16[2560,128]{1,0:T(8,128)(2,1)S(1)}, u32[]{:S(2)}, u32[]{:S(2)}) %collective-permute-start.14) | collective-permute-done | bytes 655392 | tf_op jit(solution)/shard_map/ppermute | solution.py:120
  171.6 0.0 collective-permute-done.8.other
  171.6 0.0 copy-done.9
  171.6 0.8 copy-done.11
  172.5 1.1 copy-done.8
  173.5 6.5 %merge.1 = bf16[2,128,512]{2,1,0:T(8,128)(2,1)} custom-call(s32[4]{0:T(128)} %pad_add_fusion.1.place, bf16[4,128,1280]{2,1,0:T(8,128)(2,1)} %bitcast.35, bf16[4,128,1280]{2,1,0:T(8,128)(2,1)} %copy-done.8, bf16[5120,256]{1,0:T(8,128)(2,1)} %own.1, bf16[2560,128]{1,0:T(8,128)(2,1)} %collective-permute-done.9.rest_0_, bf16[2560,128]{1,0:T(8,128)(2,1)} %copy-done.9, ...), custom_call_target="tpu_custom_call" | custom-call | tf_op jit(solution)/shard_map/merge/pallas_call | solution.py:254
  180.1 11.4 %all_to_all.20 = bf16[8,32,512]{2,1,0:T(8,128)(2,1)} all-to-all(bf16[8,32,512]{2,1,0:T(8,128)(2,1)} %bitcast.37), channel_id=1, replica_groups=mesh['z'=16,'c'=2,'y'=4,'x'=4] {'c','x'}, dimensions={0} | all-to-all | bytes 524288 | tf_op jit(solution)/shard_map/all_to_all | solution.py:347
  191.4 2.4 %place_columns.1 = bf16[32,4096]{1,0:T(8,128)(2,1)} custom-call(s32[4]{0:T(128)} %pad_add_fusion.1.place, bf16[2,4,32,512]{3,2,1,0:T(8,128)(2,1)} %bitcast.38), custom_call_target="tpu_custom_call" | custom-call | tf_op jit(solution)/shard_map/place_columns/pallas_call | solution.py:286
  (28 shorter events, 0.2 us)
Async XLA Ops:
  0.0 0.9 copy-start
  2.0 17.9 %collective-permute-start.2 = (bf16[320,640]{1,0:T(8,128)(2,1)S(1)}, bf16[320,640]{1,0:T(8,128)(2,1)S(1)}, u32[]{:S(2)}, u32[]{:S(2)}) collective-permute-start(bf16[320,640]{1,0:T(8,128)(2,1)S(1)} %pad_maximum_fusion.2), channel_id=1, source_target_pairs={{0,4},{4,8},{8,12},{12,0},{1,5},{5,9},{9,13},{13,1},{2,6},{6,10},{... | collective-permute-start | bytes 1228808 | tf_op jit(solution)/shard_map/ppermute | solution.py:30
  6.0 20.3 %collective-permute-start.1 = (bf16[320,640]{1,0:T(8,128)(2,1)S(1)}, bf16[320,640]{1,0:T(8,128)(2,1)S(1)}, u32[]{:S(2)}, u32[]{:S(2)}) collective-permute-start(bf16[320,640]{1,0:T(8,128)(2,1)S(1)} %pad_maximum_fusion.2), channel_id=1, source_target_pairs={{0,8},{4,12},{8,0},{12,4},{1,9},{5,13},{9,1},{13,5},{2,10},{6,14},... | collective-permute-start | bytes 1228808 | tf_op jit(solution)/shard_map/ppermute | solution.py:30
  10.6 15.8 %collective-permute-start = (bf16[320,640]{1,0:T(8,128)(2,1)S(1)}, bf16[320,640]{1,0:T(8,128)(2,1)S(1)}, u32[]{:S(2)}, u32[]{:S(2)}) collective-permute-start(bf16[320,640]{1,0:T(8,128)(2,1)S(1)} %pad_maximum_fusion.2), channel_id=1, source_target_pairs={{0,12},{4,0},{8,4},{12,8},{1,13},{5,1},{9,5},{13,9},{2,14},{6,2},{... | collective-permute-start | bytes 1228808 | tf_op jit(solution)/shard_map/ppermute | solution.py:30
  15.9 27.2 %all-to-all-start = ((bf16[4,128,1280]{2,1,0:T(8,128)(2,1)}), bf16[4,128,1280]{2,1,0:T(8,128)(2,1)S(1)}, u32[]{:S(2)}, u32[]{:S(2)}) async-start(bf16[4,128,1280]{2,1,0:T(8,128)(2,1)} %spread.1), calls=%async_computation | async-start | bytes 2621440 | tf_op jit(solution)/shard_map/all_to_all | solution.py:308
  19.9 12.3 %copy-start.5 = (bf16[320,640]{1,0:T(8,128)(2,1)}, bf16[320,640]{1,0:T(8,128)(2,1)S(1)}, u32[]{:S(2)}) copy-start(bf16[320,640]{1,0:T(8,128)(2,1)S(1)} %collective-permute-done.2.third) | copy-start | bytes 1228804
  26.3 5.9 %copy-start.6 = (bf16[320,640]{1,0:T(8,128)(2,1)}, bf16[320,640]{1,0:T(8,128)(2,1)S(1)}, u32[]{:S(2)}) copy-start(bf16[320,640]{1,0:T(8,128)(2,1)S(1)} %collective-permute-done.1.second) | copy-start | bytes 1228804
  26.4 6.7 %copy-start.7 = (bf16[320,640]{1,0:T(8,128)(2,1)}, bf16[320,640]{1,0:T(8,128)(2,1)S(1)}, u32[]{:S(2)}) copy-start(bf16[320,640]{1,0:T(8,128)(2,1)S(1)} %collective-permute-done.first) | copy-start | bytes 1228804
  27.6 15.5 %collective-permute-start.3 = (bf16[3,240,640]{2,1,0:T(8,128)(2,1)}, bf16[3,240,640]{2,1,0:T(8,128)(2,1)}, u32[]{:S(2)}, u32[]{:S(2)}) collective-permute-start(bf16[3,240,640]{2,1,0:T(8,128)(2,1)} %pad_maximum_fusion.1), channel_id=1, source_target_pairs={{0,16},{16,0},{1,17},{17,1},{2,18},{18,2},{3,19},{19,3},{4,20},{20... | collective-permute-start | bytes 2764808 | tf_op jit(solution)/shard_map/ppermute | solution.py:26
  33.1 22.1 %collective-permute-start.6 = (bf16[4,80,640]{2,1,0:T(8,128)(2,1)}, bf16[4,80,640]{2,1,0:T(8,128)(2,1)}, u32[]{:S(2)}, u32[]{:S(2)}) collective-permute-start(bf16[4,80,640]{2,1,0:T(8,128)(2,1)} %get-tuple-element.10), channel_id=1, source_target_pairs={{0,3},{1,0},{2,1},{3,2},{4,7},{5,4},{6,5},{7,6},{8,11},{9,8},{10,9... | collective-permute-start | bytes 1228808 | tf_op jit(solution)/shard_map/ppermute | solution.py:116
  37.5 17.7 %collective-permute-start.5 = (bf16[4,80,640]{2,1,0:T(8,128)(2,1)}, bf16[4,80,640]{2,1,0:T(8,128)(2,1)}, u32[]{:S(2)}, u32[]{:S(2)}) collective-permute-start(bf16[4,80,640]{2,1,0:T(8,128)(2,1)} %get-tuple-element.10), channel_id=1, source_target_pairs={{0,2},{1,3},{2,0},{3,1},{4,6},{5,7},{6,4},{7,5},{8,10},{9,11},{10,... | collective-permute-start | bytes 1228808 | tf_op jit(solution)/shard_map/ppermute | solution.py:116
  39.9 21.4 %collective-permute-start.4 = (bf16[4,80,640]{2,1,0:T(8,128)(2,1)}, bf16[4,80,640]{2,1,0:T(8,128)(2,1)}, u32[]{:S(2)}, u32[]{:S(2)}) collective-permute-start(bf16[4,80,640]{2,1,0:T(8,128)(2,1)} %get-tuple-element.10), channel_id=1, source_target_pairs={{0,1},{1,2},{2,3},{3,0},{4,5},{5,6},{6,7},{7,4},{8,9},{9,10},{10,1... | collective-permute-start | bytes 1228808 | tf_op jit(solution)/shard_map/ppermute | solution.py:116
  43.1 1.1 copy-start.1
  50.5 19.0 %all-to-all-start.1 = ((bf16[4,240,512]{2,1,0:T(8,128)(2,1)}), bf16[4,240,512]{2,1,0:T(8,128)(2,1)S(1)}, u32[]{:S(2)}, u32[]{:S(2)}) async-start(bf16[4,240,512]{2,1,0:T(8,128)(2,1)} %project_qkv.1), calls=%async_computation.1 | async-start | bytes 1966080 | tf_op jit(solution)/shard_map/all_to_all | solution.py:325
  61.4 3.9 %copy-start.12 = (s32[2048]{0:T(1024)S(1)}, s32[2048]{0:T(1024)}, u32[]{:S(2)}) copy-start(s32[2048]{0:T(1024)} %param.8) | copy-start | bytes 24580
  62.9 18.9 %copy-start.2 = (bf16[4,4,80,640]{3,2,1,0:T(8,128)(2,1)}, bf16[4,4,80,640]{3,2,1,0:T(8,128)(2,1)S(1)}, u32[]{:S(2)}) copy-start(bf16[4,4,80,640]{3,2,1,0:T(8,128)(2,1)S(1)} %pad_maximum_fusion.mine) | copy-start | bytes 4915204
  62.9 57.4 %collective-permute-start.7 = (bf16[4,4,80,640]{3,2,1,0:T(8,128)(2,1)S(1)}, bf16[4,4,80,640]{3,2,1,0:T(8,128)(2,1)}, u32[]{:S(2)}, u32[]{:S(2)}) collective-permute-start(bf16[4,4,80,640]{3,2,1,0:T(8,128)(2,1)S(1)} %pad_maximum_fusion.mine), channel_id=1, source_target_pairs={{0,16},{16,0},{1,17},{17,1},{2,18},{18,2},{3,19},{19,3},{4,20},{20... | collective-permute-start | bytes 4915208 | tf_op jit(solution)/shard_map/ppermute | solution.py:26
  69.5 1.0 copy-start.4
  81.7 38.5 %all-to-all-start.2 = ((bf16[16,80,512]{2,1,0:T(8,128)(2,1)}), bf16[16,80,512]{2,1,0:T(8,128)(2,1)S(1)}, u32[]{:S(2)}, u32[]{:S(2)}) async-start(bf16[16,80,512]{2,1,0:T(8,128)(2,1)} %bitcast.33), calls=%async_computation.2 | async-start | bytes 2621440 | tf_op jit(solution)/shard_map/all_to_all | solution.py:335
  88.2 30.1 %collective-permute-start.9 = (bf16[2560,128]{1,0:T(8,128)(2,1)}, bf16[2560,128]{1,0:T(8,128)(2,1)}, u32[]{:S(2)}, u32[]{:S(2)}) collective-permute-start(bf16[2560,128]{1,0:T(8,128)(2,1)} %dynamic_slice.11), channel_id=1, source_target_pairs={{0,4},{4,8},{8,12},{12,0},{1,5},{5,9},{9,13},{13,1},{2,6},{6,10},{... | collective-permute-start | bytes 1966088 | tf_op jit(solution)/shard_map/ppermute | solution.py:30
  91.5 43.2 %collective-permute-start.11 = (bf16[2560,128]{1,0:T(8,128)(2,1)}, bf16[2560,128]{1,0:T(8,128)(2,1)}, u32[]{:S(2)}, u32[]{:S(2)}) collective-permute-start(bf16[2560,128]{1,0:T(8,128)(2,1)} %dynamic_slice.11), channel_id=1, source_target_pairs={{0,12},{4,0},{8,4},{12,8},{1,13},{5,1},{9,5},{13,9},{2,14},{6,2},{... | collective-permute-start | bytes 1966088 | tf_op jit(solution)/shard_map/ppermute | solution.py:30
  118.4 25.9 %collective-permute-start.13 = (bf16[2560,128]{1,0:T(8,128)(2,1)}, bf16[2560,128]{1,0:T(8,128)(2,1)}, u32[]{:S(2)}, u32[]{:S(2)}) collective-permute-start(bf16[2560,128]{1,0:T(8,128)(2,1)} %collective-permute-done.9.rest_0_), channel_id=1, source_target_pairs={{0,4},{4,8},{8,12},{12,0},{1,5},{5,9},{9,13},{13,1},{2,6},{6,10},{... | collective-permute-start | bytes 1966088 | tf_op jit(solution)/shard_map/ppermute | solution.py:30
  120.3 1.1 copy-start.3
  128.7 43.0 %collective-permute-start.8 = (bf16[4,128,1280]{2,1,0:T(8,128)(2,1)}, bf16[4,128,1280]{2,1,0:T(8,128)(2,1)S(1)}, u32[]{:S(2)}, u32[]{:S(2)}) collective-permute-start(bf16[4,128,1280]{2,1,0:T(8,128)(2,1)} %bitcast.34), channel_id=1, source_target_pairs={{0,16},{16,0},{1,17},{17,1},{2,18},{18,2},{3,19},{19,3},{4,20},{20... | collective-permute-start | bytes 3932168 | tf_op jit(solution)/shard_map/ppermute | solution.py:26
  131.1 26.4 %collective-permute-start.10 = (bf16[2560,128]{1,0:T(8,128)(2,1)}, bf16[2560,128]{1,0:T(8,128)(2,1)S(1)}, u32[]{:S(2)}, u32[]{:S(2)}) collective-permute-start(bf16[2560,128]{1,0:T(8,128)(2,1)} %collective-permute-done.9.rest_0_), channel_id=1, source_target_pairs={{0,32},{32,64},{64,96},{96,128},{128,160},{160,192},{192,224},{224... | collective-permute-start | bytes 1966088 | tf_op jit(solution)/shard_map/ppermute | solution.py:120
  134.7 23.9 %collective-permute-start.12 = (bf16[2560,128]{1,0:T(8,128)(2,1)}, bf16[2560,128]{1,0:T(8,128)(2,1)S(1)}, u32[]{:S(2)}, u32[]{:S(2)}) collective-permute-start(bf16[2560,128]{1,0:T(8,128)(2,1)} %collective-permute-done.11.rest_2_), channel_id=1, source_target_pairs={{0,480},{32,0},{64,32},{96,64},{128,96},{160,128},{192,160},{224,1... | collective-permute-start | bytes 1966088 | tf_op jit(solution)/shard_map/ppermute | solution.py:120
  144.2 27.4 %collective-permute-start.14 = (bf16[2560,128]{1,0:T(8,128)(2,1)}, bf16[2560,128]{1,0:T(8,128)(2,1)S(1)}, u32[]{:S(2)}, u32[]{:S(2)}) collective-permute-start(bf16[2560,128]{1,0:T(8,128)(2,1)} %collective-permute-done.13.rest_4_), channel_id=1, source_target_pairs={{0,32},{32,64},{64,96},{96,128},{128,160},{160,192},{192,224},{224... | collective-permute-start | bytes 1966088 | tf_op jit(solution)/shard_map/ppermute | solution.py:120
  157.6 14.1 %copy-start.9 = (bf16[2560,128]{1,0:T(8,128)(2,1)}, bf16[2560,128]{1,0:T(8,128)(2,1)S(1)}, u32[]{:S(2)}) copy-start(bf16[2560,128]{1,0:T(8,128)(2,1)S(1)} %collective-permute-done.10.rest_1_) | copy-start | bytes 1966084
  158.6 13.0 %copy-start.10 = (bf16[2560,128]{1,0:T(8,128)(2,1)}, bf16[2560,128]{1,0:T(8,128)(2,1)S(1)}, u32[]{:S(2)}) copy-start(bf16[2560,128]{1,0:T(8,128)(2,1)S(1)} %collective-permute-done.12.rest_3_) | copy-start | bytes 1966084
  171.6 0.9 copy-start.11
  172.5 1.1 copy-start.8

commit v6 on v5

--- a/solution.py
+++ b/solution.py
@@ -116,8 +116,8 @@
     return lax.ppermute(value, "x", [(at, (at + step) % cols) for at in range(cols)])
 
 
-def shift_planes(value, step, planes):
-    return lax.ppermute(value, "z", [(at, (at + step) % planes) for at in range(planes)])
+def swap_planes(value, planes):
+    return lax.ppermute(value, "z", [(at, at ^ 1) for at in range(planes)])
 
 
 def matmul(left, right, left_dim, right_dim):
@@ -327,15 +327,15 @@
     out_rows = jnp.stack([own[wide:]] + [part[wide:] for part in ahead])
     next_out = shift_cols(out_rows, 1, cols)
     out_parts = [out_rows, next_out] + [shift_cols(out_rows, step, cols) for step in (2, 3)]
-    first_z = shift_planes(first_y, 1, planes)
-    third_z = shift_planes(third_y, planes - 1, planes)
+    first_z = swap_planes(first_y, planes)
+    third_z = swap_planes(third_y, planes)
     second_y = shift_rows(first_y, 1, rows)
 
     attended = attention(by_head, layout, cols)
     back = lax.all_to_all(
         attended.reshape(rows * cols, HEAD_DIM, row_count), ("y", "x"),
         split_axis=0, concat_axis=0, tiled=True)
-    second_z = shift_planes(second_y, 1, planes)
+    second_z = swap_planes(second_y, planes)
     mine_out = jnp.stack(out_parts)
     other_out = swap_cores(mine_out)
     merged = merge_rows(

time: 195 us -> 201 us (1.031)
  waiting for transfers between devices: 62.2 us -> 74.6 us
  starting transfers between devices: 66.3 us -> 60.2 us
    ppermute x3, waiting for transfers between devices: 25.5 us -> 37 us  [swap_planes(): return lax.ppermute(value, 'z', [(at, at ^ 1) for at in range(planes)])]
    ppermute x3, starting transfers between devices: 15 us -> 8.91 us  [swap_planes(): return lax.ppermute(value, 'z', [(at, at ^ 1) for at in range(planes)])]
  transfers between devices with their start and end apart: 18 -> 18, of which waited for: 7 -> 8; matrix products, arithmetic and copies ran while one was open for 5% -> 5% of each run, Pallas kernels for 14% -> 14%
where the time goes in v6:
time: 201 us; the launch traced here: 200 us
  waiting for transfers between devices  74.6 us (37%)
  starting transfers between devices  60.2 us (30%)
  Pallas kernels  36.2 us (18%)
  local copies, waits for them, and re-layouts  12.5 us (6%)
  blocking collectives  11.5 us (6%)
  other arithmetic  4.95 us (2%)
    ppermute x3, waiting for transfers between devices, swap_planes(): return lax.ppermute(value, 'z', [(at, at ^ 1) for at in range(planes)])  37 us
    ppermute x6, waiting for transfers between devices, shift_rows(): lax.ppermute(value, 'y', [(at, (at + step) % rows) for at in range(rows)])  30.9 us
    ppermute x6, starting transfers between devices, shift_rows(): lax.ppermute(value, 'y', [(at, (at + step) % rows) for at in range(rows)])  19.9 us
    all_to_all x1, blocking collectives, block_step(): lax.all_to_all(block.reshape(2 * cols, groups, block.shape[2]), ('c', 'x'...  11.5 us
    pallas_call x1, Pallas kernels, attention(): pl.pallas_call(attention_kernel, out_shape=jax.ShapeDtypeStruct((tiles, c...  11.3 us
    ppermute x3, starting transfers between devices, swap_cores(): return lax.ppermute(value, 'c', [(0, 1), (1, 0)])  9.48 us
    ppermute x3, starting transfers between devices, shift_cols(): lax.ppermute(value, 'x', [(at, (at + step) % cols) for at in range(cols)])  9.32 us
    ppermute x3, starting transfers between devices, swap_planes(): return lax.ppermute(value, 'z', [(at, at ^ 1) for at in range(planes)])  8.91 us
  transfers between devices with their start and end apart: 18, of which 8 were waited for; matrix products, arithmetic and copies ran while one was open for 5% of the time, Pallas kernels for 14%

profile of v6, /device:TPU:1, one launch (start us, length us, event | category | flops | bytes accessed | tf_op | source)
XLA Modules:
  0.0 200.3 jit_solution(12545832296301897050)
XLA Ops:
  0.0 0.0 copy-start
  0.0 0.9 copy-done
  0.9 1.0 dynamic-slice_bitcast_fusion
  2.0 4.0 %collective-permute-start.2 = (bf16[320,640]{1,0:T(8,128)(2,1)S(1)}, bf16[320,640]{1,0:T(8,128)(2,1)S(1)}, u32[]{:S(2)}, u32[]{:S(2)}) collective-permute-start(bf16[320,640]{1,0:T(8,128)(2,1)S(1)} %pad_maximum_fusion.2), channel_id=1, source_target_pairs={{0,4},{4,8},{8,12},{12,0},{1,5},{5,9},{9,13},{13,1},{2,6},{6,10},{... | collective-permute-start | bytes 1228808 | tf_op jit(solution)/shard_map/ppermute | solution.py:30
  6.0 4.5 %collective-permute-start.1 = (bf16[320,640]{1,0:T(8,128)(2,1)S(1)}, bf16[320,640]{1,0:T(8,128)(2,1)S(1)}, u32[]{:S(2)}, u32[]{:S(2)}) collective-permute-start(bf16[320,640]{1,0:T(8,128)(2,1)S(1)} %pad_maximum_fusion.2), channel_id=1, source_target_pairs={{0,8},{4,12},{8,0},{12,4},{1,9},{5,13},{9,1},{13,5},{2,10},{6,14},... | collective-permute-start | bytes 1228808 | tf_op jit(solution)/shard_map/ppermute | solution.py:30
  10.6 3.0 %collective-permute-start = (bf16[320,640]{1,0:T(8,128)(2,1)S(1)}, bf16[320,640]{1,0:T(8,128)(2,1)S(1)}, u32[]{:S(2)}, u32[]{:S(2)}) collective-permute-start(bf16[320,640]{1,0:T(8,128)(2,1)S(1)} %pad_maximum_fusion.2), channel_id=1, source_target_pairs={{0,12},{4,0},{8,4},{12,8},{1,13},{5,1},{9,5},{13,9},{2,14},{6,2},{... | collective-permute-start | bytes 1228808 | tf_op jit(solution)/shard_map/ppermute | solution.py:30
  13.5 2.3 %spread.1 = bf16[4,128,1280]{2,1,0:T(8,128)(2,1)} custom-call(bf16[128,1280]{1,0:T(8,128)(2,1)} %tokens.1), custom_call_target="tpu_custom_call" | custom-call | tf_op jit(solution)/shard_map/spread/pallas_call | solution.py:145
  15.9 4.0 %all-to-all-start = ((bf16[4,128,1280]{2,1,0:T(8,128)(2,1)}), bf16[4,128,1280]{2,1,0:T(8,128)(2,1)S(1)}, u32[]{:S(2)}, u32[]{:S(2)}) async-start(bf16[4,128,1280]{2,1,0:T(8,128)(2,1)} %spread.1), calls=%async_computation | async-start | bytes 2621440 | tf_op jit(solution)/shard_map/all_to_all | solution.py:308
  19.9 0.0 collective-permute-done.2.third
  20.0 6.4 %collective-permute-done.1.second = bf16[320,640]{1,0:T(8,128)(2,1)S(1)} collective-permute-done((bf16[320,640]{1,0:T(8,128)(2,1)S(1)}, bf16[320,640]{1,0:T(8,128)(2,1)S(1)}, u32[]{:S(2)}, u32[]{:S(2)}) %collective-permute-start.1) | collective-permute-done | bytes 409632 | tf_op jit(solution)/shard_map/ppermute | solution.py:30
  26.4 0.0 collective-permute-done.first
  26.4 1.2 pad_maximum_fusion.1
  27.6 4.6 %collective-permute-start.3 = (bf16[3,240,640]{2,1,0:T(8,128)(2,1)}, bf16[3,240,640]{2,1,0:T(8,128)(2,1)}, u32[]{:S(2)}, u32[]{:S(2)}) collective-permute-start(bf16[3,240,640]{2,1,0:T(8,128)(2,1)} %pad_maximum_fusion.1), channel_id=1, source_target_pairs={{0,16},{16,0},{1,17},{17,1},{2,18},{18,2},{3,19},{19,3},{4,20},{20... | collective-permute-start | bytes 2764808 | tf_op jit(solution)/shard_map/ppermute | solution.py:26
  32.3 0.8 fusion
  33.1 4.4 %collective-permute-start.6 = (bf16[4,80,640]{2,1,0:T(8,128)(2,1)}, bf16[4,80,640]{2,1,0:T(8,128)(2,1)}, u32[]{:S(2)}, u32[]{:S(2)}) collective-permute-start(bf16[4,80,640]{2,1,0:T(8,128)(2,1)} %get-tuple-element.10), channel_id=1, source_target_pairs={{0,3},{1,0},{2,1},{3,2},{4,7},{5,4},{6,5},{7,6},{8,11},{9,8},{10,9... | collective-permute-start | bytes 1228808 | tf_op jit(solution)/shard_map/ppermute | solution.py:116
  37.5 2.4 %collective-permute-start.5 = (bf16[4,80,640]{2,1,0:T(8,128)(2,1)}, bf16[4,80,640]{2,1,0:T(8,128)(2,1)}, u32[]{:S(2)}, u32[]{:S(2)}) collective-permute-start(bf16[4,80,640]{2,1,0:T(8,128)(2,1)} %get-tuple-element.10), channel_id=1, source_target_pairs={{0,2},{1,3},{2,0},{3,1},{4,6},{5,7},{6,4},{7,5},{8,10},{9,11},{10,... | collective-permute-start | bytes 1228808 | tf_op jit(solution)/shard_map/ppermute | solution.py:116
  39.9 2.5 %collective-permute-start.4 = (bf16[4,80,640]{2,1,0:T(8,128)(2,1)}, bf16[4,80,640]{2,1,0:T(8,128)(2,1)}, u32[]{:S(2)}, u32[]{:S(2)}) collective-permute-start(bf16[4,80,640]{2,1,0:T(8,128)(2,1)} %get-tuple-element.10), channel_id=1, source_target_pairs={{0,1},{1,2},{2,3},{3,0},{4,5},{5,6},{6,7},{7,4},{8,9},{9,10},{10,1... | collective-permute-start | bytes 1228808 | tf_op jit(solution)/shard_map/ppermute | solution.py:116
  42.5 0.6 pad_add_fusion.1.place
  43.1 0.0 all-to-all-done.tokens.residual
  43.1 0.0 collective-permute-done.3.other
  43.1 1.1 copy-done.1
  44.1 6.4 %project_qkv.1 = bf16[4,240,512]{2,1,0:T(8,128)(2,1)} custom-call(s32[4]{0:T(128)} %pad_add_fusion.1.place, bf16[4,128,1280]{2,1,0:T(8,128)(2,1)} %copy-done.1, f32[1280]{0:T(1024)} %gain.2, bf16[240,1280]{1,0:T(8,128)(2,1)} %bitcast.36, bf16[320,640]{1,0:T(8,128)(2,1)} %copy-done.7, bf16[320,640]{1,0:T(8,128)(2,1)} %copy-done.6, ...), custom_call_target="tpu_custom_call" | custom-call | tf_op jit(solution)/shard_map/project_qkv/pallas_call | solution.py:174
  50.5 4.1 %all-to-all-start.1 = ((bf16[4,240,512]{2,1,0:T(8,128)(2,1)}), bf16[4,240,512]{2,1,0:T(8,128)(2,1)S(1)}, u32[]{:S(2)}, u32[]{:S(2)}) async-start(bf16[4,240,512]{2,1,0:T(8,128)(2,1)} %project_qkv.1), calls=%async_computation.1 | async-start | bytes 1966080 | tf_op jit(solution)/shard_map/all_to_all | solution.py:325
  54.6 0.6 collective-permute-done.6
  55.2 0.0 collective-permute-done.5
  55.2 6.1 %collective-permute-done.4 = bf16[4,80,640]{2,1,0:T(8,128)(2,1)} collective-permute-done((bf16[4,80,640]{2,1,0:T(8,128)(2,1)}, bf16[4,80,640]{2,1,0:T(8,128)(2,1)}, u32[]{:S(2)}, u32[]{:S(2)}) %collective-permute-start.4) | collective-permute-done | bytes 409632 | tf_op jit(solution)/shard_map/ppermute | solution.py:116
  61.4 1.5 pad_maximum_fusion.mine
  62.9 0.0 copy-start.2
  62.9 2.4 %collective-permute-start.7 = (bf16[4,4,80,640]{3,2,1,0:T(8,128)(2,1)S(1)}, bf16[4,4,80,640]{3,2,1,0:T(8,128)(2,1)}, u32[]{:S(2)}, u32[]{:S(2)}) collective-permute-start(bf16[4,4,80,640]{3,2,1,0:T(8,128)(2,1)S(1)} %pad_maximum_fusion.mine), channel_id=1, source_target_pairs={{0,16},{16,0},{1,17},{17,1},{2,18},{18,2},{3,19},{19,3},{4,20},{20... | collective-permute-start | bytes 4915208 | tf_op jit(solution)/shard_map/ppermute | solution.py:26
  65.3 0.3 reshape.22
  65.6 0.2 copy.14
  65.7 2.1 %broadcast_in_dim_reshape.8.seg_col = s32[2048,1]{1,0:T(8,128)} reshape(s32[16,4,32]{2,1,0:T(4,128)S(1)} %copy.14) | data formatting | bytes 16384 | tf_op jit(solution)/shard_map/broadcast_in_dim;reshape | solution.py:89
  67.8 0.7 broadcast_in_dim_reshape.7.seg_row
  68.5 0.2 slice_reduce_fusion.1
  68.7 0.2 convert_reduce_fusion.1
  68.9 0.6 pad_add_fusion.bounds
  69.5 0.0 all-to-all-done.1.qkv
  69.5 1.0 copy-done.4
  70.5 11.3 %attention.1 = bf16[4,4,80,512]{3,2,1,0:T(8,128)(2,1)} custom-call(s32[2,4]{1,0:T(2,128)} %pad_add_fusion.bounds, bf16[4,240,512]{2,1,0:T(8,128)(2,1)} %copy-done.4, s32[2048,1]{1,0:T(8,128)} %broadcast_in_dim_reshape.8.seg_col, s32[1,2048]{1,0:T(1,128)} %broadcast_in_dim_reshape.7.seg_row), custom_call_target="tpu_custom_call" | custom-call | tf_op jit(solution)/shard_map/attention/pallas_call | solution.py:97
  81.7 4.5 %all-to-all-start.2 = ((bf16[16,80,512]{2,1,0:T(8,128)(2,1)}), bf16[16,80,512]{2,1,0:T(8,128)(2,1)S(1)}, u32[]{:S(2)}, u32[]{:S(2)}) async-start(bf16[16,80,512]{2,1,0:T(8,128)(2,1)} %bitcast.33), calls=%async_computation.2 | async-start | bytes 2621440 | tf_op jit(solution)/shard_map/all_to_all | solution.py:335
  86.2 2.0 dynamic_slice.11
  88.2 3.2 %collective-permute-start.9 = (bf16[2560,128]{1,0:T(8,128)(2,1)}, bf16[2560,128]{1,0:T(8,128)(2,1)}, u32[]{:S(2)}, u32[]{:S(2)}) collective-permute-start(bf16[2560,128]{1,0:T(8,128)(2,1)} %dynamic_slice.11), channel_id=1, source_target_pairs={{0,4},{4,8},{8,12},{12,0},{1,5},{5,9},{9,13},{13,1},{2,6},{6,10},{... | collective-permute-start | bytes 1966088 | tf_op jit(solution)/shard_map/ppermute | solution.py:30
  91.5 3.2 %collective-permute-start.11 = (bf16[2560,128]{1,0:T(8,128)(2,1)}, bf16[2560,128]{1,0:T(8,128)(2,1)}, u32[]{:S(2)}, u32[]{:S(2)}) collective-permute-start(bf16[2560,128]{1,0:T(8,128)(2,1)} %dynamic_slice.11), channel_id=1, source_target_pairs={{0,12},{4,0},{8,4},{12,8},{1,13},{5,1},{9,5},{13,9},{2,14},{6,2},{... | collective-permute-start | bytes 1966088 | tf_op jit(solution)/shard_map/ppermute | solution.py:30
  94.7 23.6 %collective-permute-done.9.rest_0_ = bf16[2560,128]{1,0:T(8,128)(2,1)} collective-permute-done((bf16[2560,128]{1,0:T(8,128)(2,1)}, bf16[2560,128]{1,0:T(8,128)(2,1)}, u32[]{:S(2)}, u32[]{:S(2)}) %collective-permute-start.9) | collective-permute-done | bytes 655392 | tf_op jit(solution)/shard_map/ppermute | solution.py:30
  118.4 1.9 collective-permute-start.13
  120.3 0.0 collective-permute-done.7.other
  120.3 0.0 all-to-all-done.2.back
  120.3 1.1 copy-done.3
  121.4 7.3 %merge_rows.1 = bf16[4,4,32,1280]{3,2,1,0:T(8,128)(2,1)} custom-call(s32[4]{0:T(128)} %pad_add_fusion.1.place, bf16[16,80,512]{2,1,0:T(8,128)(2,1)} %copy-done.3, bf16[4,128,1280]{2,1,0:T(8,128)(2,1)} %copy-done.1, bf16[4,4,80,640]{3,2,1,0:T(8,128)(2,1)} %copy-done.2, bf16[4,4,80,640]{3,2,1,0:T(8,128)(2,1)} %collective-permute-done.7.other, f32[1280]{0:T(1024)} %gain.3), custom_call_target="tpu_custom_call" | custom-call | tf_op jit(solution)/shard_map/merge_rows/pallas_call | solution.py:214
  128.7 2.5 %collective-permute-start.8 = (bf16[4,128,1280]{2,1,0:T(8,128)(2,1)}, bf16[4,128,1280]{2,1,0:T(8,128)(2,1)S(1)}, u32[]{:S(2)}, u32[]{:S(2)}) collective-permute-start(bf16[4,128,1280]{2,1,0:T(8,128)(2,1)} %bitcast.34), channel_id=1, source_target_pairs={{0,16},{16,0},{1,17},{17,1},{2,18},{18,2},{3,19},{19,3},{4,20},{20... | collective-permute-start | bytes 3932168 | tf_op jit(solution)/shard_map/ppermute | solution.py:26
  131.1 3.5 %collective-permute-start.10 = (bf16[2560,128]{1,0:T(8,128)(2,1)}, bf16[2560,128]{1,0:T(8,128)(2,1)S(1)}, u32[]{:S(2)}, u32[]{:S(2)}) collective-permute-start(bf16[2560,128]{1,0:T(8,128)(2,1)} %collective-permute-done.9.rest_0_), channel_id=1, source_target_pairs={{0,32},{32,0},{64,96},{96,64},{128,160},{160,128},{192,224},{224,1... | collective-permute-start | bytes 1966088 | tf_op jit(solution)/shard_map/ppermute | solution.py:120
  134.7 0.0 collective-permute-done.11.rest_2_
  134.7 1.9 collective-permute-start.12
  136.6 0.9 collective-permute-done.13.rest_4_
  137.5 3.5 %collective-permute-start.14 = (bf16[2560,128]{1,0:T(8,128)(2,1)}, bf16[2560,128]{1,0:T(8,128)(2,1)S(1)}, u32[]{:S(2)}, u32[]{:S(2)}) collective-permute-start(bf16[2560,128]{1,0:T(8,128)(2,1)} %collective-permute-done.13.rest_4_), channel_id=1, source_target_pairs={{0,32},{32,0},{64,96},{96,64},{128,160},{160,128},{192,224},{224,1... | collective-permute-start | bytes 1966088 | tf_op jit(solution)/shard_map/ppermute | solution.py:120
  140.9 8.9 %collective-permute-done.10.rest_1_ = bf16[2560,128]{1,0:T(8,128)(2,1)S(1)} collective-permute-done((bf16[2560,128]{1,0:T(8,128)(2,1)}, bf16[2560,128]{1,0:T(8,128)(2,1)S(1)}, u32[]{:S(2)}, u32[]{:S(2)}) %collective-permute-start.10) | collective-permute-done | bytes 655392 | tf_op jit(solution)/shard_map/ppermute | solution.py:120
  149.9 14.0 %collective-permute-done.12.rest_3_ = bf16[2560,128]{1,0:T(8,128)(2,1)S(1)} collective-permute-done((bf16[2560,128]{1,0:T(8,128)(2,1)}, bf16[2560,128]{1,0:T(8,128)(2,1)S(1)}, u32[]{:S(2)}, u32[]{:S(2)}) %collective-permute-start.12) | collective-permute-done | bytes 655392 | tf_op jit(solution)/shard_map/ppermute | solution.py:120
  163.9 14.0 %collective-permute-done.14.rest_5_ = bf16[2560,128]{1,0:T(8,128)(2,1)S(1)} collective-permute-done((bf16[2560,128]{1,0:T(8,128)(2,1)}, bf16[2560,128]{1,0:T(8,128)(2,1)S(1)}, u32[]{:S(2)}, u32[]{:S(2)}) %collective-permute-start.14) | collective-permute-done | bytes 655392 | tf_op jit(solution)/shard_map/ppermute | solution.py:120
  177.9 0.0 collective-permute-done.8.other
  178.0 0.8 copy-done.11
  178.8 1.1 copy-done.8
  179.9 6.5 %merge.1 = bf16[2,128,512]{2,1,0:T(8,128)(2,1)} custom-call(s32[4]{0:T(128)} %pad_add_fusion.1.place, bf16[4,128,1280]{2,1,0:T(8,128)(2,1)} %bitcast.35, bf16[4,128,1280]{2,1,0:T(8,128)(2,1)} %copy-done.8, bf16[5120,256]{1,0:T(8,128)(2,1)} %own.1, bf16[2560,128]{1,0:T(8,128)(2,1)} %collective-permute-done.9.rest_0_, bf16[2560,128]{1,0:T(8,128)(2,1)} %copy-done.9, ...), custom_call_target="tpu_custom_call" | custom-call | tf_op jit(solution)/shard_map/merge/pallas_call | solution.py:254
  186.4 11.5 %all_to_all.20 = bf16[8,32,512]{2,1,0:T(8,128)(2,1)} all-to-all(bf16[8,32,512]{2,1,0:T(8,128)(2,1)} %bitcast.37), channel_id=1, replica_groups=mesh['z'=16,'c'=2,'y'=4,'x'=4] {'c','x'}, dimensions={0} | all-to-all | bytes 524288 | tf_op jit(solution)/shard_map/all_to_all | solution.py:347
  197.9 2.4 %place_columns.1 = bf16[32,4096]{1,0:T(8,128)(2,1)} custom-call(s32[4]{0:T(128)} %pad_add_fusion.1.place, bf16[2,4,32,512]{3,2,1,0:T(8,128)(2,1)} %bitcast.38), custom_call_target="tpu_custom_call" | custom-call | tf_op jit(solution)/shard_map/place_columns/pallas_call | solution.py:286
  (28 shorter events, 0.2 us)
Async XLA Ops:
  0.0 0.9 copy-start
  2.0 17.9 %collective-permute-start.2 = (bf16[320,640]{1,0:T(8,128)(2,1)S(1)}, bf16[320,640]{1,0:T(8,128)(2,1)S(1)}, u32[]{:S(2)}, u32[]{:S(2)}) collective-permute-start(bf16[320,640]{1,0:T(8,128)(2,1)S(1)} %pad_maximum_fusion.2), channel_id=1, source_target_pairs={{0,4},{4,8},{8,12},{12,0},{1,5},{5,9},{9,13},{13,1},{2,6},{6,10},{... | collective-permute-start | bytes 1228808 | tf_op jit(solution)/shard_map/ppermute | solution.py:30
  6.0 20.3 %collective-permute-start.1 = (bf16[320,640]{1,0:T(8,128)(2,1)S(1)}, bf16[320,640]{1,0:T(8,128)(2,1)S(1)}, u32[]{:S(2)}, u32[]{:S(2)}) collective-permute-start(bf16[320,640]{1,0:T(8,128)(2,1)S(1)} %pad_maximum_fusion.2), channel_id=1, source_target_pairs={{0,8},{4,12},{8,0},{12,4},{1,9},{5,13},{9,1},{13,5},{2,10},{6,14},... | collective-permute-start | bytes 1228808 | tf_op jit(solution)/shard_map/ppermute | solution.py:30
  10.6 15.8 %collective-permute-start = (bf16[320,640]{1,0:T(8,128)(2,1)S(1)}, bf16[320,640]{1,0:T(8,128)(2,1)S(1)}, u32[]{:S(2)}, u32[]{:S(2)}) collective-permute-start(bf16[320,640]{1,0:T(8,128)(2,1)S(1)} %pad_maximum_fusion.2), channel_id=1, source_target_pairs={{0,12},{4,0},{8,4},{12,8},{1,13},{5,1},{9,5},{13,9},{2,14},{6,2},{... | collective-permute-start | bytes 1228808 | tf_op jit(solution)/shard_map/ppermute | solution.py:30
  15.9 27.2 %all-to-all-start = ((bf16[4,128,1280]{2,1,0:T(8,128)(2,1)}), bf16[4,128,1280]{2,1,0:T(8,128)(2,1)S(1)}, u32[]{:S(2)}, u32[]{:S(2)}) async-start(bf16[4,128,1280]{2,1,0:T(8,128)(2,1)} %spread.1), calls=%async_computation | async-start | bytes 2621440 | tf_op jit(solution)/shard_map/all_to_all | solution.py:308
  19.9 12.3 %copy-start.5 = (bf16[320,640]{1,0:T(8,128)(2,1)}, bf16[320,640]{1,0:T(8,128)(2,1)S(1)}, u32[]{:S(2)}) copy-start(bf16[320,640]{1,0:T(8,128)(2,1)S(1)} %collective-permute-done.2.third) | copy-start | bytes 1228804
  26.3 5.9 %copy-start.6 = (bf16[320,640]{1,0:T(8,128)(2,1)}, bf16[320,640]{1,0:T(8,128)(2,1)S(1)}, u32[]{:S(2)}) copy-start(bf16[320,640]{1,0:T(8,128)(2,1)S(1)} %collective-permute-done.1.second) | copy-start | bytes 1228804
  26.4 6.7 %copy-start.7 = (bf16[320,640]{1,0:T(8,128)(2,1)}, bf16[320,640]{1,0:T(8,128)(2,1)S(1)}, u32[]{:S(2)}) copy-start(bf16[320,640]{1,0:T(8,128)(2,1)S(1)} %collective-permute-done.first) | copy-start | bytes 1228804
  27.6 15.5 %collective-permute-start.3 = (bf16[3,240,640]{2,1,0:T(8,128)(2,1)}, bf16[3,240,640]{2,1,0:T(8,128)(2,1)}, u32[]{:S(2)}, u32[]{:S(2)}) collective-permute-start(bf16[3,240,640]{2,1,0:T(8,128)(2,1)} %pad_maximum_fusion.1), channel_id=1, source_target_pairs={{0,16},{16,0},{1,17},{17,1},{2,18},{18,2},{3,19},{19,3},{4,20},{20... | collective-permute-start | bytes 2764808 | tf_op jit(solution)/shard_map/ppermute | solution.py:26
  33.1 22.1 %collective-permute-start.6 = (bf16[4,80,640]{2,1,0:T(8,128)(2,1)}, bf16[4,80,640]{2,1,0:T(8,128)(2,1)}, u32[]{:S(2)}, u32[]{:S(2)}) collective-permute-start(bf16[4,80,640]{2,1,0:T(8,128)(2,1)} %get-tuple-element.10), channel_id=1, source_target_pairs={{0,3},{1,0},{2,1},{3,2},{4,7},{5,4},{6,5},{7,6},{8,11},{9,8},{10,9... | collective-permute-start | bytes 1228808 | tf_op jit(solution)/shard_map/ppermute | solution.py:116
  37.5 17.7 %collective-permute-start.5 = (bf16[4,80,640]{2,1,0:T(8,128)(2,1)}, bf16[4,80,640]{2,1,0:T(8,128)(2,1)}, u32[]{:S(2)}, u32[]{:S(2)}) collective-permute-start(bf16[4,80,640]{2,1,0:T(8,128)(2,1)} %get-tuple-element.10), channel_id=1, source_target_pairs={{0,2},{1,3},{2,0},{3,1},{4,6},{5,7},{6,4},{7,5},{8,10},{9,11},{10,... | collective-permute-start | bytes 1228808 | tf_op jit(solution)/shard_map/ppermute | solution.py:116
  39.9 21.4 %collective-permute-start.4 = (bf16[4,80,640]{2,1,0:T(8,128)(2,1)}, bf16[4,80,640]{2,1,0:T(8,128)(2,1)}, u32[]{:S(2)}, u32[]{:S(2)}) collective-permute-start(bf16[4,80,640]{2,1,0:T(8,128)(2,1)} %get-tuple-element.10), channel_id=1, source_target_pairs={{0,1},{1,2},{2,3},{3,0},{4,5},{5,6},{6,7},{7,4},{8,9},{9,10},{10,1... | collective-permute-start | bytes 1228808 | tf_op jit(solution)/shard_map/ppermute | solution.py:116
  43.1 1.1 copy-start.1
  50.5 19.0 %all-to-all-start.1 = ((bf16[4,240,512]{2,1,0:T(8,128)(2,1)}), bf16[4,240,512]{2,1,0:T(8,128)(2,1)S(1)}, u32[]{:S(2)}, u32[]{:S(2)}) async-start(bf16[4,240,512]{2,1,0:T(8,128)(2,1)} %project_qkv.1), calls=%async_computation.1 | async-start | bytes 1966080 | tf_op jit(solution)/shard_map/all_to_all | solution.py:325
  61.4 3.9 %copy-start.12 = (s32[2048]{0:T(1024)S(1)}, s32[2048]{0:T(1024)}, u32[]{:S(2)}) copy-start(s32[2048]{0:T(1024)} %param.8) | copy-start | bytes 24580
  62.9 18.9 %copy-start.2 = (bf16[4,4,80,640]{3,2,1,0:T(8,128)(2,1)}, bf16[4,4,80,640]{3,2,1,0:T(8,128)(2,1)S(1)}, u32[]{:S(2)}) copy-start(bf16[4,4,80,640]{3,2,1,0:T(8,128)(2,1)S(1)} %pad_maximum_fusion.mine) | copy-start | bytes 4915204
  62.9 57.4 %collective-permute-start.7 = (bf16[4,4,80,640]{3,2,1,0:T(8,128)(2,1)S(1)}, bf16[4,4,80,640]{3,2,1,0:T(8,128)(2,1)}, u32[]{:S(2)}, u32[]{:S(2)}) collective-permute-start(bf16[4,4,80,640]{3,2,1,0:T(8,128)(2,1)S(1)} %pad_maximum_fusion.mine), channel_id=1, source_target_pairs={{0,16},{16,0},{1,17},{17,1},{2,18},{18,2},{3,19},{19,3},{4,20},{20... | collective-permute-start | bytes 4915208 | tf_op jit(solution)/shard_map/ppermute | solution.py:26
  69.5 1.0 copy-start.4
  81.7 38.5 %all-to-all-start.2 = ((bf16[16,80,512]{2,1,0:T(8,128)(2,1)}), bf16[16,80,512]{2,1,0:T(8,128)(2,1)S(1)}, u32[]{:S(2)}, u32[]{:S(2)}) async-start(bf16[16,80,512]{2,1,0:T(8,128)(2,1)} %bitcast.33), calls=%async_computation.2 | async-start | bytes 2621440 | tf_op jit(solution)/shard_map/all_to_all | solution.py:335
  88.2 30.1 %collective-permute-start.9 = (bf16[2560,128]{1,0:T(8,128)(2,1)}, bf16[2560,128]{1,0:T(8,128)(2,1)}, u32[]{:S(2)}, u32[]{:S(2)}) collective-permute-start(bf16[2560,128]{1,0:T(8,128)(2,1)} %dynamic_slice.11), channel_id=1, source_target_pairs={{0,4},{4,8},{8,12},{12,0},{1,5},{5,9},{9,13},{13,1},{2,6},{6,10},{... | collective-permute-start | bytes 1966088 | tf_op jit(solution)/shard_map/ppermute | solution.py:30
  91.5 43.2 %collective-permute-start.11 = (bf16[2560,128]{1,0:T(8,128)(2,1)}, bf16[2560,128]{1,0:T(8,128)(2,1)}, u32[]{:S(2)}, u32[]{:S(2)}) collective-permute-start(bf16[2560,128]{1,0:T(8,128)(2,1)} %dynamic_slice.11), channel_id=1, source_target_pairs={{0,12},{4,0},{8,4},{12,8},{1,13},{5,1},{9,5},{13,9},{2,14},{6,2},{... | collective-permute-start | bytes 1966088 | tf_op jit(solution)/shard_map/ppermute | solution.py:30
  118.4 19.1 %collective-permute-start.13 = (bf16[2560,128]{1,0:T(8,128)(2,1)}, bf16[2560,128]{1,0:T(8,128)(2,1)}, u32[]{:S(2)}, u32[]{:S(2)}) collective-permute-start(bf16[2560,128]{1,0:T(8,128)(2,1)} %collective-permute-done.9.rest_0_), channel_id=1, source_target_pairs={{0,4},{4,8},{8,12},{12,0},{1,5},{5,9},{9,13},{13,1},{2,6},{6,10},{... | collective-permute-start | bytes 1966088 | tf_op jit(solution)/shard_map/ppermute | solution.py:30
  120.3 1.1 copy-start.3
  128.7 49.3 %collective-permute-start.8 = (bf16[4,128,1280]{2,1,0:T(8,128)(2,1)}, bf16[4,128,1280]{2,1,0:T(8,128)(2,1)S(1)}, u32[]{:S(2)}, u32[]{:S(2)}) collective-permute-start(bf16[4,128,1280]{2,1,0:T(8,128)(2,1)} %bitcast.34), channel_id=1, source_target_pairs={{0,16},{16,0},{1,17},{17,1},{2,18},{18,2},{3,19},{19,3},{4,20},{20... | collective-permute-start | bytes 3932168 | tf_op jit(solution)/shard_map/ppermute | solution.py:26
  131.1 18.7 %collective-permute-start.10 = (bf16[2560,128]{1,0:T(8,128)(2,1)}, bf16[2560,128]{1,0:T(8,128)(2,1)S(1)}, u32[]{:S(2)}, u32[]{:S(2)}) collective-permute-start(bf16[2560,128]{1,0:T(8,128)(2,1)} %collective-permute-done.9.rest_0_), channel_id=1, source_target_pairs={{0,32},{32,0},{64,96},{96,64},{128,160},{160,128},{192,224},{224,1... | collective-permute-start | bytes 1966088 | tf_op jit(solution)/shard_map/ppermute | solution.py:120
  134.7 29.2 %collective-permute-start.12 = (bf16[2560,128]{1,0:T(8,128)(2,1)}, bf16[2560,128]{1,0:T(8,128)(2,1)S(1)}, u32[]{:S(2)}, u32[]{:S(2)}) collective-permute-start(bf16[2560,128]{1,0:T(8,128)(2,1)} %collective-permute-done.11.rest_2_), channel_id=1, source_target_pairs={{0,32},{32,0},{64,96},{96,64},{128,160},{160,128},{192,224},{224,1... | collective-permute-start | bytes 1966088 | tf_op jit(solution)/shard_map/ppermute | solution.py:120
  137.5 40.5 %collective-permute-start.14 = (bf16[2560,128]{1,0:T(8,128)(2,1)}, bf16[2560,128]{1,0:T(8,128)(2,1)S(1)}, u32[]{:S(2)}, u32[]{:S(2)}) collective-permute-start(bf16[2560,128]{1,0:T(8,128)(2,1)} %collective-permute-done.13.rest_4_), channel_id=1, source_target_pairs={{0,32},{32,0},{64,96},{96,64},{128,160},{160,128},{192,224},{224,1... | collective-permute-start | bytes 1966088 | tf_op jit(solution)/shard_map/ppermute | solution.py:120
  149.9 28.1 %copy-start.9 = (bf16[2560,128]{1,0:T(8,128)(2,1)}, bf16[2560,128]{1,0:T(8,128)(2,1)S(1)}, u32[]{:S(2)}) copy-start(bf16[2560,128]{1,0:T(8,128)(2,1)S(1)} %collective-permute-done.10.rest_1_) | copy-start | bytes 1966084
  163.9 14.1 %copy-start.10 = (bf16[2560,128]{1,0:T(8,128)(2,1)}, bf16[2560,128]{1,0:T(8,128)(2,1)S(1)}, u32[]{:S(2)}) copy-start(bf16[2560,128]{1,0:T(8,128)(2,1)S(1)} %collective-permute-done.12.rest_3_) | copy-start | bytes 1966084
  177.9 0.9 copy-start.11
  178.8 1.1 copy-start.8
